TPU v7x, 32 devices: a whole 2x2x4 slice. The times are simulated.
32 devices in a mesh: groups: 2 (over y), dp: 4 (over z), fsdp: 4 (over x, core).
Axes of the slice: x: 2, y: 2, z: 4, core: 2. Of those that a mesh axis runs over, the one named last changes fastest.
Arguments:
- tokens: bfloat16 [8192, 4096], P(('groups', 'dp', 'fsdp')), parts along dimension 0, may hold values from -6 to 6
- key_value_weight: bfloat16 [4096, 2048], P('fsdp'), may hold values from -0.09375 to 0.09375
- adapter_down_maps: bfloat16 [8, 32, 4096], P(('groups', 'fsdp')), parts along dimension 0, may hold values from -0.09375 to 0.09375
- adapter_up_maps: bfloat16 [8, 32, 1024], P(('groups', 'fsdp')), parts along dimension 0, may hold values from -0.75 to 0.75
- counts: int32 [8, 4], P(('groups', 'dp')), parts along dimension 0, may hold values from 1 to 512, 1024 in all within a row
- tenant_slot_index: int32 [8], P('groups'), parts along dimension 0, may hold values from 0 to 3, each once
- cotangent: bfloat16 [8192, 2048], P(('groups', 'dp', 'fsdp')), parts along dimension 0, may hold values from -6 to 6
Outputs:
- key_value_output: bfloat16 [8192, 2048], P(('groups', 'dp', 'fsdp')), parts along dimension 0
- grad_x: bfloat16 [8192, 4096], P(('groups', 'dp', 'fsdp')), parts along dimension 0
- grad_down: float32 [8, 32, 4096], P(('groups', 'fsdp')), parts along dimension 0
- grad_up: float32 [8, 32, 1024], P(('groups', 'fsdp')), parts along dimension 0
There are 2 independent parts, one for each index of `groups`. A program takes and returns all parts, laid end to end along the dimension named above; an argument that names none is the same for every part. Nothing has to cross between parts.
Inputs may be any that keep to these rules, and one draw needn't show every extreme that they name: Each row gives the token counts of the 4 tenants in one data group, in the order in which their tokens stand, and sums to 1024; every tenant has a token in every group and some tenant holds exactly 512 tokens of each group. `tenant_slot_index`: A permutation of the slots.
All inputs are finite; a program needn't handle non-finite values.
Results may differ from a plain program's by a relative error of at most 0.0095.
Values may be sent and summed in bfloat16 or wider, within the bound.
No kernel may reach another device: no remote copies, remote signals or barrier semaphores. Data moves between devices by JAX's collectives and lax.ppermute only.
A program may use at most 128 MiB of HBM per device.

v0:
```python
import jax
import jax.numpy as jnp
from jax import lax
from jax.sharding import PartitionSpec as P

ADAPTER_SCALE = 2.0


def per_device(
    tokens,
    key_value_weight,
    adapter_down_maps,
    adapter_up_maps,
    counts,
    tenant_slot_index,
    cotangent,
):
    tok_rows = tokens.shape[0]
    width = tokens.shape[1]
    tenants = tenant_slot_index.shape[0]
    doubled_rank = adapter_down_maps.shape[1]
    rank_half = doubled_rank // 2
    key_value_span = adapter_up_maps.shape[2]
    first_pos = lax.axis_index("fsdp") * tok_rows
    positions = first_pos + lax.iota(jnp.int32, tok_rows)
    tenant_ends = jnp.cumsum(counts[0])
    tenant_starts = tenant_ends - counts[0]
    tenant = jnp.sum((positions[:, None] >= tenant_ends[None, :]).astype(jnp.int32), axis=1)
    numbers = lax.iota(jnp.int32, tenants)
    slot_ids = jnp.sum(
        jnp.where(tenant[:, None] == numbers[None, :], tenant_slot_index[None, :], 0), axis=1
    )
    select = (slot_ids[:, None] == numbers[None, :])[:, :, None]
    bf_zero = jnp.zeros((), jnp.bfloat16)
    run_sizes = jnp.maximum(
        jnp.minimum(tenant_ends, first_pos + tok_rows) - jnp.maximum(tenant_starts, first_pos), 0
    )
    weights, down_all, up_all = (
        lax.all_gather(key_value_weight, "fsdp", axis=0, tiled=True),
        lax.all_gather(adapter_down_maps, "fsdp", axis=0, tiled=True),
        lax.all_gather(adapter_up_maps, "fsdp", axis=0, tiled=True),
    )
    down_tenant = jnp.take(down_all, tenant_slot_index, axis=0)
    up_tenant = jnp.take(up_all, tenant_slot_index, axis=0)
    up_tenant_keys = up_tenant[:, :rank_half, :]
    up_tenant_vals = up_tenant[:, rank_half:, :]
    frozen_output = jnp.dot(tokens, weights, preferred_element_type=jnp.float32)
    low_rank = lax.ragged_dot(
        tokens, jnp.transpose(down_tenant, (0, 2, 1)), run_sizes, preferred_element_type=jnp.float32
    ).astype(jnp.bfloat16)
    key_update = lax.ragged_dot(
        low_rank[:, :rank_half], up_tenant_keys, run_sizes, preferred_element_type=jnp.float32
    )
    value_update = lax.ragged_dot(
        low_rank[:, rank_half:], up_tenant_vals, run_sizes, preferred_element_type=jnp.float32
    )
    adapter_update = jnp.concatenate([key_update, value_update], axis=1)
    key_value_output = (frozen_output + ADAPTER_SCALE * adapter_update).astype(jnp.bfloat16)
    cot_keys = cotangent[:, :key_value_span]
    cot_vals = cotangent[:, key_value_span:]
    contract = (((1,), (1,)), ((), ()))
    back_keys = lax.ragged_dot(
        cot_keys,
        jnp.transpose(up_tenant_keys, (0, 2, 1)),
        run_sizes,
        preferred_element_type=jnp.float32,
    )
    back_vals = lax.ragged_dot(
        cot_vals,
        jnp.transpose(up_tenant_vals, (0, 2, 1)),
        run_sizes,
        preferred_element_type=jnp.float32,
    )
    grad_low = (ADAPTER_SCALE * jnp.concatenate([back_keys, back_vals], axis=1)).astype(
        jnp.bfloat16
    )
    low_term = lax.ragged_dot(grad_low, down_tenant, run_sizes, preferred_element_type=jnp.float32)
    grad_x = (
        lax.dot_general(cotangent, weights, contract, preferred_element_type=jnp.float32) + low_term
    ).astype(jnp.bfloat16)
    spread = jnp.where(select, low_rank[:, None, :], bf_zero)
    widened_keys = spread[:, :, :rank_half].reshape(tok_rows, tenants * rank_half)
    spread_vals = spread[:, :, rank_half:].reshape(tok_rows, tenants * rank_half)
    spread_grad = jnp.where(select, grad_low[:, None, :], bf_zero).reshape(
        tok_rows, tenants * doubled_rank
    )
    rows_first = (((0,), (0,)), ((), ()))
    part_down = lax.dot_general(
        spread_grad, tokens, rows_first, preferred_element_type=jnp.float32
    ).reshape(tenants, doubled_rank, width)
    up_keys_term = ADAPTER_SCALE * lax.dot_general(
        widened_keys, cot_keys, rows_first, preferred_element_type=jnp.float32
    )
    up_vals_term = ADAPTER_SCALE * lax.dot_general(
        spread_vals, cot_vals, rows_first, preferred_element_type=jnp.float32
    )
    part_up = jnp.concatenate(
        [
            up_keys_term.reshape(tenants, rank_half, key_value_span),
            up_vals_term.reshape(tenants, rank_half, key_value_span),
        ],
        axis=1,
    )
    owned_sums = (
        lax.psum_scatter(
            part_down.astype(jnp.bfloat16), "fsdp", scatter_dimension=0, tiled=True
        ).astype(jnp.float32),
        lax.psum_scatter(
            part_up.astype(jnp.bfloat16), "fsdp", scatter_dimension=0, tiled=True
        ).astype(jnp.float32),
    )
    grad_down, grad_up = (
        lax.psum(owned_sums[0].astype(jnp.bfloat16), "dp").astype(jnp.float32),
        lax.psum(owned_sums[1].astype(jnp.bfloat16), "dp").astype(jnp.float32),
    )
    return (key_value_output, grad_x, grad_down, grad_up)


def solution(mesh):
    in_specs = (
        P(("groups", "dp", "fsdp"), None),
        P("fsdp", None),
        P(("groups", "fsdp"), None, None),
        P(("groups", "fsdp"), None, None),
        P(("groups", "dp"), None),
        P("groups"),
        P(("groups", "dp", "fsdp"), None),
    )
    out_specs = (
        P(("groups", "dp", "fsdp"), None),
        P(("groups", "dp", "fsdp"), None),
        P(("groups", "fsdp"), None, None),
        P(("groups", "fsdp"), None, None),
    )
    return jax.shard_map(
        per_device, mesh=mesh, in_specs=in_specs, out_specs=out_specs, check_vma=False
    )
```

profile of v0, /device:TPU:0, one launch (start us, length us, event | category | flops | bytes accessed | tf_op | source)
XLA Modules:
  0.0 268.3 jit_solution(1640852649975119332)
XLA Ops:
  7.2 0.7 all-gather.5.cloned.1.call-update
  8.6 0.7 compare_and_fusion
  9.3 0.8 reduce-window.8
  10.1 1.2 fusion.13
  11.3 1.3 ragged-dot-metadata
  12.6 7.5 %all_gather.11 = bf16[4,32,1024]{2,1,0:T(8,128)(2,1)S(1)} all-gather(bf16[1,32,1024]{2,1,0:T(8,128)(2,1)} %param.10), channel_id=1, replica_groups=mesh['groups'=2,'dp'=4,'fsdp'=4] {'fsdp'}, dimensions={0}, use_global_device_ids=true | all-gather | bytes 327680 | tf_op jit(solution)/shard_map/all_gather | solution.py:41
  21.4 1.1 fusion.17
  22.5 2.7 slice_bitcast_fusion.1
  25.2 4.1 %ragged-dot-none.1 = f32[256,16]{1,0:T(8,128)} custom-call(s32[1]{0:T(128)} %get-tuple-element.20, s32[5]{0:T(128)} %get-tuple-element.21, s32[4]{0:T(128)} %get-tuple-element.22, s32[4]{0:T(128)} %get-tuple-element.23, s32[1]{0:T(128)} %get-tuple-element.20, bf16[256,1024]{1,0:T(8,128)(2,1)} %get-tuple-element.35, bf16[4,1024,16]{2,1,0:T(8,128)(2,1)} %get-tuple-element.31), custom_call_target="tpu_custom_call" | custom-call | flops 8388608 | bytes 671760 | tf_op jit(solution)/shard_map/ragged_dot_general/ragged-dot-none
  29.3 4.0 %ragged-dot-none.2 = f32[256,16]{1,0:T(8,128)} custom-call(s32[1]{0:T(128)} %get-tuple-element.20, s32[5]{0:T(128)} %get-tuple-element.21, s32[4]{0:T(128)} %get-tuple-element.22, s32[4]{0:T(128)} %get-tuple-element.23, s32[1]{0:T(128)} %get-tuple-element.20, bf16[256,1024]{1,0:T(8,128)(2,1)} %get-tuple-element.34, bf16[4,1024,16]{2,1,0:T(8,128)(2,1)} %get-tuple-element.30), custom_call_target="tpu_custom_call" | custom-call | flops 8388608 | bytes 671760 | tf_op jit(solution)/shard_map/ragged_dot_general/ragged-dot-none
  33.3 1.1 fusion.5
  34.7 1.4 convolution_convert_fusion
  36.2 1.8 gather_fusion
  38.2 3.1 %copy.37 = bf16[4,4096,32]{2,1,0:T(8,128)(2,1)} copy(bf16[4,4096,32]{1,2,0:T(8,128)(2,1)S(1)} %fusion.26) | data formatting | bytes 2097152 | tf_op jit(solution)/shard_map/jit(_take)/select_n | solution.py:43
  41.4 5.3 %ragged-dot-none.5 = f32[256,32]{1,0:T(8,128)} custom-call(s32[1]{0:T(128)} %get-tuple-element.20, s32[5]{0:T(128)} %get-tuple-element.21, s32[4]{0:T(128)} %get-tuple-element.22, s32[4]{0:T(128)} %get-tuple-element.23, s32[1]{0:T(128)} %get-tuple-element.20, bf16[256,4096]{1,0:T(8,128)(2,1)} %param.7, bf16[4,4096,32]{2,1,0:T(8,128)(2,1)} %copy.37), custom_call_target="tpu_custom_call" | custom-call | flops 67108864 | bytes 3178512 | tf_op jit(solution)/shard_map/ragged_dot_general/ragged-dot-none
  46.7 0.9 convert_element_type.33
  48.1 0.7 pad_maximum_fusion
  48.9 13.5 %reduce-scatter.3.cloned.1.call-done = bf16[1,32,4096]{2,1,0:T(8,128)(2,1)} async-done(((bf16[4,32,4096]{2,1,0:T(8,128)(2,1)}), bf16[1,32,4096]{2,1,0:T(8,128)(2,1)}) %reduce-scatter.3.cloned.1.call-update) | async-done | bytes 262160 | tf_op jit(solution)/shard_map/reduce_scatter | solution.py:105
  62.5 23.3 %reduce-scatter.5.cloned.1.call-done = bf16[1,32,1024]{2,1,0:T(8,128)(2,1)} async-done(((bf16[4,32,1024]{2,1,0:T(8,128)(2,1)}), bf16[1,32,1024]{2,1,0:T(8,128)(2,1)}) %reduce-scatter.5.cloned.1.call-update) | async-done | bytes 65552 | tf_op jit(solution)/shard_map/reduce_scatter | solution.py:108
  86.3 2.2 copy.40
  88.5 1.0 copy.39
  89.5 0.7 fusion.19
  90.2 4.0 %ragged-dot-none.3 = f32[256,1024]{1,0:T(8,128)} custom-call(s32[1]{0:T(128)} %get-tuple-element.20, s32[5]{0:T(128)} %get-tuple-element.21, s32[4]{0:T(128)} %get-tuple-element.22, s32[4]{0:T(128)} %get-tuple-element.23, s32[1]{0:T(128)} %get-tuple-element.20, bf16[256,16]{1,0:T(8,128)(2,1)} %get-tuple-element.39, bf16[4,16,1024]{2,1,0:T(8,128)(2,1)} %copy.40), custom_call_target="tpu_custom_call" | custom-call | flops 8388608 | bytes 1187856 | tf_op jit(solution)/shard_map/ragged_dot_general/ragged-dot-none
  94.2 4.0 %ragged-dot-none.4 = f32[256,1024]{1,0:T(8,128)} custom-call(s32[1]{0:T(128)} %get-tuple-element.20, s32[5]{0:T(128)} %get-tuple-element.21, s32[4]{0:T(128)} %get-tuple-element.22, s32[4]{0:T(128)} %get-tuple-element.23, s32[1]{0:T(128)} %get-tuple-element.20, bf16[256,16]{1,0:T(8,128)(2,1)} %get-tuple-element.38, bf16[4,16,1024]{2,1,0:T(8,128)(2,1)} %copy.39), custom_call_target="tpu_custom_call" | custom-call | flops 8388608 | bytes 1187856 | tf_op jit(solution)/shard_map/ragged_dot_general/ragged-dot-none
  98.3 1.1 broadcast_select_fusion.1
  99.4 5.6 %ragged-dot-none = f32[256,4096]{1,0:T(8,128)} custom-call(s32[1]{0:T(128)} %get-tuple-element.20, s32[5]{0:T(128)} %get-tuple-element.21, s32[4]{0:T(128)} %get-tuple-element.22, s32[4]{0:T(128)} %get-tuple-element.23, s32[1]{0:T(128)} %get-tuple-element.20, bf16[256,32]{1,0:T(8,128)(2,1)} %copy-done.4, bf16[4,32,4096]{2,1,0:T(8,128)(2,1)} %broadcast_select_fusion.1), custom_call_target="tpu_custom_call" | custom-call | flops 67108864 | bytes 5259280 | tf_op jit(solution)/shard_map/ragged_dot_general/ragged-dot-none
  105.0 19.4 %all-reduce.3.cloned.1.call-done = (bf16[1,32,4096]{2,1,0:T(8,128)(2,1)}, bf16[1,32,1024]{2,1,0:T(8,128)(2,1)}) async-done(((bf16[1,32,4096]{2,1,0:T(8,128)(2,1)}, bf16[1,32,1024]{2,1,0:T(8,128)(2,1)}), (bf16[1,32,4096]{2,1,0:T(8,128)(2,1)}, bf16[1,32,1024]{2,1,0:T(8,128)(2,1)})) %all-reduce.3.cloned.1.call-update) | async-done | bytes 327696 | tf_op jit(solution)/shard_map/psum | solution.py:113
  124.3 1.8 convert_element_type.39
  126.1 1.5 convert_element_type.40
  127.6 103.8 %all-gather.3.cloned.1.call-done = bf16[4096,2048]{1,0:T(8,128)(2,1)} async-done(((bf16[1024,2048]{1,0:T(8,128)(2,1)}), bf16[4096,2048]{1,0:T(8,128)(2,1)}) %all-gather.3.cloned.1.call-update) | async-done | bytes 16777232 | tf_op jit(solution)/shard_map/all_gather | solution.py:39
  231.5 18.7 %fusion = bf16[256,4096]{1,0:T(8,128)(2,1)} fusion(f32[256,4096]{1,0:T(8,128)} %ragged-dot-none, bf16[256,2048]{1,0:T(8,128)(2,1)S(1)} %copy-done.2, bf16[4096,2048]{1,0:T(8,128)(2,1)} %all-gather.3.cloned.1.call-done), kind=kOutput, calls=%fused_computation.3 | convolution fusion | flops 4297064448 | bytes 24117248 | tf_op jit(solution)/shard_map/dot_general | solution.py:79
  250.1 11.6 %fusion.1 = bf16[256,2048]{1,0:T(8,128)(2,1)} fusion(bf16[256,4096]{1,0:T(8,128)(2,1)S(1)} %copy-done.1, bf16[4096,2048]{1,0:T(8,128)(2,1)} %all-gather.3.cloned.1.call-done, f32[256,1024]{1,0:T(8,128)} %ragged-dot-none.3, f32[256,1024]{1,0:T(8,128)} %ragged-dot-none.4), kind=kOutput, calls=%fused_computation.6 | convolution fusion | flops 4297064448 | bytes 22020096 | tf_op jit(solution)/shard_map/dot_general | solution.py:47
  (38 shorter events, 3.6 us)
Async XLA Ops:
  7.2 29.0 %all-gather.5.cloned.1.call-start = ((), (), s32[]{:S(2)}) async-start(), calls=%async_computation.3 | async-start | bytes 1310720 | tf_op jit(solution)/shard_map/all_gather | solution.py:40
  7.9 54.6 %reduce-scatter.3.cloned.1.call-start = ((), (), s32[]{:S(2)}) async-start(), calls=%async_computation.4 | async-start | bytes 1310720 | tf_op jit(solution)/shard_map/reduce_scatter | solution.py:105
  12.6 8.8 %copy-start.2 = (bf16[256,2048]{1,0:T(8,128)(2,1)S(1)}, bf16[256,2048]{1,0:T(8,128)(2,1)}, u32[]{:S(2)}) copy-start(bf16[256,2048]{1,0:T(8,128)(2,1)} %param.13) | copy-start | bytes 3145732
  25.2 9.4 %copy-start.5 = (s32[4]{0:T(128)S(1)}, s32[4]{0:T(128)}, u32[]{:S(2)}) copy-start(s32[4]{0:T(128)} %param.12) | copy-start | bytes 52
  25.2 9.5 %copy-start = (bf16[256,4096]{1,0:T(8,128)(2,1)S(1)}, bf16[256,4096]{1,0:T(8,128)(2,1)}, u32[]{:S(2)}) copy-start(bf16[256,4096]{1,0:T(8,128)(2,1)} %param.7) | copy-start | bytes 6291460
  34.4 1.7 copy-start.4
  36.1 49.6 %reduce-scatter.5.cloned.1.call-start = ((), (), s32[]{:S(2)}) async-start(), calls=%async_computation.5 | async-start | bytes 327680 | tf_op jit(solution)/shard_map/reduce_scatter | solution.py:108
  48.9 75.5 %all-reduce.3.cloned.1.call-start = ((), (), s32[]{:S(2)}) async-start(), calls=%async_computation.6 | async-start | bytes 655360 | tf_op jit(solution)/shard_map/psum | solution.py:113
  85.7 2.8 %copy-start.3 = (bf16[4,16,1024]{1,2,0:T(8,128)(2,1)S(1)}, bf16[4,16,1024]{1,2,0:T(8,128)(2,1)}, u32[]{:S(2)}) copy-start(bf16[4,16,1024]{1,2,0:T(8,128)(2,1)} %get-tuple-element.33) | copy-start | bytes 393220
  85.7 145.7 %all-gather.3.cloned.1.call-start = ((), (), s32[]{:S(2)}) async-start(), calls=%async_computation.2 | async-start | bytes 20971520 | tf_op jit(solution)/shard_map/all_gather | solution.py:39
  127.6 122.5 %copy-start.1 = (bf16[256,4096]{1,0:T(8,128)(2,1)S(1)}, bf16[256,4096]{1,0:T(8,128)(2,1)}, u32[]{:S(2)}) copy-start(bf16[256,4096]{1,0:T(8,128)(2,1)} %param.7) | copy-start | bytes 6291460
Sparse Core Ops, SparseCore 0:
  9.6 19.4 all-gather.4
  36.2 26.1 reduce-scatter.2
  65.6 20.0 reduce-scatter.4
  88.0 36.3 all-reduce.2
  125.7 105.6 all-gather.2
where the time goes:
time: 270 us; the launch traced here: 268 us
  waiting for transfers between devices  161 us (60%)
  matrix products  32.1 us (12%)
  Pallas kernels  28.4 us (11%)
  between operations  13.9 us (5%)
  local copies, waits for them, and re-layouts  13.8 us (5%)
  other arithmetic  11 us (4%)
  blocking collectives  7.54 us (3%)
    all_gather x1, waiting for transfers between devices, per_device(): lax.all_gather(key_value_weight, 'fsdp', axis=0, tiled=True)  104 us
    another operation x6, Pallas kernels  27 us
    reduce_scatter x1, waiting for transfers between devices, per_device(): lax.psum_scatter(part_up.astype(jnp.bfloat16), 'fsdp', scatter_dimension=...  23.3 us
    psum x1, waiting for transfers between devices, per_device(): lax.psum(owned_sums[0].astype(jnp.bfloat16), 'dp').astype(jnp.float32)  19.4 us
    dot_general x1, matrix products, per_device(): lax.dot_general(cotangent, weights, contract, preferred_element_type=jnp....  18.7 us
    reduce_scatter x1, waiting for transfers between devices, per_device(): lax.psum_scatter(part_down.astype(jnp.bfloat16), 'fsdp', scatter_dimensio...  13.5 us
    dot_general x1, matrix products, per_device(): frozen_output = jnp.dot(tokens, weights, preferred_element_type=jnp.float32)  11.6 us
    all_gather x1, blocking collectives, per_device(): lax.all_gather(adapter_up_maps, 'fsdp', axis=0, tiled=True)  7.54 us
  transfers between devices with their start and end apart: 5, of which 4 were waited for; matrix products, arithmetic and copies ran while one was open for 10% of the time, Pallas kernels for 11%

commit v1 on v0

v1 whole, which is shorter than its diff:
```python
import functools

import jax
import jax.numpy as jnp
from jax import lax
from jax.experimental import pallas as pl
from jax.experimental.pallas import tpu as pltpu
from jax.sharding import PartitionSpec as P

ADAPTER_SCALE = 2.0
F32 = jnp.float32
BF16 = jnp.bfloat16
CONTRACT_LAST = (((1,), (1,)), ((), ()))
CONTRACT_FIRST = (((0,), (0,)), ((), ()))


def dot(a, b, dims=(((1,), (0,)), ((), ()))):
    return lax.dot_general(a, b, dims, preferred_element_type=F32)


def low_rank_kernel(slots, rank2, width, kv, bounds, tok, cot, *refs):
    packs = refs[:slots]
    spread_low, spread_grad, down_cat, up_cat, keep, send = refs[slots:]
    rows = tok.shape[0]
    for r in range(slots):
        down_cat[pl.ds(r * rank2, rank2), :] = packs[r][:, :width]
        up_cat[pl.ds(r * rank2, rank2), :] = packs[r][:, width:]
    pos = lax.broadcasted_iota(jnp.int32, (rows, slots * rank2), 0)
    col = lax.broadcasted_iota(jnp.int32, (rows, slots * rank2), 1)
    slot = col // rank2
    is_key = (col % rank2) < (rank2 // 2)
    mask = jnp.zeros((rows, slots * rank2), jnp.bool_)
    for r in range(slots):
        inside = (pos >= bounds[0, r]) & (pos < bounds[1, r])
        mask = mask | ((slot == r) & inside)
    low = jnp.where(mask, dot(tok[...], down_cat[...], CONTRACT_LAST), 0.0).astype(BF16)
    spread_low[...] = low
    back_keys = dot(cot[:, :kv], up_cat[...], CONTRACT_LAST)
    back_vals = dot(cot[:, kv:], up_cat[...], CONTRACT_LAST)
    back = ADAPTER_SCALE * jnp.where(is_key, back_keys, back_vals)
    grad = jnp.where(mask, back, 0.0).astype(BF16)
    spread_grad[...] = grad

    def put(r, cols, value):
        ref = keep if r % 2 == 0 else send
        ref[r // 2, :, cols] = value.astype(BF16)

    step = 1024
    for start in range(0, width, step):
        part = dot(grad, tok[:, start : start + step], CONTRACT_FIRST)
        for r in range(slots):
            put(r, slice(start, start + step), part[r * rank2 : (r + 1) * rank2])
    part_keys = ADAPTER_SCALE * dot(low, cot[:, :kv], CONTRACT_FIRST)
    part_vals = ADAPTER_SCALE * dot(low, cot[:, kv:], CONTRACT_FIRST)
    row = lax.broadcasted_iota(jnp.int32, (slots * rank2, kv), 0)
    part = jnp.where((row % rank2) < (rank2 // 2), part_keys, part_vals)
    for r in range(slots):
        put(r, slice(width, width + kv), part[r * rank2 : (r + 1) * rank2])


def low_rank_call(bounds, tok, cot, packs, width, kv):
    slots = len(packs)
    rank2 = packs[0].shape[0]
    rows = tok.shape[0]
    vm = pl.BlockSpec(memory_space=pltpu.VMEM)
    half = jax.ShapeDtypeStruct((slots // 2, rank2, width + kv), BF16)
    return pl.pallas_call(
        functools.partial(low_rank_kernel, slots, rank2, width, kv),
        out_shape=(
            jax.ShapeDtypeStruct((rows, slots * rank2), BF16),
            jax.ShapeDtypeStruct((rows, slots * rank2), BF16),
            jax.ShapeDtypeStruct((slots * rank2, width), BF16),
            jax.ShapeDtypeStruct((slots * rank2, kv), BF16),
            half,
            half,
        ),
        in_specs=[pl.BlockSpec(memory_space=pltpu.SMEM)] + [vm] * (2 + slots),
        out_specs=(vm,) * 6,
        compiler_params=pltpu.CompilerParams(vmem_limit_bytes=40 << 20),
        cost_estimate=pl.CostEstimate(
            flops=12 * rows * width * slots * rank2, bytes_accessed=8 << 20, transcendentals=0
        ),
        name="low_rank",
    )(bounds, tok, cot, *packs)


def matmul_kernel(layout, rank2, kv, first, last, *refs):
    refs = list(refs)
    refs.pop(0)
    tok, cot, low, grad, down, up = (refs.pop(0) for _ in range(6))
    sources = [[refs.pop(0) for _ in range(count)] for count, _, _ in layout]
    if not first:
        acc_in = refs.pop(0)
        refs.pop(0)
    out, gx = refs.pop(0), refs.pop(0)
    acc = refs.pop(0) if last else out
    step = pl.program_id(0)
    total = pl.num_programs(0)

    @pl.when(step == 0)
    def _():
        if first:
            col = lax.broadcasted_iota(jnp.int32, low.shape, 1)
            is_key = (col % rank2) < (rank2 // 2)
            zero = jnp.zeros(low.shape, BF16)
            low_keys = jnp.where(is_key, low[...], zero)
            low_vals = jnp.where(is_key, zero, low[...])
            acc[:, :kv] = ADAPTER_SCALE * dot(low_keys, up[...])
            acc[:, kv:] = ADAPTER_SCALE * dot(low_vals, up[...])
        else:
            acc[...] = acc_in[...]

    for (_, offset, blocks), chunks in zip(layout, sources):

        @pl.when((step >= offset) & (step < offset + blocks))
        def _():
            back = dot(grad[...], down[...])
            start = 0
            for chunk in chunks:
                cols = slice(start, start + chunk.shape[1])
                start += chunk.shape[1]
                weight = chunk[...]
                acc[:, cols] += dot(tok[...], weight)
                back += dot(cot[:, cols], weight, CONTRACT_LAST)
            gx[...] = back.astype(BF16)

    if last:

        @pl.when(step == total - 1)
        def _():
            out[...] = acc[...].astype(BF16)


def matmul_call(table, tok, cot, low, grad, down, up, sources, block, prev, last, name):
    rows, width = tok.shape
    cols = cot.shape[1]
    kv = up.shape[1]
    slot_rows = down.shape[0]
    layout, specs, arrays, offset = [], [], [], 0
    for chunks in sources:
        blocks = chunks[0].shape[0] // block
        layout.append((len(chunks), offset, blocks))
        for chunk in chunks:
            index = functools.partial(
                lambda o, n, s, t: (jnp.clip(s - o, 0, n - 1), 0), offset, blocks
            )
            specs.append(pl.BlockSpec((block, chunk.shape[1]), index))
            arrays.append(chunk)
        offset += blocks
    fixed = lambda s, t: (0, 0)
    moving = lambda s, t: (0, t[s])
    in_specs = [
        pl.BlockSpec((rows, block), moving),
        pl.BlockSpec(cot.shape, fixed),
        pl.BlockSpec(low.shape, fixed),
        pl.BlockSpec(grad.shape, fixed),
        pl.BlockSpec((slot_rows, block), moving),
        pl.BlockSpec(up.shape, fixed),
    ] + specs
    args = [table, tok, cot, low, grad, down, up] + arrays
    first = prev is None
    aliases = {}
    if not first:
        in_specs += [
            pl.BlockSpec((rows, cols), fixed),
            pl.BlockSpec(memory_space=pl.ANY),
        ]
        args += list(prev)
        aliases = {len(args) - 1: 1}
        if not last:
            aliases[len(args) - 2] = 0
    rank2 = ADAPTER_ROWS
    return pl.pallas_call(
        functools.partial(matmul_kernel, tuple(layout), rank2, kv, first, last),
        out_shape=(
            jax.ShapeDtypeStruct((rows, cols), BF16 if last else F32),
            jax.ShapeDtypeStruct((rows, width), BF16),
        ),
        grid_spec=pltpu.PrefetchScalarGridSpec(
            num_scalar_prefetch=1,
            grid=(offset,),
            in_specs=in_specs,
            out_specs=(
                pl.BlockSpec((rows, cols), fixed),
                pl.BlockSpec((rows, block), moving),
            ),
            scratch_shapes=[pltpu.VMEM((rows, cols), F32)] if last else [],
        ),
        input_output_aliases=aliases,
        compiler_params=pltpu.CompilerParams(
            vmem_limit_bytes=40 << 20, dimension_semantics=("arbitrary",)
        ),
        cost_estimate=pl.CostEstimate(
            flops=4 * rows * block * offset * cols,
            bytes_accessed=2 * block * offset * cols,
            transcendentals=0,
        ),
        name=name,
    )(*args)


ADAPTER_ROWS = 32


def xor_swap(value, axis, size, bit):
    return lax.ppermute(value, axis, [(i, i ^ bit) for i in range(size)])


def per_device(
    n_groups,
    n_dp,
    n_fsdp,
    tokens,
    key_value_weight,
    adapter_down_maps,
    adapter_up_maps,
    counts,
    tenant_slot_index,
    cotangent,
):
    rows, width = tokens.shape
    slots = tenant_slot_index.shape[0]
    kv = adapter_up_maps.shape[2]
    shard = key_value_weight.shape[0]
    cols = key_value_weight.shape[1]
    me = lax.axis_index("fsdp")
    group = lax.axis_index("groups")
    data = lax.axis_index("dp")
    swap = lambda value, bit: xor_swap(value, "fsdp", n_fsdp, bit)
    high_bits = [b for b in range(2, n_fsdp, 2)]

    pack = jnp.concatenate([adapter_down_maps[0], adapter_up_maps[0]], axis=1)
    packs = {0: pack}
    for bit in high_bits:
        packs[bit] = swap(pack, bit)
    for bit in [0] + high_bits:
        packs[bit + 1] = swap(packs[bit], 1)

    quartered = n_groups == 2 and n_dp % 2 == 0 and shard % 1024 == 0
    pieces = [[(0, 0, [key_value_weight])], [(1, 0, [swap(key_value_weight, 1)])]]
    if quartered:
        block = shard // 4
        parity = data % 2
        pos = lambda a, b: (((group + a) % 2) * 2 + (parity + b) % 2) * block
        mine = lax.dynamic_slice_in_dim(key_value_weight, pos(0, 0), block, 0)
        chunks = 2
        span = cols // chunks
        sent = [mine[:, i * span : (i + 1) * span] for i in range(chunks)]
        stages = []
        for bit in high_bits:
            direct = [swap(c, bit) for c in sent]
            via_y = [xor_swap(c, "groups", n_groups, 1) for c in direct]
            via_z = [xor_swap(c, "dp", n_dp, 1) for c in direct]
            diagonal = [
                xor_swap(via_z[0], "groups", n_groups, 1),
                xor_swap(via_y[1], "dp", n_dp, 1),
            ]
            stages.append([(bit, pos(0, 0), direct)])
            stages.append([(bit, pos(1, 0), via_y), (bit, pos(0, 1), via_z)])
            stages.append([(bit, pos(1, 1), diagonal)])
        for stage in stages:
            both = []
            for rel, at, parts in stage:
                both.append((rel, at, parts))
                both.append((rel + 1, at, [swap(c, 1) for c in parts]))
            pieces.append(both)
    else:
        block = min(shard, 256)
        for bit in high_bits:
            direct = swap(key_value_weight, bit)
            pieces.append([(bit, 0, [direct]), (bit + 1, 0, [swap(direct, 1)])])
    calls = [pieces[0] + pieces[1]]
    rest = pieces[2:]
    if len(rest) > 3:
        rest = [sum(rest, [])]
    calls += rest

    ends = jnp.cumsum(counts[0]) - me * rows
    starts = ends - counts[0]
    rel_slot = jnp.bitwise_xor(tenant_slot_index, me)
    hit = rel_slot[None, :] == lax.iota(jnp.int32, slots)[:, None]
    bounds = jnp.stack(
        [
            jnp.sum(jnp.where(hit, starts[None, :], 0), axis=1),
            jnp.sum(jnp.where(hit, ends[None, :], 0), axis=1),
        ]
    ).astype(jnp.int32)
    low, grad, down_cat, up_cat, keep, send = low_rank_call(
        bounds, tokens, cotangent, [packs[r] for r in range(slots)], width, kv
    )

    add = lambda a, b: (a.astype(F32) + b.astype(F32)).astype(BF16)
    total = add(keep, swap(send, 1))
    bit = 2
    while bit < n_fsdp:
        pairs = total.reshape((total.shape[0] // 2, 2) + total.shape[1:])
        total = add(pairs[:, 0], swap(pairs[:, 1], bit))
        bit *= 2
    total = total[0]
    bit, trail = 1, []
    while bit < n_dp:
        if bit * 2 < n_dp and total.shape[0] % 32 == 0:
            half = total.shape[0] // 2
            upper = (data // bit) % 2 == 1
            mine = jnp.where(upper, total[half:], total[:half])
            other = jnp.where(upper, total[:half], total[half:])
            total = add(mine, xor_swap(other, "dp", n_dp, bit))
            trail.append((bit, upper))
        else:
            total = add(total, xor_swap(total, "dp", n_dp, bit))
        bit *= 2
    for bit, upper in reversed(trail):
        other = xor_swap(total, "dp", n_dp, bit)
        total = jnp.concatenate(
            [jnp.where(upper, other, total), jnp.where(upper, total, other)], axis=0
        )
    total = total.astype(F32)
    grad_down, grad_up = total[None, :, :width], total[None, :, width:]

    prev = None
    per_shard = shard // block
    for number, call in enumerate(calls):
        table, sources = [], []
        for rel, at, parts in call:
            base = jnp.bitwise_xor(me, rel) * per_shard + at // block
            table += [base + i for i in range(parts[0].shape[0] // block)]
            sources.append(parts)
        prev = matmul_call(
            jnp.stack(table).astype(jnp.int32),
            tokens,
            cotangent,
            low,
            grad,
            down_cat,
            up_cat,
            sources,
            block,
            prev,
            number == len(calls) - 1,
            f"matmul_{number}",
        )
    return prev[0], prev[1], grad_down, grad_up


def solution(mesh):
    in_specs = (
        P(("groups", "dp", "fsdp"), None),
        P("fsdp", None),
        P(("groups", "fsdp"), None, None),
        P(("groups", "fsdp"), None, None),
        P(("groups", "dp"), None),
        P("groups"),
        P(("groups", "dp", "fsdp"), None),
    )
    out_specs = (
        P(("groups", "dp", "fsdp"), None),
        P(("groups", "dp", "fsdp"), None),
        P(("groups", "fsdp"), None, None),
        P(("groups", "fsdp"), None, None),
    )
    body = functools.partial(
        per_device, mesh.shape["groups"], mesh.shape["dp"], mesh.shape["fsdp"]
    )
    return jax.shard_map(
        body, mesh=mesh, in_specs=in_specs, out_specs=out_specs, check_vma=False
    )
```

time: 270 us -> 138 us (0.51)
  waiting for transfers between devices: 161 us -> 67.7 us
  matrix products: 32.1 us -> 0 us
  starting transfers between devices: 0.2 us -> 22.1 us
  between operations: 13.9 us -> 0.76 us
  blocking collectives: 7.54 us -> 0 us
  Pallas kernels: 28.4 us -> 25.3 us
  other arithmetic: 11 us -> 7.95 us
    all_gather x2 -> x0, waiting for transfers between devices: 104 us -> none  [the longest x1 104 us: per_device(): lax.all_gather(key_value_weight, 'fsdp', axis=0, tiled=True)]
    ppermute x0 -> x25, waiting for transfers between devices: none -> 67.7 us  [xor_swap(): return lax.ppermute(value, axis, [(i, i ^ bit) for i in range(size)])]
    reduce_scatter x2 -> x0, waiting for transfers between devices: 36.8 us -> none  [the longest x1 23.3 us: per_device(): lax.psum_scatter(part_up.astype(jnp.bfloat16), 'fsdp', scatter_dimension=...]
    dot_general x5 -> x0, matrix products: 32.1 us -> none  [the longest x1 18.7 us: per_device(): lax.dot_general(cotangent, weights, contract, preferred_element_type=jnp....]
    another operation x6 -> x0, Pallas kernels: 27 us -> none
    pallas_call x0 -> x5, Pallas kernels: none -> 25.3 us  [the longest x4 23.1 us: matmul_call(): pl.pallas_call(functools.partial(matmul_kernel, tuple(layout), rank2, kv,...]
    ppermute x0 -> x25, starting transfers between devices: none -> 22.1 us  [xor_swap(): return lax.ppermute(value, axis, [(i, i ^ bit) for i in range(size)])]
    psum x1 -> x0, waiting for transfers between devices: 19.4 us -> none  [per_device(): lax.psum(owned_sums[0].astype(jnp.bfloat16), 'dp').astype(jnp.float32)]
  transfers between devices with their start and end apart: 5 -> 25, of which waited for: 4 -> 11; matrix products, arithmetic and copies ran while one was open for 10% -> 7% of each run, Pallas kernels for 11% -> 14%
where the time goes in v1:
time: 138 us
  waiting for transfers between devices  67.7 us (49%)
  Pallas kernels  25.3 us (18%)
  starting transfers between devices  22.1 us (16%)
  local copies, waits for them, and re-layouts  13.8 us (10%)
  other arithmetic  7.95 us (6%)
    ppermute x25, waiting for transfers between devices, xor_swap(): return lax.ppermute(value, axis, [(i, i ^ bit) for i in range(size)])  67.7 us
    pallas_call x4, Pallas kernels, matmul_call(): pl.pallas_call(functools.partial(matmul_kernel, tuple(layout), rank2, kv,...  23.1 us
    ppermute x25, starting transfers between devices, xor_swap(): return lax.ppermute(value, axis, [(i, i ^ bit) for i in range(size)])  22.1 us
    unnamed x22, local copies, waits for them, and re-layouts  10.6 us
  transfers between devices with their start and end apart: 25, of which 11 were waited for; matrix products, arithmetic and copies ran while one was open for 7% of the time, Pallas kernels for 14%

profile of v1, /device:TPU:0, one launch (start us, length us, event | category | flops | bytes accessed | tf_op | source)
XLA Modules:
  0.0 137.6 jit_solution(14422615035477065188)
XLA Ops:
  1.6 3.0 %collective-permute-start.1 = (bf16[32,5120]{1,0:T(8,128)(2,1)S(1)}, bf16[32,5120]{1,0:T(8,128)(2,1)S(1)}, u32[]{:S(2)}, u32[]{:S(2)}) collective-permute-start(bf16[32,5120]{1,0:T(8,128)(2,1)S(1)} %pad_maximum_fusion.refs_0_), channel_id=1, source_target_pairs={{0,2},{1,3},{2,0},{3,1},{4,6},{5,7},{6,4},{7,5},{8,10},{9,11},{10,... | collective-permute-start | bytes 983048 | tf_op jit(solution)/shard_map/ppermute | solution.py:206
  6.1 6.2 %collective-permute-done.1.refs_2_ = bf16[32,5120]{1,0:T(8,128)(2,1)S(1)} collective-permute-done((bf16[32,5120]{1,0:T(8,128)(2,1)S(1)}, bf16[32,5120]{1,0:T(8,128)(2,1)S(1)}, u32[]{:S(2)}, u32[]{:S(2)}) %collective-permute-start.1) | collective-permute-done | bytes 327712 | tf_op jit(solution)/shard_map/ppermute | solution.py:206
  14.7 1.6 %copy-done = bf16[256,4096]{1,0:T(8,128)(2,1)S(1)} copy-done((bf16[256,4096]{1,0:T(8,128)(2,1)S(1)}, bf16[256,4096]{1,0:T(8,128)(2,1)}, u32[]{:S(2)}) %copy-start) | copy-done | bytes 2097176
  16.2 1.2 copy-done.2
  19.4 2.2 %low_rank.1 = (bf16[256,128]{1,0:T(8,128)(2,1)S(1)}, bf16[256,128]{1,0:T(8,128)(2,1)S(1)}, bf16[128,4096]{1,0:T(8,128)(2,1)S(1)}, bf16[128,1024]{1,0:T(8,128)(2,...) custom-call(s32[2,4]{1,0:T(2,128)S(1)} %pad_add_fusion.bounds, bf16[256,4096]{1,0:T(8,128)(2,1)S(1)} %copy-done, ...), custom_call_target="tpu_custom_call" | custom-call | flops 1610612736 | bytes 8388608 | tf_op jit(solution)/shard_map/low_rank/pallas_call | solution.py:67
  23.1 1.7 %collective-permute-done.20 = bf16[2,32,5120]{2,1,0:T(8,128)(2,1)S(1)} collective-permute-done((bf16[2,32,5120]{2,1,0:T(8,128)(2,1)S(1)}, bf16[2,32,5120]{2,1,0:T(8,128)(2,1)S(1)}, u32[]{:S(2)}, u32[]{:S(2)}) %collective-permute-start.20) | collective-permute-done | bytes 655392 | tf_op jit(solution)/shard_map/ppermute | solution.py:206
  25.0 1.8 %collective-permute-start.21 = (bf16[1,32,5120]{2,1,0:T(8,128)(2,1)S(1)}, bf16[1,32,5120]{2,1,0:T(8,128)(2,1)S(1)}, u32[]{:S(2)}, u32[]{:S(2)}) collective-permute-start(bf16[1,32,5120]{2,1,0:T(8,128)(2,1)S(1)} %slice_bitcast_fusion.1), channel_id=1, source_target_pairs={{0,2},{1,3},{2,0},{3,1},{4,6},{5,7},{6,4},{7,5},{8,10},{9,11},{10,... | collective-permute-start | bytes 983048 | tf_op jit(solution)/shard_map/ppermute | solution.py:206
  26.9 8.2 %collective-permute-done.21 = bf16[1,32,5120]{2,1,0:T(8,128)(2,1)S(1)} collective-permute-done((bf16[1,32,5120]{2,1,0:T(8,128)(2,1)S(1)}, bf16[1,32,5120]{2,1,0:T(8,128)(2,1)S(1)}, u32[]{:S(2)}, u32[]{:S(2)}) %collective-permute-start.21) | collective-permute-done | bytes 327712 | tf_op jit(solution)/shard_map/ppermute | solution.py:206
  35.2 1.9 %collective-permute-start.22 = (bf16[16,5120]{1,0:T(8,128)(2,1)S(1)}, bf16[16,5120]{1,0:T(8,128)(2,1)S(1)}, u32[]{:S(2)}, u32[]{:S(2)}) collective-permute-start(bf16[16,5120]{1,0:T(8,128)(2,1)S(1)} %select_bitcast_fusion), channel_id=1, source_target_pairs={{0,4},{4,0},{8,12},{12,8},{1,5},{5,1},{9,13},{13,9},{2,6},{6,2},{1... | collective-permute-start | bytes 491528 | tf_op jit(solution)/shard_map/ppermute | solution.py:206
  37.1 3.9 %collective-permute-done.22 = bf16[16,5120]{1,0:T(8,128)(2,1)S(1)} collective-permute-done((bf16[16,5120]{1,0:T(8,128)(2,1)S(1)}, bf16[16,5120]{1,0:T(8,128)(2,1)S(1)}, u32[]{:S(2)}, u32[]{:S(2)}) %collective-permute-start.22) | collective-permute-done | bytes 163872 | tf_op jit(solution)/shard_map/ppermute | solution.py:206
  41.7 2.8 %collective-permute-start.23 = (bf16[16,5120]{1,0:T(8,128)(2,1)}, bf16[16,5120]{1,0:T(8,128)(2,1)}, u32[]{:S(2)}, u32[]{:S(2)}) collective-permute-start(bf16[16,5120]{1,0:T(8,128)(2,1)} %fusion.2), channel_id=1, source_target_pairs={{0,8},{4,12},{8,0},{12,4},{1,9},{5,13},{9,1},{13,5},{2,10},{6,14},... | collective-permute-start | bytes 491528 | tf_op jit(solution)/shard_map/ppermute | solution.py:206
  44.5 2.2 %fusion.4 = (bf16[256,1024]{1,0:T(8,128)(2,1)}, bf16[256,1024]{1,0:T(8,128)(2,1)}) fusion(bf16[1024,2048]{1,0:T(8,128)(2,1)} %refs_7_.1, s32[]{:T(128)S(6)} %select_n.99, s32[]{:T(128)S(6)} %add.142), kind=kLoop, calls=%fused_computation.28 | loop fusion | bytes 2097160 | tf_op jit(solution)/shard_map/slice | solution.py:248
  46.7 1.5 %collective-permute-start.3 = (bf16[256,1024]{1,0:T(8,128)(2,1)}, bf16[256,1024]{1,0:T(8,128)(2,1)}, u32[]{:S(2)}, u32[]{:S(2)}) collective-permute-start(bf16[256,1024]{1,0:T(8,128)(2,1)} %get-tuple-element.35), channel_id=1, source_target_pairs={{0,2},{1,3},{2,0},{3,1},{4,6},{5,7},{6,4},{7,5},{8,10},{9,11},{10,... | collective-permute-start | bytes 1572872 | tf_op jit(solution)/shard_map/ppermute | solution.py:206
  48.8 2.5 %collective-permute-done.23 = bf16[16,5120]{1,0:T(8,128)(2,1)} collective-permute-done((bf16[16,5120]{1,0:T(8,128)(2,1)}, bf16[16,5120]{1,0:T(8,128)(2,1)}, u32[]{:S(2)}, u32[]{:S(2)}) %collective-permute-start.23) | collective-permute-done | bytes 163872 | tf_op jit(solution)/shard_map/ppermute | solution.py:206
  51.3 1.7 %add_convert_fusion.1 = bf16[16,5120]{1,0:T(8,128)(2,1)} fusion(bf16[16,5120]{1,0:T(8,128)(2,1)} %collective-permute-done.23, bf16[16,5120]{1,0:T(8,128)(2,1)} %fusion.2), kind=kLoop, calls=%fused_computation.11 | loop fusion | flops 327680 | bytes 491520 | tf_op jit(solution)/shard_map/convert_element_type | solution.py:292
  54.0 7.9 %collective-permute-done.3.refs_7_ = bf16[256,1024]{1,0:T(8,128)(2,1)} collective-permute-done((bf16[256,1024]{1,0:T(8,128)(2,1)}, bf16[256,1024]{1,0:T(8,128)(2,1)}, u32[]{:S(2)}, u32[]{:S(2)}) %collective-permute-start.3) | collective-permute-done | bytes 524320 | tf_op jit(solution)/shard_map/ppermute | solution.py:206
  61.9 1.5 %collective-permute-start.11 = (bf16[256,1024]{1,0:T(8,128)(2,1)}, bf16[256,1024]{1,0:T(8,128)(2,1)S(1)}, u32[]{:S(2)}, u32[]{:S(2)}) collective-permute-start(bf16[256,1024]{1,0:T(8,128)(2,1)} %collective-permute-done.3.refs_7_), channel_id=1, source_target_pairs={{0,16},{16,0},{1,17},{17,1},{2,18},{18,2},{3,19},{19,3},{4,20},{20... | collective-permute-start | bytes 1572872 | tf_op jit(solution)/shard_map/ppermute | solution.py:206
  63.4 7.0 %collective-permute-done.6.refs_8_ = bf16[256,1024]{1,0:T(8,128)(2,1)} collective-permute-done((bf16[256,1024]{1,0:T(8,128)(2,1)}, bf16[256,1024]{1,0:T(8,128)(2,1)}, u32[]{:S(2)}, u32[]{:S(2)}) %collective-permute-start.6) | collective-permute-done | bytes 524320 | tf_op jit(solution)/shard_map/ppermute | solution.py:206
  70.5 1.5 %collective-permute-start.7 = (bf16[256,1024]{1,0:T(8,128)(2,1)}, bf16[256,1024]{1,0:T(8,128)(2,1)S(1)}, u32[]{:S(2)}, u32[]{:S(2)}) collective-permute-start(bf16[256,1024]{1,0:T(8,128)(2,1)} %collective-permute-done.6.refs_8_), channel_id=1, source_target_pairs={{0,16},{16,0},{1,17},{17,1},{2,18},{18,2},{3,19},{19,3},{4,20},{20... | collective-permute-start | bytes 1572872 | tf_op jit(solution)/shard_map/ppermute | solution.py:206
  73.0 1.6 %collective-permute-start.4 = (bf16[256,1024]{1,0:T(8,128)(2,1)}, bf16[256,1024]{1,0:T(8,128)(2,1)S(1)}, u32[]{:S(2)}, u32[]{:S(2)}) collective-permute-start(bf16[256,1024]{1,0:T(8,128)(2,1)} %collective-permute-done.3.refs_7_), channel_id=1, source_target_pairs={{0,4},{4,0},{8,12},{12,8},{1,5},{5,1},{9,13},{13,9},{2,6},{6,2},{1... | collective-permute-start | bytes 1572872 | tf_op jit(solution)/shard_map/ppermute | solution.py:206
  75.2 1.6 %collective-permute-done.11.refs_7_ = bf16[256,1024]{1,0:T(8,128)(2,1)S(1)} collective-permute-done((bf16[256,1024]{1,0:T(8,128)(2,1)}, bf16[256,1024]{1,0:T(8,128)(2,1)S(1)}, u32[]{:S(2)}, u32[]{:S(2)}) %collective-permute-start.11) | collective-permute-done | bytes 524320 | tf_op jit(solution)/shard_map/ppermute | solution.py:206
  76.8 10.8 %collective-permute-done.7.refs_8_ = bf16[256,1024]{1,0:T(8,128)(2,1)S(1)} collective-permute-done((bf16[256,1024]{1,0:T(8,128)(2,1)}, bf16[256,1024]{1,0:T(8,128)(2,1)S(1)}, u32[]{:S(2)}, u32[]{:S(2)}) %collective-permute-start.7) | collective-permute-done | bytes 524320 | tf_op jit(solution)/shard_map/ppermute | solution.py:206
  87.7 1.6 %collective-permute-start.8 = (bf16[256,1024]{1,0:T(8,128)(2,1)S(1)}, bf16[256,1024]{1,0:T(8,128)(2,1)S(1)}, u32[]{:S(2)}, u32[]{:S(2)}) collective-permute-start(bf16[256,1024]{1,0:T(8,128)(2,1)S(1)} %collective-permute-done.7.refs_8_), channel_id=1, source_target_pairs={{0,4},{4,0},{8,12},{12,8},{1,5},{5,1},{9,13},{13,9},{2,6},{6,2},{1... | collective-permute-start | bytes 1572872 | tf_op jit(solution)/shard_map/ppermute | solution.py:206
  89.3 1.5 %collective-permute-start.5 = (bf16[256,1024]{1,0:T(8,128)(2,1)S(1)}, bf16[256,1024]{1,0:T(8,128)(2,1)S(1)}, u32[]{:S(2)}, u32[]{:S(2)}) collective-permute-start(bf16[256,1024]{1,0:T(8,128)(2,1)S(1)} %collective-permute-done.4.refs_11_), channel_id=1, source_target_pairs={{0,16},{16,0},{1,17},{17,1},{2,18},{18,2},{3,19},{19,3},{4,20},{20... | collective-permute-start | bytes 1572872 | tf_op jit(solution)/shard_map/ppermute | solution.py:206
  91.6 7.7 %collective-permute-done.14.refs_12_ = bf16[256,1024]{1,0:T(8,128)(2,1)S(1)} collective-permute-done((bf16[256,1024]{1,0:T(8,128)(2,1)}, bf16[256,1024]{1,0:T(8,128)(2,1)S(1)}, u32[]{:S(2)}, u32[]{:S(2)}) %collective-permute-start.14) | collective-permute-done | bytes 524320 | tf_op jit(solution)/shard_map/ppermute | solution.py:206
  99.8 10.0 %collective-permute-done.8.refs_8_ = bf16[256,1024]{1,0:T(8,128)(2,1)S(1)} collective-permute-done((bf16[256,1024]{1,0:T(8,128)(2,1)S(1)}, bf16[256,1024]{1,0:T(8,128)(2,1)S(1)}, u32[]{:S(2)}, u32[]{:S(2)}) %collective-permute-start.8) | collective-permute-done | bytes 524320 | tf_op jit(solution)/shard_map/ppermute | solution.py:206
  111.1 1.2 copy-done.5
  112.3 2.2 %copy-done.6 = bf16[1024,2048]{1,0:T(8,128)(2,1)S(1)} copy-done((bf16[1024,2048]{1,0:T(8,128)(2,1)S(1)}, bf16[1024,2048]{1,0:T(8,128)(2,1)}, u32[]{:S(2)}) %copy-start.6) | copy-done | bytes 4194328
  114.5 10.5 %matmul_0.1 = (f32[256,2048]{1,0:T(8,128)S(1)}, bf16[256,4096]{1,0:T(8,128)(2,1)}) custom-call(s32[8]{0:T(128)S(1)} %stack.91.refs_0_, bf16[256,4096]{1,0:T(8,128)(2,1)S(1)} %copy-done.1, bf16[256,2048]{1,0:T(8,128)(2,1)S(1)} %copy-done.3, bf16[256,128]{1,0:T(8,128)(2,1)S(1)} %get-tuple-element.18.refs_3_, bf16[256,128]{1,0:T(8,128)(2,1)S(1)} %get-tuple-element.19.refs_4_, ...), custom_call_target="tpu_custom_call" | custom-call | flops 4294967296 | bytes 8388608 | tf_op jit(solution)/shard_map/matmul_0/pallas_call | solution.py:173
  125.0 4.3 %matmul_1.1 = (f32[256,2048]{1,0:T(8,128)S(1)}, bf16[256,4096]{1,0:T(8,128)(2,1)}) custom-call(s32[2]{0:T(128)S(1)} %pad_add_fusion.3.refs_0_, bf16[256,4096]{1,0:T(8,128)(2,1)S(1)} %copy-done.1, bf16[256,2048]{1,0:T(8,128)(2,1)S(1)} %copy-done.3, bf16[256,128]{1,0:T(8,128)(2,1)S(1)} %get-tuple-element.18.refs_3_, ...), custom_call_target="tpu_custom_call", output_to_operand_aliasing={{1}: (12, {}), {0}: (11, {})} | custom-call | flops 1073741824 | bytes 2097152 | tf_op jit(solution)/shard_map/matmul_1/pallas_call | solution.py:173
  129.3 4.9 %matmul_2.1 = (f32[256,2048]{1,0:T(8,128)S(1)}, bf16[256,4096]{1,0:T(8,128)(2,1)}) custom-call(s32[4]{0:T(128)S(1)} %pad_add_fusion.2.refs_0_, bf16[256,4096]{1,0:T(8,128)(2,1)S(1)} %copy-done.1, bf16[256,2048]{1,0:T(8,128)(2,1)S(1)} %copy-done.3, bf16[256,128]{1,0:T(8,128)(2,1)S(1)} %get-tuple-element.18.refs_3_, ...), custom_call_target="tpu_custom_call", output_to_operand_aliasing={{1}: (16, {}), {0}: (15, {})} | custom-call | flops 2147483648 | bytes 4194304 | tf_op jit(solution)/shard_map/matmul_2/pallas_call | solution.py:173
  134.2 3.5 %matmul_3.1 = (bf16[256,2048]{1,0:T(8,128)(2,1)}, bf16[256,4096]{1,0:T(8,128)(2,1)}) custom-call(s32[2]{0:T(128)S(1)} %pad_add_fusion.1.refs_0_, bf16[256,4096]{1,0:T(8,128)(2,1)S(1)} %copy-done.1, bf16[256,2048]{1,0:T(8,128)(2,1)S(1)} %copy-done.3, bf16[256,128]{1,0:T(8,128)(2,1)S(1)} %get-tuple-element.18.refs_3_, ...), custom_call_target="tpu_custom_call", output_to_operand_aliasing={{1}: (12, {})} | custom-call | flops 1073741824 | bytes 2097152 | tf_op jit(solution)/shard_map/matmul_3/pallas_call | solution.py:173
  (67 shorter events, 15.0 us)
Async XLA Ops:
  1.6 10.7 %collective-permute-start.1 = (bf16[32,5120]{1,0:T(8,128)(2,1)S(1)}, bf16[32,5120]{1,0:T(8,128)(2,1)S(1)}, u32[]{:S(2)}, u32[]{:S(2)}) collective-permute-start(bf16[32,5120]{1,0:T(8,128)(2,1)S(1)} %pad_maximum_fusion.refs_0_), channel_id=1, source_target_pairs={{0,2},{1,3},{2,0},{3,1},{4,6},{5,7},{6,4},{7,5},{8,10},{9,11},{10,... | collective-permute-start | bytes 983048 | tf_op jit(solution)/shard_map/ppermute | solution.py:206
  4.7 9.3 %collective-permute-start = (bf16[32,5120]{1,0:T(8,128)(2,1)S(1)}, bf16[32,5120]{1,0:T(8,128)(2,1)S(1)}, u32[]{:S(2)}, u32[]{:S(2)}) collective-permute-start(bf16[32,5120]{1,0:T(8,128)(2,1)S(1)} %pad_maximum_fusion.refs_0_), channel_id=1, source_target_pairs={{0,1},{1,0},{2,3},{3,2},{4,5},{5,4},{6,7},{7,6},{8,9},{9,8},{10,11... | collective-permute-start | bytes 983048 | tf_op jit(solution)/shard_map/ppermute | solution.py:206
  12.4 2.3 %collective-permute-start.2 = (bf16[32,5120]{1,0:T(8,128)(2,1)S(1)}, bf16[32,5120]{1,0:T(8,128)(2,1)S(1)}, u32[]{:S(2)}, u32[]{:S(2)}) collective-permute-start(bf16[32,5120]{1,0:T(8,128)(2,1)S(1)} %collective-permute-done.1.refs_2_), channel_id=1, source_target_pairs={{0,1},{1,0},{2,3},{3,2},{4,5},{5,4},{6,7},{7,6},{8,9},{9,8},{10,11... | collective-permute-start | bytes 983048 | tf_op jit(solution)/shard_map/ppermute | solution.py:206
  14.7 1.6 %copy-start = (bf16[256,4096]{1,0:T(8,128)(2,1)S(1)}, bf16[256,4096]{1,0:T(8,128)(2,1)}, u32[]{:S(2)}) copy-start(bf16[256,4096]{1,0:T(8,128)(2,1)} %refs_1_.7) | copy-start | bytes 6291460
  16.2 1.2 copy-start.2
  21.6 1.0 copy-start.4
  22.6 2.2 %collective-permute-start.20 = (bf16[2,32,5120]{2,1,0:T(8,128)(2,1)S(1)}, bf16[2,32,5120]{2,1,0:T(8,128)(2,1)S(1)}, u32[]{:S(2)}, u32[]{:S(2)}) collective-permute-start(bf16[2,32,5120]{2,1,0:T(8,128)(2,1)S(1)} %get-tuple-element.31), channel_id=1, source_target_pairs={{0,1},{1,0},{2,3},{3,2},{4,5},{5,4},{6,7},{7,6},{8,9},{9,8},{10,11... | collective-permute-start | bytes 1966088 | tf_op jit(solution)/shard_map/ppermute | solution.py:206
  25.0 10.1 %collective-permute-start.21 = (bf16[1,32,5120]{2,1,0:T(8,128)(2,1)S(1)}, bf16[1,32,5120]{2,1,0:T(8,128)(2,1)S(1)}, u32[]{:S(2)}, u32[]{:S(2)}) collective-permute-start(bf16[1,32,5120]{2,1,0:T(8,128)(2,1)S(1)} %slice_bitcast_fusion.1), channel_id=1, source_target_pairs={{0,2},{1,3},{2,0},{3,1},{4,6},{5,7},{6,4},{7,5},{8,10},{9,11},{10,... | collective-permute-start | bytes 983048 | tf_op jit(solution)/shard_map/ppermute | solution.py:206
  35.2 5.8 %collective-permute-start.22 = (bf16[16,5120]{1,0:T(8,128)(2,1)S(1)}, bf16[16,5120]{1,0:T(8,128)(2,1)S(1)}, u32[]{:S(2)}, u32[]{:S(2)}) collective-permute-start(bf16[16,5120]{1,0:T(8,128)(2,1)S(1)} %select_bitcast_fusion), channel_id=1, source_target_pairs={{0,4},{4,0},{8,12},{12,8},{1,5},{5,1},{9,13},{13,9},{2,6},{6,2},{1... | collective-permute-start | bytes 491528 | tf_op jit(solution)/shard_map/ppermute | solution.py:206
  37.1 73.9 %collective-permute-start.19 = (bf16[1024,2048]{1,0:T(8,128)(2,1)}, bf16[1024,2048]{1,0:T(8,128)(2,1)}, u32[]{:S(2)}, u32[]{:S(2)}) collective-permute-start(bf16[1024,2048]{1,0:T(8,128)(2,1)} %refs_7_.1), channel_id=1, source_target_pairs={{0,1},{1,0},{2,3},{3,2},{4,5},{5,4},{6,7},{7,6},{8,9},{9,8},{10,11... | collective-permute-start | bytes 12582920 | tf_op jit(solution)/shard_map/ppermute | solution.py:206
  41.7 9.6 %collective-permute-start.23 = (bf16[16,5120]{1,0:T(8,128)(2,1)}, bf16[16,5120]{1,0:T(8,128)(2,1)}, u32[]{:S(2)}, u32[]{:S(2)}) collective-permute-start(bf16[16,5120]{1,0:T(8,128)(2,1)} %fusion.2), channel_id=1, source_target_pairs={{0,8},{4,12},{8,0},{12,4},{1,9},{5,13},{9,1},{13,5},{2,10},{6,14},... | collective-permute-start | bytes 491528 | tf_op jit(solution)/shard_map/ppermute | solution.py:206
  46.7 64.4 %copy-start.1 = (bf16[256,4096]{1,0:T(8,128)(2,1)S(1)}, bf16[256,4096]{1,0:T(8,128)(2,1)}, u32[]{:S(2)}) copy-start(bf16[256,4096]{1,0:T(8,128)(2,1)} %refs_1_.7) | copy-start | bytes 6291460
  46.7 64.4 %copy-start.3 = (bf16[256,2048]{1,0:T(8,128)(2,1)S(1)}, bf16[256,2048]{1,0:T(8,128)(2,1)}, u32[]{:S(2)}) copy-start(bf16[256,2048]{1,0:T(8,128)(2,1)} %refs_2_.7) | copy-start | bytes 3145732
  46.7 15.2 %collective-permute-start.3 = (bf16[256,1024]{1,0:T(8,128)(2,1)}, bf16[256,1024]{1,0:T(8,128)(2,1)}, u32[]{:S(2)}, u32[]{:S(2)}) collective-permute-start(bf16[256,1024]{1,0:T(8,128)(2,1)} %get-tuple-element.35), channel_id=1, source_target_pairs={{0,2},{1,3},{2,0},{3,1},{4,6},{5,7},{6,4},{7,5},{8,10},{9,11},{10,... | collective-permute-start | bytes 1572872 | tf_op jit(solution)/shard_map/ppermute | solution.py:206
  48.2 22.3 %collective-permute-start.6 = (bf16[256,1024]{1,0:T(8,128)(2,1)}, bf16[256,1024]{1,0:T(8,128)(2,1)}, u32[]{:S(2)}, u32[]{:S(2)}) collective-permute-start(bf16[256,1024]{1,0:T(8,128)(2,1)} %get-tuple-element.34), channel_id=1, source_target_pairs={{0,2},{1,3},{2,0},{3,1},{4,6},{5,7},{6,4},{7,5},{8,10},{9,11},{10,... | collective-permute-start | bytes 1572872 | tf_op jit(solution)/shard_map/ppermute | solution.py:206
  53.0 17.5 %collective-permute-start.24 = (bf16[16,5120]{1,0:T(8,128)(2,1)}, bf16[16,5120]{1,0:T(8,128)(2,1)}, u32[]{:S(2)}, u32[]{:S(2)}) collective-permute-start(bf16[16,5120]{1,0:T(8,128)(2,1)} %add_convert_fusion.1), channel_id=1, source_target_pairs={{0,4},{4,0},{8,12},{12,8},{1,5},{5,1},{9,13},{13,9},{2,6},{6,2},{1... | collective-permute-start | bytes 491528 | tf_op jit(solution)/shard_map/ppermute | solution.py:206
  61.9 11.1 %collective-permute-start.17 = (bf16[256,1024]{1,0:T(8,128)(2,1)}, bf16[256,1024]{1,0:T(8,128)(2,1)S(1)}, u32[]{:S(2)}, u32[]{:S(2)}) collective-permute-start(bf16[256,1024]{1,0:T(8,128)(2,1)} %collective-permute-done.3.refs_7_), channel_id=1, source_target_pairs={{0,1},{1,0},{2,3},{3,2},{4,5},{5,4},{6,7},{7,6},{8,9},{9,8},{10,11... | collective-permute-start | bytes 1572872 | tf_op jit(solution)/shard_map/ppermute | solution.py:206
  61.9 14.9 %collective-permute-start.11 = (bf16[256,1024]{1,0:T(8,128)(2,1)}, bf16[256,1024]{1,0:T(8,128)(2,1)S(1)}, u32[]{:S(2)}, u32[]{:S(2)}) collective-permute-start(bf16[256,1024]{1,0:T(8,128)(2,1)} %collective-permute-done.3.refs_7_), channel_id=1, source_target_pairs={{0,16},{16,0},{1,17},{17,1},{2,18},{18,2},{3,19},{19,3},{4,20},{20... | collective-permute-start | bytes 1572872 | tf_op jit(solution)/shard_map/ppermute | solution.py:206
  70.5 4.3 %collective-permute-start.18 = (bf16[256,1024]{1,0:T(8,128)(2,1)}, bf16[256,1024]{1,0:T(8,128)(2,1)S(1)}, u32[]{:S(2)}, u32[]{:S(2)}) collective-permute-start(bf16[256,1024]{1,0:T(8,128)(2,1)} %collective-permute-done.6.refs_8_), channel_id=1, source_target_pairs={{0,1},{1,0},{2,3},{3,2},{4,5},{5,4},{6,7},{7,6},{8,9},{9,8},{10,11... | collective-permute-start | bytes 1572872 | tf_op jit(solution)/shard_map/ppermute | solution.py:206
  70.5 17.2 %collective-permute-start.7 = (bf16[256,1024]{1,0:T(8,128)(2,1)}, bf16[256,1024]{1,0:T(8,128)(2,1)S(1)}, u32[]{:S(2)}, u32[]{:S(2)}) collective-permute-start(bf16[256,1024]{1,0:T(8,128)(2,1)} %collective-permute-done.6.refs_8_), channel_id=1, source_target_pairs={{0,16},{16,0},{1,17},{17,1},{2,18},{18,2},{3,19},{19,3},{4,20},{20... | collective-permute-start | bytes 1572872 | tf_op jit(solution)/shard_map/ppermute | solution.py:206
  73.0 16.2 %collective-permute-start.4 = (bf16[256,1024]{1,0:T(8,128)(2,1)}, bf16[256,1024]{1,0:T(8,128)(2,1)S(1)}, u32[]{:S(2)}, u32[]{:S(2)}) collective-permute-start(bf16[256,1024]{1,0:T(8,128)(2,1)} %collective-permute-done.3.refs_7_), channel_id=1, source_target_pairs={{0,4},{4,0},{8,12},{12,8},{1,5},{5,1},{9,13},{13,9},{2,6},{6,2},{1... | collective-permute-start | bytes 1572872 | tf_op jit(solution)/shard_map/ppermute | solution.py:206
  74.7 24.6 %collective-permute-start.14 = (bf16[256,1024]{1,0:T(8,128)(2,1)}, bf16[256,1024]{1,0:T(8,128)(2,1)S(1)}, u32[]{:S(2)}, u32[]{:S(2)}) collective-permute-start(bf16[256,1024]{1,0:T(8,128)(2,1)} %collective-permute-done.6.refs_8_), channel_id=1, source_target_pairs={{0,4},{4,0},{8,12},{12,8},{1,5},{5,1},{9,13},{13,9},{2,6},{6,2},{1... | collective-permute-start | bytes 1572872 | tf_op jit(solution)/shard_map/ppermute | solution.py:206
  76.8 22.5 %collective-permute-start.12 = (bf16[256,1024]{1,0:T(8,128)(2,1)S(1)}, bf16[256,1024]{1,0:T(8,128)(2,1)S(1)}, u32[]{:S(2)}, u32[]{:S(2)}) collective-permute-start(bf16[256,1024]{1,0:T(8,128)(2,1)S(1)} %collective-permute-done.11.refs_7_), channel_id=1, source_target_pairs={{0,1},{1,0},{2,3},{3,2},{4,5},{5,4},{6,7},{7,6},{8,9},{9,8},{10,11... | collective-permute-start | bytes 1572872 | tf_op jit(solution)/shard_map/ppermute | solution.py:206
  87.7 22.1 %collective-permute-start.8 = (bf16[256,1024]{1,0:T(8,128)(2,1)S(1)}, bf16[256,1024]{1,0:T(8,128)(2,1)S(1)}, u32[]{:S(2)}, u32[]{:S(2)}) collective-permute-start(bf16[256,1024]{1,0:T(8,128)(2,1)S(1)} %collective-permute-done.7.refs_8_), channel_id=1, source_target_pairs={{0,4},{4,0},{8,12},{12,8},{1,5},{5,1},{9,13},{13,9},{2,6},{6,2},{1... | collective-permute-start | bytes 1572872 | tf_op jit(solution)/shard_map/ppermute | solution.py:206
  89.3 21.2 %collective-permute-start.5 = (bf16[256,1024]{1,0:T(8,128)(2,1)S(1)}, bf16[256,1024]{1,0:T(8,128)(2,1)S(1)}, u32[]{:S(2)}, u32[]{:S(2)}) collective-permute-start(bf16[256,1024]{1,0:T(8,128)(2,1)S(1)} %collective-permute-done.4.refs_11_), channel_id=1, source_target_pairs={{0,16},{16,0},{1,17},{17,1},{2,18},{18,2},{3,19},{19,3},{4,20},{20... | collective-permute-start | bytes 1572872 | tf_op jit(solution)/shard_map/ppermute | solution.py:206
  99.3 30.0 %collective-permute-start.13 = (bf16[256,1024]{1,0:T(8,128)(2,1)S(1)}, bf16[256,1024]{1,0:T(8,128)(2,1)S(1)}, u32[]{:S(2)}, u32[]{:S(2)}) collective-permute-start(bf16[256,1024]{1,0:T(8,128)(2,1)S(1)} %collective-permute-done.7.refs_8_), channel_id=1, source_target_pairs={{0,1},{1,0},{2,3},{3,2},{4,5},{5,4},{6,7},{7,6},{8,9},{9,8},{10,11... | collective-permute-start | bytes 1572872 | tf_op jit(solution)/shard_map/ppermute | solution.py:206
  99.3 30.0 %collective-permute-start.15 = (bf16[256,1024]{1,0:T(8,128)(2,1)S(1)}, bf16[256,1024]{1,0:T(8,128)(2,1)S(1)}, u32[]{:S(2)}, u32[]{:S(2)}) collective-permute-start(bf16[256,1024]{1,0:T(8,128)(2,1)S(1)} %collective-permute-done.4.refs_11_), channel_id=1, source_target_pairs={{0,1},{1,0},{2,3},{3,2},{4,5},{5,4},{6,7},{7,6},{8,9},{9,8},{10,11... | collective-permute-start | bytes 1572872 | tf_op jit(solution)/shard_map/ppermute | solution.py:206
  109.8 19.4 %collective-permute-start.16 = (bf16[256,1024]{1,0:T(8,128)(2,1)S(1)}, bf16[256,1024]{1,0:T(8,128)(2,1)S(1)}, u32[]{:S(2)}, u32[]{:S(2)}) collective-permute-start(bf16[256,1024]{1,0:T(8,128)(2,1)S(1)} %collective-permute-done.14.refs_12_), channel_id=1, source_target_pairs={{0,1},{1,0},{2,3},{3,2},{4,5},{5,4},{6,7},{7,6},{8,9},{9,8},{10,11... | collective-permute-start | bytes 1572872 | tf_op jit(solution)/shard_map/ppermute | solution.py:206
  110.5 23.6 %collective-permute-start.10 = (bf16[256,1024]{1,0:T(8,128)(2,1)S(1)}, bf16[256,1024]{1,0:T(8,128)(2,1)S(1)}, u32[]{:S(2)}, u32[]{:S(2)}) collective-permute-start(bf16[256,1024]{1,0:T(8,128)(2,1)S(1)} %collective-permute-done.8.refs_8_), channel_id=1, source_target_pairs={{0,1},{1,0},{2,3},{3,2},{4,5},{5,4},{6,7},{7,6},{8,9},{9,8},{10,11... | collective-permute-start | bytes 1572872 | tf_op jit(solution)/shard_map/ppermute | solution.py:206
  111.0 23.1 %collective-permute-start.9 = (bf16[256,1024]{1,0:T(8,128)(2,1)S(1)}, bf16[256,1024]{1,0:T(8,128)(2,1)S(1)}, u32[]{:S(2)}, u32[]{:S(2)}) collective-permute-start(bf16[256,1024]{1,0:T(8,128)(2,1)S(1)} %collective-permute-done.5.refs_7_), channel_id=1, source_target_pairs={{0,1},{1,0},{2,3},{3,2},{4,5},{5,4},{6,7},{7,6},{8,9},{9,8},{10,11... | collective-permute-start | bytes 1572872 | tf_op jit(solution)/shard_map/ppermute | solution.py:206
  111.1 1.2 copy-start.5
  112.3 2.2 %copy-start.6 = (bf16[1024,2048]{1,0:T(8,128)(2,1)S(1)}, bf16[1024,2048]{1,0:T(8,128)(2,1)}, u32[]{:S(2)}) copy-start(bf16[1024,2048]{1,0:T(8,128)(2,1)} %refs_7_.1) | copy-start | bytes 12582916
  (4 other events, 3.4 us)

commit v2 on v0

v2 whole, which is shorter than its diff:
```python
import functools

import jax
import jax.numpy as jnp
from jax import lax
from jax.experimental import pallas as pl
from jax.experimental.pallas import tpu as pltpu
from jax.sharding import PartitionSpec as P

ADAPTER_SCALE = 2.0
F32 = jnp.float32
BF16 = jnp.bfloat16
CONTRACT_LAST = (((1,), (1,)), ((), ()))
CONTRACT_FIRST = (((0,), (0,)), ((), ()))
VMEM = pl.BlockSpec(memory_space=pltpu.VMEM)
SMEM = pl.BlockSpec(memory_space=pltpu.SMEM)
HBM = pl.BlockSpec(memory_space=pltpu.HBM)
COST = pl.CostEstimate(flops=1, bytes_accessed=1, transcendentals=0)


def params(mib=16):
    return pltpu.CompilerParams(vmem_limit_bytes=mib << 20)


def weight_row(shard, rel, key):
    me = lax.axis_index("fsdp")
    row = jnp.bitwise_xor(me, rel) * shard
    if key is not None:
        row = row + quarter_row(shard, key)
    return row


def quarter_row(shard, key):
    group, data = lax.axis_index("groups"), lax.axis_index("dp")
    a, b = key
    return (((group + a) % 2) * 2 + (data + b) % 2) * (shard // 4)


def dot(a, b, dims=(((1,), (0,)), ((), ()))):
    return lax.dot_general(a, b, dims, preferred_element_type=F32)


def struct(shape, dtype=BF16):
    return jax.ShapeDtypeStruct(shape, dtype)


def prep_kernel(block, cuts, weight, *refs):
    outs, sems = refs[: len(cuts)], refs[len(cuts)]
    copies = []
    for i, (key, start, span) in enumerate(cuts):
        row = pl.multiple_of(quarter_row(weight.shape[0], key), block)
        source = weight.at[pl.ds(row, block), pl.ds(start, span)]
        copies.append(pltpu.make_async_copy(source, outs[i], sems.at[i]))
    for copy in copies:
        copy.start()
    for copy in copies:
        copy.wait()


def load_kernel(count, *refs):
    sems = refs[2 * count]
    copies = [
        pltpu.make_async_copy(refs[i], refs[count + i], sems.at[i]) for i in range(count)
    ]
    for copy in copies:
        copy.start()
    for copy in copies:
        copy.wait()


def low_rank_kernel(slots, rank2, width, kv, place, tok, cot, *refs):
    downs, ups = refs[:slots], refs[slots : 2 * slots]
    spread_low, spread_grad, down_cat, up_cat, keep, send = refs[2 * slots :]
    rows = tok.shape[0]
    me = lax.axis_index("fsdp")
    for r in range(slots):
        down_cat[pl.ds(r * rank2, rank2), :] = downs[r][0]
        up_cat[pl.ds(r * rank2, rank2), :] = ups[r][0]
    pos = me * rows + lax.broadcasted_iota(jnp.int32, (rows, slots * rank2), 0)
    col = lax.broadcasted_iota(jnp.int32, (rows, slots * rank2), 1)
    slot = col // rank2
    is_key = (col % rank2) < (rank2 // 2)
    own = jnp.full((rows, slots * rank2), -1, jnp.int32)
    start = jnp.int32(0)
    for u in range(slots):
        rel = jnp.bitwise_xor(place[slots + u], me)
        own = jnp.where(pos >= start, rel, own)
        start = start + place[u]
    mask = slot == own
    low = jnp.where(mask, dot(tok[...], down_cat[...], CONTRACT_LAST), 0.0).astype(BF16)
    spread_low[...] = low
    back_keys = dot(cot[:, :kv], up_cat[...], CONTRACT_LAST)
    back_vals = dot(cot[:, kv:], up_cat[...], CONTRACT_LAST)
    back = ADAPTER_SCALE * jnp.where(is_key, back_keys, back_vals)
    grad = jnp.where(mask, back, 0.0).astype(BF16)
    spread_grad[...] = grad

    def put(r, cols, value):
        ref = keep if r % 2 == 0 else send
        ref[r // 2, :, cols] = value.astype(BF16)

    step = 1024
    for start in range(0, width, step):
        part = dot(grad, tok[:, start : start + step], CONTRACT_FIRST)
        for r in range(slots):
            put(r, slice(start, start + step), part[r * rank2 : (r + 1) * rank2])
    part_keys = ADAPTER_SCALE * dot(low, cot[:, :kv], CONTRACT_FIRST)
    part_vals = ADAPTER_SCALE * dot(low, cot[:, kv:], CONTRACT_FIRST)
    row = lax.broadcasted_iota(jnp.int32, (slots * rank2, kv), 0)
    part = jnp.where((row % rank2) < (rank2 // 2), part_keys, part_vals)
    for r in range(slots):
        put(r, slice(width, width + kv), part[r * rank2 : (r + 1) * rank2])


def low_rank_call(place, tok, cot, downs, ups):
    slots = len(downs)
    rank2, width = downs[0].shape[1:]
    kv = ups[0].shape[2]
    rows = tok.shape[0]
    half = struct((slots // 2, rank2, width + kv))
    return pl.pallas_call(
        functools.partial(low_rank_kernel, slots, rank2, width, kv),
        out_shape=(
            struct((rows, slots * rank2)),
            struct((rows, slots * rank2)),
            struct((slots * rank2, width)),
            struct((slots * rank2, kv)),
            half,
            half,
        ),
        in_specs=[SMEM] + [VMEM] * (2 + 2 * slots),
        out_specs=(VMEM,) * 6,
        compiler_params=params(),
        cost_estimate=COST,
        name="low_rank",
    )(place, tok, cot, *downs, *ups)


def matmul_kernel(plan, block, shard, rank2, kv, first, last, *refs):
    refs = list(refs)
    tok, cot, low, grad, down, up = (refs.pop(0) for _ in range(6))
    sources = [[refs.pop(0) for _ in range(count)] for count, _, _ in plan]
    if not first:
        acc_in = refs.pop(0)
        refs.pop(0)
    out, gx = refs.pop(0), refs.pop(0)
    stage, sems = refs.pop(0), refs.pop(0)
    acc = out
    if first:
        col = lax.broadcasted_iota(jnp.int32, low.shape, 1)
        is_key = (col % rank2) < (rank2 // 2)
        zero = jnp.zeros(low.shape, BF16)
        low_keys = jnp.where(is_key, low[...], zero)
        low_vals = jnp.where(is_key, zero, low[...])
        acc[:, :kv] = ADAPTER_SCALE * dot(low_keys, up[...])
        acc[:, kv:] = ADAPTER_SCALE * dot(low_vals, up[...])
    copies, pieces = [], []
    for (_, entry, total), chunks in zip(plan, sources):
        for at in range(0, total, block):
            number = len(pieces)
            offset = pl.multiple_of(weight_row(shard, *entry) + at, block)
            where = pl.ds(offset, block)
            back = dot(grad[...], down[:, where])
            start, parts = 0, []
            for chunk in chunks:
                cols = slice(start, start + chunk.shape[1])
                start += chunk.shape[1]
                parts.append((cols, chunk, at))
                back += dot(cot[:, cols], chunk[pl.ds(at, block), :], CONTRACT_LAST)
            stage[number] = back.astype(BF16)
            copy = pltpu.make_async_copy(stage.at[number], gx.at[:, where], sems.at[number])
            copy.start()
            copies.append(copy)
            pieces.append((where, parts))
    edges = sorted({cols.stop for _, parts in pieces for cols, _, _ in parts})
    for low_edge, edge in zip([0] + edges, edges):
        cols = slice(low_edge, edge)
        total = acc[:, cols] if first else acc_in[:, cols]
        for where, parts in pieces:
            span, chunk, at = next(p for p in parts if p[0].stop >= edge)
            inner = slice(low_edge - span.start, edge - span.start)
            total += dot(tok[:, where], chunk[pl.ds(at, block), inner])
        if last:
            out[:, cols] = total.astype(BF16)
        else:
            out[:, cols] = total
    for copy in copies:
        copy.wait()


def matmul_call(shard, tok, cot, low, grad, down, up, sources, prev, last, rank2, name):
    rows, width = tok.shape
    cols = cot.shape[1]
    kv = up.shape[1]
    block = min(512, min(parts[0].shape[0] for _, parts in sources))
    plan = tuple((len(parts), entry, parts[0].shape[0]) for entry, parts in sources)
    flops = 4 * rows * cols * sum(total for _, _, total in plan)
    cost = pl.CostEstimate(flops=flops, bytes_accessed=1, transcendentals=0)
    count = sum(total // block for _, _, total in plan)
    arrays = [part for _, parts in sources for part in parts]
    args = [tok, cot, low, grad, down, up] + arrays
    in_specs = [VMEM] * (6 + len(arrays))
    first = prev is None
    aliases = {}
    if not first:
        args += list(prev)
        in_specs += [VMEM, HBM]
        aliases = {len(args) - 1: 1}
        if not last:
            aliases[len(args) - 2] = 0
    scratch = [pltpu.VMEM((count, rows, block), BF16), pltpu.SemaphoreType.DMA((count,))]
    return pl.pallas_call(
        functools.partial(matmul_kernel, plan, block, shard, rank2, kv, first, last),
        out_shape=(struct((rows, cols), BF16 if last else F32), struct((rows, width))),
        in_specs=in_specs,
        out_specs=(VMEM, HBM),
        scratch_shapes=scratch,
        input_output_aliases=aliases,
        compiler_params=params(),
        cost_estimate=cost,
        name=name,
    )(*args)


def even_odd_kernel(keep, recv, even, odd):
    for i in range(even.shape[0]):
        for out, j in ((even, 2 * i), (odd, 2 * i + 1)):
            out[i] = (keep[j].astype(F32) + recv[j].astype(F32)).astype(BF16)


def halves_kernel(keep, recv, mine, other):
    half = mine.shape[0]
    parity = lax.axis_index("dp") % 2
    for out, upper in ((mine, parity), (other, 1 - parity)):
        row = pl.ds(pl.multiple_of(upper * half, half), half)
        out[...] = (keep[0, row, :].astype(F32) + recv[0, row, :].astype(F32)).astype(BF16)


def finish_kernel(width, mine, recv, down, up):
    half = mine.shape[0]
    parity = lax.axis_index("dp") % 2
    for part, upper in ((mine, parity), (recv, 1 - parity)):
        row = pl.ds(pl.multiple_of(upper * half, half), half)
        down[0, row, :] = part[:, :width].astype(F32)
        up[0, row, :] = part[:, width:].astype(F32)


def xor_swap(value, axis, size, bit):
    return lax.ppermute(value, axis, [(i, i ^ bit) for i in range(size)])


PREP_MIB = 54
SPANS = (4, 8, 4)


def per_device(
    n_groups,
    n_dp,
    n_fsdp,
    tokens,
    key_value_weight,
    adapter_down_maps,
    adapter_up_maps,
    counts,
    tenant_slot_index,
    cotangent,
):
    rows, width = tokens.shape
    slots = tenant_slot_index.shape[0]
    rank2 = adapter_down_maps.shape[1]
    kv = adapter_up_maps.shape[2]
    shard = key_value_weight.shape[0]
    cols = key_value_weight.shape[1]
    swap = lambda value, bit: xor_swap(value, "fsdp", n_fsdp, bit)
    swap_y = lambda value: xor_swap(value, "groups", n_groups, 1)
    swap_z = lambda value: xor_swap(value, "dp", n_dp, 1)
    high_bits = [b for b in range(2, n_fsdp, 2)]
    quartered = n_groups == 2 and n_dp % 2 == 0 and n_fsdp == 4 and shard % 1024 == 0
    block = shard // 4
    place = jnp.concatenate([counts[0], tenant_slot_index])

    def local(kernel, outs, args, name, scratch=(), spaces=None, mib=16):
        spaces = spaces or [SMEM if a is place else VMEM for a in args]
        return pl.pallas_call(
            kernel,
            out_shape=tuple(outs),
            in_specs=spaces,
            out_specs=(VMEM,) * len(outs),
            scratch_shapes=list(scratch),
            compiler_params=params(mib),
            cost_estimate=COST,
            name=name,
        )(*args)

    barrier = lambda *values: lax.optimization_barrier(values)

    downs, ups = {0: adapter_down_maps}, {0: adapter_up_maps}
    for bit in high_bits + [1]:
        downs[bit], ups[bit] = swap(adapter_down_maps, bit), swap(adapter_up_maps, bit)
    sibling = swap(key_value_weight, 1)

    span = cols // 4
    if quartered:
        cuts, start = [], 0
        for size in SPANS:
            cuts.append(((0, 0), start * cols // 16, size * cols // 16))
            start += size
        start = SPANS[0] * cols // 16
        cuts.append(((1, 1), start, cols - start))
        sent = local(
            functools.partial(prep_kernel, block, cuts[:1]),
            [struct((block, size)) for _, _, size in cuts[:1]],
            (key_value_weight,),
            "prep",
            [pltpu.SemaphoreType.DMA((1,))],
            [HBM],
            PREP_MIB,
        )
        direct = [swap(sent[0], 2)]
        sent = list(sent) + list(
            local(
                functools.partial(prep_kernel, block, cuts[1:]),
                [struct((block, size)) for _, _, size in cuts[1:]],
                (key_value_weight,),
                "split",
                [pltpu.SemaphoreType.DMA((len(cuts) - 1,))],
                [HBM],
            )
        )
        first, second, *rest = sent
    loads = (tokens, cotangent, key_value_weight)
    tok, cot, weight = local(
        functools.partial(load_kernel, len(loads)),
        [struct(a.shape) for a in loads],
        loads,
        "load",
        [pltpu.SemaphoreType.DMA((len(loads),))],
        [HBM] * len(loads),
    )
    if quartered:
        direct[0], downs[2], ups[2], tok, second, sibling, *rest = barrier(
            direct[0], downs[2], ups[2], tok, second, sibling, *rest
        )
    for bit in high_bits:
        downs[bit], ups[bit], tok = barrier(downs[bit], ups[bit], tok)
        downs[bit + 1], ups[bit + 1] = swap(downs[bit], 1), swap(ups[bit], 1)

    low, grad, down_cat, up_cat, keep, send = low_rank_call(
        place, tok, cot, [downs[r] for r in range(slots)], [ups[r] for r in range(slots)]
    )

    def matmul(number, sources, prev, last=False):
        return matmul_call(
            shard,
            tok,
            cot,
            low,
            grad,
            down_cat,
            up_cat,
            sources,
            prev,
            last,
            rank2,
            f"matmul_{number}",
        )

    add = lambda a, b: (a.astype(F32) + b.astype(F32)).astype(BF16)
    half = struct((rank2 // 2, width + kv))
    finish = lambda mine, recv: local(
        functools.partial(finish_kernel, width),
        (struct((1, rank2, width), F32), struct((1, rank2, kv), F32)),
        (mine, recv),
        "finish",
    )
    recv = swap(send, 1)
    if not quartered:
        bit = 2
        while bit < n_fsdp:
            parts = struct((keep.shape[0] // 2,) + keep.shape[1:])
            keep, send = local(even_odd_kernel, (parts, parts), (keep, recv), "even_odd")
            recv = swap(send, bit)
            bit *= 2
        if n_dp == 1:
            total = add(keep[0], recv[0]).astype(F32)
            grad_down, grad_up = total[None, :, :width], total[None, :, width:]
        else:
            mine, other = local(halves_kernel, (half, half), (keep, recv), "halves")
            mine = add(mine, swap_z(other))
            bit = 2
            while bit < n_dp:
                mine = add(mine, xor_swap(mine, "dp", n_dp, bit))
                bit *= 2
            grad_down, grad_up = finish(mine, swap_z(mine))
        calls = [
            [((0, None), [weight])],
            [((1, None), [sibling])],
        ]
        for bit in high_bits:
            through = swap(key_value_weight, bit)
            calls.append(
                [
                    ((bit, None), [through]),
                    ((bit + 1, None), [swap(through, 1)]),
                ]
            )
        prev = None
        for number, sources in enumerate(calls):
            prev = matmul(number, sources, prev, number == len(calls) - 1)
        return prev[0], prev[1], grad_down, grad_up

    link = [keep]

    def after(*values):
        held = barrier(*values, *link)[: len(values)]
        link[:] = held[:1]
        return held if len(values) > 1 else held[0]

    def ready(values):
        held = after(*values)
        return list(held) if len(values) > 1 else [held]

    core = lambda parts: [swap(c, 1) for c in parts]
    parts = struct((1,) + keep.shape[1:])
    via_y, via_z = [swap_y(direct[0])], [swap_z(direct[0])]
    keep, recv = after(keep, recv)
    keep, send = local(even_odd_kernel, (parts, parts), (keep, recv), "even_odd")
    keep, send = after(keep, send)
    recv = swap(send, 2)
    low = after(low)
    prev = matmul(0, [((0, None), [weight])], None)
    second, *rest = after(second, *rest, *prev)[: len(sent) - 1]
    direct += [swap(c, 2) for c in (second, rest[0])]
    across = swap(rest[1], 2)
    recv, keep = after(recv, keep)
    mine, other = local(halves_kernel, (half, half), (keep, recv), "halves")
    mine, other = after(mine, other)
    recv = swap_z(other)
    via_z[0], via_y[0] = after(via_z[0], via_y[0])
    diagonal = [swap_y(via_z[0])]
    prev = after(*prev)
    prev = matmul(1, [((1, None), [sibling])], prev)
    prev = after(*prev)
    mine, recv = after(mine, recv)
    mine = after(add(mine, recv))
    bit = 2
    recv = xor_swap(mine, "dp", n_dp, bit) if n_dp > 2 else None
    diagonal[0] = after(diagonal[0])
    direct[1] = after(direct[1])
    via_y.append(swap_y(direct[1]))
    via_z.append(swap_z(direct[1]))
    direct[2] = after(direct[2])
    via_y.append(swap_y(direct[2]))
    via_z.append(swap_z(direct[2]))
    while bit < n_dp:
        if bit > 2:
            recv = xor_swap(mine, "dp", n_dp, bit)
        mine, recv = after(mine, recv)
        mine = after(add(mine, recv))
        bit *= 2
    other = swap_z(mine)

    prev = matmul(2, [((2, (0, 0)), direct)], prev)
    prev = after(*prev)
    mine, other = after(mine, other)
    grad_down, grad_up = after(*finish(mine, other))
    via_y[1], via_z[1] = after(via_y[1], via_z[1])
    via_y[2], via_z[2] = after(via_y[2], via_z[2])
    prev = matmul(3, [((2, (1, 0)), via_y), ((2, (0, 1)), via_z)], prev)
    prev = after(*prev)
    diagonal.append(after(across))
    crossed = [core(p) for p in (direct, diagonal, via_y, via_z)]
    prev = matmul(4, [((2, (1, 1)), diagonal)], prev)
    keys = ((0, 0), (1, 1), (1, 0), (0, 1))
    sources = [((3, key), p) for key, p in zip(keys, crossed)]
    prev = matmul(5, sources, prev, True)
    return prev[0], prev[1], grad_down, grad_up


def solution(mesh):
    in_specs = (
        P(("groups", "dp", "fsdp"), None),
        P("fsdp", None),
        P(("groups", "fsdp"), None, None),
        P(("groups", "fsdp"), None, None),
        P(("groups", "dp"), None),
        P("groups"),
        P(("groups", "dp", "fsdp"), None),
    )
    out_specs = (
        P(("groups", "dp", "fsdp"), None),
        P(("groups", "dp", "fsdp"), None),
        P(("groups", "fsdp"), None, None),
        P(("groups", "fsdp"), None, None),
    )
    body = functools.partial(
        per_device, mesh.shape["groups"], mesh.shape["dp"], mesh.shape["fsdp"]
    )
    return jax.shard_map(
        body, mesh=mesh, in_specs=in_specs, out_specs=out_specs, check_vma=False
    )
```

time: 270 us -> 84.8 us (0.31)
  waiting for transfers between devices: 161 us -> 34.1 us
  matrix products: 32.1 us -> 0 us
  starting transfers between devices: 0.2 us -> 29.2 us
  local copies, waits for them, and re-layouts: 13.8 us -> 0.18 us
  between operations: 13.9 us -> 0.88 us
  other arithmetic: 11 us -> 0.16 us
  Pallas kernels: 28.4 us -> 19.7 us
  blocking collectives: 7.54 us -> 0 us
    all_gather x2 -> x0, waiting for transfers between devices: 104 us -> none  [the longest x1 104 us: per_device(): lax.all_gather(key_value_weight, 'fsdp', axis=0, tiled=True)]
    reduce_scatter x2 -> x0, waiting for transfers between devices: 36.8 us -> none  [the longest x1 23.3 us: per_device(): lax.psum_scatter(part_up.astype(jnp.bfloat16), 'fsdp', scatter_dimension=...]
    ppermute x0 -> x34, waiting for transfers between devices: none -> 34.1 us  [xor_swap(): return lax.ppermute(value, axis, [(i, i ^ bit) for i in range(size)])]
    dot_general x5 -> x0, matrix products: 32.1 us -> none  [the longest x1 18.7 us: per_device(): lax.dot_general(cotangent, weights, contract, preferred_element_type=jnp....]
    ppermute x0 -> x34, starting transfers between devices: none -> 29.2 us  [xor_swap(): return lax.ppermute(value, axis, [(i, i ^ bit) for i in range(size)])]
    another operation x6 -> x0, Pallas kernels: 27 us -> none
    pallas_call x0 -> x13, Pallas kernels: none -> 19.7 us  [the longest x6 14.2 us: matmul_call(): pl.pallas_call(functools.partial(matmul_kernel, plan, block, shard, rank2...]
    psum x1 -> x0, waiting for transfers between devices: 19.4 us -> none  [per_device(): lax.psum(owned_sums[0].astype(jnp.bfloat16), 'dp').astype(jnp.float32)]
  transfers between devices with their start and end apart: 5 -> 34, of which waited for: 4 -> 13; matrix products, arithmetic and copies ran while one was open for 10% -> 0% of each run, Pallas kernels for 11% -> 16%
where the time goes in v2:
time: 84.8 us; the launch traced here: 84.2 us
  waiting for transfers between devices  34.1 us (40%)
  starting transfers between devices  29.2 us (34%)
  Pallas kernels  19.7 us (23%)
  between operations  0.88 us (1%)
    ppermute x34, waiting for transfers between devices, xor_swap(): return lax.ppermute(value, axis, [(i, i ^ bit) for i in range(size)])  34.1 us
    ppermute x34, starting transfers between devices, xor_swap(): return lax.ppermute(value, axis, [(i, i ^ bit) for i in range(size)])  29.2 us
    pallas_call x6, Pallas kernels, matmul_call(): pl.pallas_call(functools.partial(matmul_kernel, plan, block, shard, rank2...  14.2 us
    pallas_call x6, Pallas kernels, local(): pl.pallas_call(kernel, out_shape=tuple(outs), in_specs=spaces, out_specs=...  3.44 us
    pallas_call x1, Pallas kernels, low_rank_call(): pl.pallas_call(functools.partial(low_rank_kernel, slots, rank2, width, kv...  2.1 us
  transfers between devices with their start and end apart: 34, of which 13 were waited for; matrix products, arithmetic and copies ran while one was open for 0% of the time, Pallas kernels for 16%

profile of v2, /device:TPU:0, one launch (start us, length us, event | category | flops | bytes accessed | tf_op | source)
XLA Modules:
  0.0 84.2 jit_solution(17833894143676214830)
XLA Ops:
  1.2 1.7 %prep.1 = bf16[256,512]{1,0:T(8,128)(2,1)} custom-call(bf16[1024,2048]{1,0:T(8,128)(2,1)} %weight.3), custom_call_target="tpu_custom_call" | custom-call | flops 1 | bytes 1 | tf_op jit(solution)/shard_map/prep/pallas_call | solution.py:284
  2.9 2.7 %collective-permute-start = (bf16[256,512]{1,0:T(8,128)(2,1)}, bf16[256,512]{1,0:T(8,128)(2,1)S(1)}, u32[]{:S(2)}, u32[]{:S(2)}) collective-permute-start(bf16[256,512]{1,0:T(8,128)(2,1)} %prep.1), channel_id=1, source_target_pairs={{0,2},{1,3},{2,0},{3,1},{4,6},{5,7},{6,4},{7,5},{8,10},{9,11},{10,... | collective-permute-start | bytes 786440 | tf_op jit(solution)/shard_map/ppermute | solution.py:249
  5.7 1.9 %collective-permute-start.2 = (bf16[1,32,1024]{2,1,0:T(8,128)(2,1)}, bf16[1,32,1024]{2,1,0:T(8,128)(2,1)S(1)}, u32[]{:S(2)}, u32[]{:S(2)}) collective-permute-start(bf16[1,32,1024]{2,1,0:T(8,128)(2,1)} %refs_4_.1), channel_id=1, source_target_pairs={{0,2},{1,3},{2,0},{3,1},{4,6},{5,7},{6,4},{7,5},{8,10},{9,11},{10,... | collective-permute-start | bytes 196616 | tf_op jit(solution)/shard_map/ppermute | solution.py:249
  8.4 11.4 %collective-permute-done.2.refs_6_ = bf16[1,32,1024]{2,1,0:T(8,128)(2,1)S(1)} collective-permute-done((bf16[1,32,1024]{2,1,0:T(8,128)(2,1)}, bf16[1,32,1024]{2,1,0:T(8,128)(2,1)S(1)}, u32[]{:S(2)}, u32[]{:S(2)}) %collective-permute-start.2) | collective-permute-done | bytes 65568 | tf_op jit(solution)/shard_map/ppermute | solution.py:249
  20.5 0.9 %collective-permute-done.6.refs_5_ = bf16[1,32,1024]{2,1,0:T(8,128)(2,1)S(1)} collective-permute-done((bf16[1,32,1024]{2,1,0:T(8,128)(2,1)S(1)}, bf16[1,32,1024]{2,1,0:T(8,128)(2,1)S(1)}, u32[]{:S(2)}, u32[]{:S(2)}) %collective-permute-start.6) | collective-permute-done | bytes 65568 | tf_op jit(solution)/shard_map/ppermute | solution.py:249
  21.6 2.1 %low_rank.1 = (bf16[256,128]{1,0:T(8,128)(2,1)S(1)}, bf16[256,128]{1,0:T(8,128)(2,1)S(1)}, bf16[128,4096]{1,0:T(8,128)(2,1)S(1)}, bf16[128,1024]{1,0:T(8,128)(2,...) custom-call(s32[8]{0:T(128)S(1)} %pad_add_fusion.place, ...), custom_call_target="tpu_custom_call" | custom-call | flops 1 | bytes 1 | tf_op jit(solution)/shard_map/low_rank/pallas_call | solution.py:121
  23.9 1.9 %collective-permute-done.8.recv = bf16[2,32,5120]{2,1,0:T(8,128)(2,1)S(1)} collective-permute-done((bf16[2,32,5120]{2,1,0:T(8,128)(2,1)S(1)}, bf16[2,32,5120]{2,1,0:T(8,128)(2,1)S(1)}, u32[]{:S(2)}, u32[]{:S(2)}) %collective-permute-start.8) | collective-permute-done | bytes 655392 | tf_op jit(solution)/shard_map/ppermute | solution.py:249
  26.0 1.8 %collective-permute-start.13 = (bf16[1,32,5120]{2,1,0:T(8,128)(2,1)S(1)}, bf16[1,32,5120]{2,1,0:T(8,128)(2,1)S(1)}, u32[]{:S(2)}, u32[]{:S(2)}) collective-permute-start(bf16[1,32,5120]{2,1,0:T(8,128)(2,1)S(1)} %get-tuple-element.116), channel_id=1, source_target_pairs={{0,2},{1,3},{2,0},{3,1},{4,6},{5,7},{6,4},{7,5},{8,10},{9,11},{10,... | collective-permute-start | bytes 983048 | tf_op jit(solution)/shard_map/ppermute | solution.py:249
  27.8 1.6 %collective-permute-start.11 = (bf16[256,512]{1,0:T(8,128)(2,1)S(1)}, bf16[256,512]{1,0:T(8,128)(2,1)S(1)}, u32[]{:S(2)}, u32[]{:S(2)}) collective-permute-start(bf16[256,512]{1,0:T(8,128)(2,1)S(1)} %collective-permute-done.refs_6_), channel_id=1, source_target_pairs={{0,4},{4,0},{8,12},{12,8},{1,5},{5,1},{9,13},{13,9},{2,6},{6,2},{1... | collective-permute-start | bytes 786440 | tf_op jit(solution)/shard_map/ppermute | solution.py:249
  29.4 1.5 %collective-permute-start.12 = (bf16[256,512]{1,0:T(8,128)(2,1)S(1)}, bf16[256,512]{1,0:T(8,128)(2,1)S(1)}, u32[]{:S(2)}, u32[]{:S(2)}) collective-permute-start(bf16[256,512]{1,0:T(8,128)(2,1)S(1)} %collective-permute-done.refs_6_), channel_id=1, source_target_pairs={{0,16},{16,0},{1,17},{17,1},{2,18},{18,2},{3,19},{19,3},{4,20},{20... | collective-permute-start | bytes 786440 | tf_op jit(solution)/shard_map/ppermute | solution.py:249
  30.9 2.8 %matmul_0.1 = (f32[256,2048]{1,0:T(8,128)S(1)}, bf16[256,4096]{1,0:T(8,128)(2,1)}) custom-call(bf16[256,4096]{1,0:T(8,128)(2,1)S(1)} %get-tuple-element.92.tok.refs_0_, bf16[256,2048]{1,0:T(8,128)(2,1)S(1)} %get-tuple-element.93.cot.refs_1_, bf16[256,128]{1,0:T(8,128)(2,1)S(1)} %get-tuple-element.104.refs_2_, ...), custom_call_target="tpu_custom_call" | custom-call | flops 2147483648 | bytes 1 | tf_op jit(solution)/shard_map/matmul_0/pallas_call | solution.py:212
  34.3 1.5 %collective-permute-start.17 = (bf16[256,512]{1,0:T(8,128)(2,1)S(1)}, bf16[256,512]{1,0:T(8,128)(2,1)S(1)}, u32[]{:S(2)}, u32[]{:S(2)}) collective-permute-start(bf16[256,512]{1,0:T(8,128)(2,1)S(1)} %get-tuple-element.135), channel_id=1, source_target_pairs={{0,2},{1,3},{2,0},{3,1},{4,6},{5,7},{6,4},{7,5},{8,10},{9,11},{10,... | collective-permute-start | bytes 786440 | tf_op jit(solution)/shard_map/ppermute | solution.py:249
  36.1 1.1 %collective-permute-done.12.refs_6_ = bf16[256,512]{1,0:T(8,128)(2,1)S(1)} collective-permute-done((bf16[256,512]{1,0:T(8,128)(2,1)S(1)}, bf16[256,512]{1,0:T(8,128)(2,1)S(1)}, u32[]{:S(2)}, u32[]{:S(2)}) %collective-permute-start.12) | collective-permute-done | bytes 262176 | tf_op jit(solution)/shard_map/ppermute | solution.py:249
  37.2 1.5 %collective-permute-start.14 = (bf16[256,512]{1,0:T(8,128)(2,1)S(1)}, bf16[256,512]{1,0:T(8,128)(2,1)S(1)}, u32[]{:S(2)}, u32[]{:S(2)}) collective-permute-start(bf16[256,512]{1,0:T(8,128)(2,1)S(1)} %collective-permute-done.11.refs_9_), channel_id=1, source_target_pairs={{0,16},{16,0},{1,17},{17,1},{2,18},{18,2},{3,19},{19,3},{4,20},{20... | collective-permute-start | bytes 786440 | tf_op jit(solution)/shard_map/ppermute | solution.py:249
  38.9 1.5 %collective-permute-start.15 = (bf16[16,5120]{1,0:T(8,128)(2,1)S(1)}, bf16[16,5120]{1,0:T(8,128)(2,1)S(1)}, u32[]{:S(2)}, u32[]{:S(2)}) collective-permute-start(bf16[16,5120]{1,0:T(8,128)(2,1)S(1)} %get-tuple-element.123), channel_id=1, source_target_pairs={{0,4},{4,0},{8,12},{12,8},{1,5},{5,1},{9,13},{13,9},{2,6},{6,2},{1... | collective-permute-start | bytes 491528 | tf_op jit(solution)/shard_map/ppermute | solution.py:249
  40.4 2.7 %matmul_1.1 = (f32[256,2048]{1,0:T(8,128)S(1)}, bf16[256,4096]{1,0:T(8,128)(2,1)}) custom-call(bf16[256,4096]{1,0:T(8,128)(2,1)S(1)} %get-tuple-element.92.tok.refs_0_, bf16[256,2048]{1,0:T(8,128)(2,1)S(1)} %get-tuple-element.93.cot.refs_1_, bf16[256,128]{1,0:T(8,128)(2,1)S(1)} %get-tuple-element.104.refs_2_, ...), custom_call_target="tpu_custom_call", output_to_operand_aliasing={{1}: (8, {}), {0}: (7, {})} | custom-call | flops 2147483648 | bytes 1 | tf_op jit(solution)/shard_map/matmul_1/pallas_call | solution.py:212
  43.0 1.2 %collective-permute-done.15 = bf16[16,5120]{1,0:T(8,128)(2,1)S(1)} collective-permute-done((bf16[16,5120]{1,0:T(8,128)(2,1)S(1)}, bf16[16,5120]{1,0:T(8,128)(2,1)S(1)}, u32[]{:S(2)}, u32[]{:S(2)}) %collective-permute-start.15) | collective-permute-done | bytes 163872 | tf_op jit(solution)/shard_map/ppermute | solution.py:249
  44.3 2.7 %collective-permute-start.23 = (bf16[16,5120]{1,0:T(8,128)(2,1)S(1)}, bf16[16,5120]{1,0:T(8,128)(2,1)S(1)}, u32[]{:S(2)}, u32[]{:S(2)}) collective-permute-start(bf16[16,5120]{1,0:T(8,128)(2,1)S(1)} %add_convert_fusion.1), channel_id=1, source_target_pairs={{0,8},{4,12},{8,0},{12,4},{1,9},{5,13},{9,1},{13,5},{2,10},{6,14},... | collective-permute-start | bytes 491528 | tf_op jit(solution)/shard_map/ppermute | solution.py:249
  47.0 1.2 %collective-permute-start.20 = (bf16[256,1536]{1,0:T(8,128)(2,1)S(1)}, bf16[256,1536]{1,0:T(8,128)(2,1)S(1)}, u32[]{:S(2)}, u32[]{:S(2)}) collective-permute-start(bf16[256,1536]{1,0:T(8,128)(2,1)S(1)} %get-tuple-element.137), channel_id=1, source_target_pairs={{0,2},{1,3},{2,0},{3,1},{4,6},{5,7},{6,4},{7,5},{8,10},{9,11},{10,... | collective-permute-start | bytes 2359304 | tf_op jit(solution)/shard_map/ppermute | solution.py:249
  48.6 1.0 %collective-permute-start.21 = (bf16[256,1024]{1,0:T(8,128)(2,1)S(1)}, bf16[256,1024]{1,0:T(8,128)(2,1)S(1)}, u32[]{:S(2)}, u32[]{:S(2)}) collective-permute-start(bf16[256,1024]{1,0:T(8,128)(2,1)S(1)} %collective-permute-done.10.refs_7_), channel_id=1, source_target_pairs={{0,16},{16,0},{1,17},{17,1},{2,18},{18,2},{3,19},{19,3},{4,20},{20... | collective-permute-start | bytes 1572872 | tf_op jit(solution)/shard_map/ppermute | solution.py:249
  49.6 1.6 %collective-permute-start.22 = (bf16[256,1024]{1,0:T(8,128)(2,1)S(1)}, bf16[256,1024]{1,0:T(8,128)(2,1)S(1)}, u32[]{:S(2)}, u32[]{:S(2)}) collective-permute-start(bf16[256,1024]{1,0:T(8,128)(2,1)S(1)} %collective-permute-done.10.refs_7_), channel_id=1, source_target_pairs={{0,4},{4,0},{8,12},{12,8},{1,5},{5,1},{9,13},{13,9},{2,6},{6,2},{1... | collective-permute-start | bytes 1572872 | tf_op jit(solution)/shard_map/ppermute | solution.py:249
  51.2 3.0 %collective-permute-done.17.refs_8_ = bf16[256,512]{1,0:T(8,128)(2,1)S(1)} collective-permute-done((bf16[256,512]{1,0:T(8,128)(2,1)S(1)}, bf16[256,512]{1,0:T(8,128)(2,1)S(1)}, u32[]{:S(2)}, u32[]{:S(2)}) %collective-permute-start.17) | collective-permute-done | bytes 262176 | tf_op jit(solution)/shard_map/ppermute | solution.py:249
  54.3 1.2 %collective-permute-start.24 = (bf16[16,5120]{1,0:T(8,128)(2,1)S(1)}, bf16[16,5120]{1,0:T(8,128)(2,1)S(1)}, u32[]{:S(2)}, u32[]{:S(2)}) collective-permute-start(bf16[16,5120]{1,0:T(8,128)(2,1)S(1)} %add_convert_fusion.mine), channel_id=1, source_target_pairs={{0,4},{4,0},{8,12},{12,8},{1,5},{5,1},{9,13},{13,9},{2,6},{6,2},{1... | collective-permute-start | bytes 491528 | tf_op jit(solution)/shard_map/ppermute | solution.py:249
  55.4 1.5 %collective-permute-start.25 = (bf16[256,512]{1,0:T(8,128)(2,1)S(1)}, bf16[256,512]{1,0:T(8,128)(2,1)S(1)}, u32[]{:S(2)}, u32[]{:S(2)}) collective-permute-start(bf16[256,512]{1,0:T(8,128)(2,1)S(1)} %collective-permute-done.17.refs_8_), channel_id=1, source_target_pairs={{0,16},{16,0},{1,17},{17,1},{2,18},{18,2},{3,19},{19,3},{4,20},{20... | collective-permute-start | bytes 786440 | tf_op jit(solution)/shard_map/ppermute | solution.py:249
  56.9 9.2 %collective-permute-done.24.recv = bf16[16,5120]{1,0:T(8,128)(2,1)S(1)} collective-permute-done((bf16[16,5120]{1,0:T(8,128)(2,1)S(1)}, bf16[16,5120]{1,0:T(8,128)(2,1)S(1)}, u32[]{:S(2)}, u32[]{:S(2)}) %collective-permute-start.24) | collective-permute-done | bytes 163872 | tf_op jit(solution)/shard_map/ppermute | solution.py:249
  66.1 1.0 %collective-permute-start.26 = (bf16[256,512]{1,0:T(8,128)(2,1)S(1)}, bf16[256,512]{1,0:T(8,128)(2,1)S(1)}, u32[]{:S(2)}, u32[]{:S(2)}) collective-permute-start(bf16[256,512]{1,0:T(8,128)(2,1)S(1)} %collective-permute-done.17.refs_8_), channel_id=1, source_target_pairs={{0,4},{4,0},{8,12},{12,8},{1,5},{5,1},{9,13},{13,9},{2,6},{6,2},{1... | collective-permute-start | bytes 786440 | tf_op jit(solution)/shard_map/ppermute | solution.py:249
  67.2 1.5 %matmul_2.1 = (f32[256,2048]{1,0:T(8,128)S(1)}, bf16[256,4096]{1,0:T(8,128)(2,1)}) custom-call(bf16[256,4096]{1,0:T(8,128)(2,1)S(1)} %get-tuple-element.92.tok.refs_0_, bf16[256,2048]{1,0:T(8,128)(2,1)S(1)} %get-tuple-element.93.cot.refs_1_, bf16[256,128]{1,0:T(8,128)(2,1)S(1)} %get-tuple-element.104.refs_2_, ...), custom_call_target="tpu_custom_call", output_to_operand_aliasing={{1}: (10, {}), {0}: (9, {})} | custom-call | flops 536870912 | bytes 1 | tf_op jit(solution)/shard_map/matmul_2/pallas_call | solution.py:212
  70.2 2.4 %collective-permute-done.26.refs_11_ = bf16[256,512]{1,0:T(8,128)(2,1)S(1)} collective-permute-done((bf16[256,512]{1,0:T(8,128)(2,1)S(1)}, bf16[256,512]{1,0:T(8,128)(2,1)S(1)}, u32[]{:S(2)}, u32[]{:S(2)}) %collective-permute-start.26) | collective-permute-done | bytes 262176 | tf_op jit(solution)/shard_map/ppermute | solution.py:249
  72.6 1.7 %matmul_3.1 = (f32[256,2048]{1,0:T(8,128)S(1)}, bf16[256,4096]{1,0:T(8,128)(2,1)}) custom-call(bf16[256,4096]{1,0:T(8,128)(2,1)S(1)} %get-tuple-element.92.tok.refs_0_, bf16[256,2048]{1,0:T(8,128)(2,1)S(1)} %get-tuple-element.93.cot.refs_1_, bf16[256,128]{1,0:T(8,128)(2,1)S(1)} %get-tuple-element.104.refs_2_, ...), custom_call_target="tpu_custom_call", output_to_operand_aliasing={{1}: (13, {}), {0}: (12, {})} | custom-call | flops 1073741824 | bytes 1 | tf_op jit(solution)/shard_map/matmul_3/pallas_call | solution.py:212
  75.9 2.0 %collective-permute-done.19.refs_9_ = bf16[256,512]{1,0:T(8,128)(2,1)S(1)} collective-permute-done((bf16[256,512]{1,0:T(8,128)(2,1)S(1)}, bf16[256,512]{1,0:T(8,128)(2,1)S(1)}, u32[]{:S(2)}, u32[]{:S(2)}) %collective-permute-start.19) | collective-permute-done | bytes 262176 | tf_op jit(solution)/shard_map/ppermute | solution.py:249
  78.4 1.5 %matmul_4.1 = (f32[256,2048]{1,0:T(8,128)S(1)}, bf16[256,4096]{1,0:T(8,128)(2,1)}) custom-call(bf16[256,4096]{1,0:T(8,128)(2,1)S(1)} %get-tuple-element.92.tok.refs_0_, bf16[256,2048]{1,0:T(8,128)(2,1)S(1)} %get-tuple-element.93.cot.refs_1_, bf16[256,128]{1,0:T(8,128)(2,1)S(1)} %get-tuple-element.104.refs_2_, ...), custom_call_target="tpu_custom_call", output_to_operand_aliasing={{1}: (9, {}), {0}: (8, {})} | custom-call | flops 536870912 | bytes 1 | tf_op jit(solution)/shard_map/matmul_4/pallas_call | solution.py:212
  80.1 4.0 %matmul_5.1 = (bf16[256,2048]{1,0:T(8,128)(2,1)}, bf16[256,4096]{1,0:T(8,128)(2,1)}) custom-call(bf16[256,4096]{1,0:T(8,128)(2,1)S(1)} %get-tuple-element.92.tok.refs_0_, bf16[256,2048]{1,0:T(8,128)(2,1)S(1)} %get-tuple-element.93.cot.refs_1_, bf16[256,128]{1,0:T(8,128)(2,1)S(1)} %get-tuple-element.104.refs_2_, ...), custom_call_target="tpu_custom_call", output_to_operand_aliasing={{1}: (18, {})} | custom-call | flops 2147483648 | bytes 1 | tf_op jit(solution)/shard_map/matmul_5/pallas_call | solution.py:212
  (67 shorter events, 7.8 us)
Async XLA Ops:
  0.7 19.1 %collective-permute-start.3 = (bf16[1024,2048]{1,0:T(8,128)(2,1)}, bf16[1024,2048]{1,0:T(8,128)(2,1)S(1)}, u32[]{:S(2)}, u32[]{:S(2)}) collective-permute-start(bf16[1024,2048]{1,0:T(8,128)(2,1)} %weight.3), channel_id=1, source_target_pairs={{0,1},{1,0},{2,3},{3,2},{4,5},{5,4},{6,7},{7,6},{8,9},{9,8},{10,11... | collective-permute-start | bytes 12582920 | tf_op jit(solution)/shard_map/ppermute | solution.py:249
  2.9 16.9 %collective-permute-start = (bf16[256,512]{1,0:T(8,128)(2,1)}, bf16[256,512]{1,0:T(8,128)(2,1)S(1)}, u32[]{:S(2)}, u32[]{:S(2)}) collective-permute-start(bf16[256,512]{1,0:T(8,128)(2,1)} %prep.1), channel_id=1, source_target_pairs={{0,2},{1,3},{2,0},{3,1},{4,6},{5,7},{6,4},{7,5},{8,10},{9,11},{10,... | collective-permute-start | bytes 786440 | tf_op jit(solution)/shard_map/ppermute | solution.py:249
  5.6 14.1 %collective-permute-start.1 = (bf16[1,32,4096]{2,1,0:T(8,128)(2,1)S(1)}, bf16[1,32,4096]{2,1,0:T(8,128)(2,1)S(1)}, u32[]{:S(2)}, u32[]{:S(2)}) collective-permute-start(bf16[1,32,4096]{2,1,0:T(8,128)(2,1)S(1)} %copy-done.3), channel_id=1, source_target_pairs={{0,2},{1,3},{2,0},{3,1},{4,6},{5,7},{6,4},{7,5},{8,10},{9,11},{10,... | collective-permute-start | bytes 786440 | tf_op jit(solution)/shard_map/ppermute | solution.py:249
  5.7 14.1 %collective-permute-start.2 = (bf16[1,32,1024]{2,1,0:T(8,128)(2,1)}, bf16[1,32,1024]{2,1,0:T(8,128)(2,1)S(1)}, u32[]{:S(2)}, u32[]{:S(2)}) collective-permute-start(bf16[1,32,1024]{2,1,0:T(8,128)(2,1)} %refs_4_.1), channel_id=1, source_target_pairs={{0,2},{1,3},{2,0},{3,1},{4,6},{5,7},{6,4},{7,5},{8,10},{9,11},{10,... | collective-permute-start | bytes 196616 | tf_op jit(solution)/shard_map/ppermute | solution.py:249
  7.6 13.8 %collective-permute-start.4 = (bf16[1,32,4096]{2,1,0:T(8,128)(2,1)S(1)}, bf16[1,32,4096]{2,1,0:T(8,128)(2,1)S(1)}, u32[]{:S(2)}, u32[]{:S(2)}) collective-permute-start(bf16[1,32,4096]{2,1,0:T(8,128)(2,1)S(1)} %copy-done.3), channel_id=1, source_target_pairs={{0,1},{1,0},{2,3},{3,2},{4,5},{5,4},{6,7},{7,6},{8,9},{9,8},{10,11... | collective-permute-start | bytes 786440 | tf_op jit(solution)/shard_map/ppermute | solution.py:249
  19.7 1.8 %collective-permute-start.5 = (bf16[1,32,4096]{2,1,0:T(8,128)(2,1)S(1)}, bf16[1,32,4096]{2,1,0:T(8,128)(2,1)S(1)}, u32[]{:S(2)}, u32[]{:S(2)}) collective-permute-start(bf16[1,32,4096]{2,1,0:T(8,128)(2,1)S(1)} %collective-permute-done.1.refs_2_), channel_id=1, source_target_pairs={{0,1},{1,0},{2,3},{3,2},{4,5},{5,4},{6,7},{7,6},{8,9},{9,8},{10,11... | collective-permute-start | bytes 786440 | tf_op jit(solution)/shard_map/ppermute | solution.py:249
  23.7 2.2 %collective-permute-start.8 = (bf16[2,32,5120]{2,1,0:T(8,128)(2,1)S(1)}, bf16[2,32,5120]{2,1,0:T(8,128)(2,1)S(1)}, u32[]{:S(2)}, u32[]{:S(2)}) collective-permute-start(bf16[2,32,5120]{2,1,0:T(8,128)(2,1)S(1)} %get-tuple-element.98), channel_id=1, source_target_pairs={{0,1},{1,0},{2,3},{3,2},{4,5},{5,4},{6,7},{7,6},{8,9},{9,8},{10,11... | collective-permute-start | bytes 1966088 | tf_op jit(solution)/shard_map/ppermute | solution.py:249
  26.0 10.0 %collective-permute-start.13 = (bf16[1,32,5120]{2,1,0:T(8,128)(2,1)S(1)}, bf16[1,32,5120]{2,1,0:T(8,128)(2,1)S(1)}, u32[]{:S(2)}, u32[]{:S(2)}) collective-permute-start(bf16[1,32,5120]{2,1,0:T(8,128)(2,1)S(1)} %get-tuple-element.116), channel_id=1, source_target_pairs={{0,2},{1,3},{2,0},{3,1},{4,6},{5,7},{6,4},{7,5},{8,10},{9,11},{10,... | collective-permute-start | bytes 983048 | tf_op jit(solution)/shard_map/ppermute | solution.py:249
  27.8 8.2 %collective-permute-start.11 = (bf16[256,512]{1,0:T(8,128)(2,1)S(1)}, bf16[256,512]{1,0:T(8,128)(2,1)S(1)}, u32[]{:S(2)}, u32[]{:S(2)}) collective-permute-start(bf16[256,512]{1,0:T(8,128)(2,1)S(1)} %collective-permute-done.refs_6_), channel_id=1, source_target_pairs={{0,4},{4,0},{8,12},{12,8},{1,5},{5,1},{9,13},{13,9},{2,6},{6,2},{1... | collective-permute-start | bytes 786440 | tf_op jit(solution)/shard_map/ppermute | solution.py:249
  29.4 7.8 %collective-permute-start.12 = (bf16[256,512]{1,0:T(8,128)(2,1)S(1)}, bf16[256,512]{1,0:T(8,128)(2,1)S(1)}, u32[]{:S(2)}, u32[]{:S(2)}) collective-permute-start(bf16[256,512]{1,0:T(8,128)(2,1)S(1)} %collective-permute-done.refs_6_), channel_id=1, source_target_pairs={{0,16},{16,0},{1,17},{17,1},{2,18},{18,2},{3,19},{19,3},{4,20},{20... | collective-permute-start | bytes 786440 | tf_op jit(solution)/shard_map/ppermute | solution.py:249
  33.7 14.9 %collective-permute-start.10 = (bf16[256,1024]{1,0:T(8,128)(2,1)S(1)}, bf16[256,1024]{1,0:T(8,128)(2,1)S(1)}, u32[]{:S(2)}, u32[]{:S(2)}) collective-permute-start(bf16[256,1024]{1,0:T(8,128)(2,1)S(1)} %get-tuple-element.115), channel_id=1, source_target_pairs={{0,2},{1,3},{2,0},{3,1},{4,6},{5,7},{6,4},{7,5},{8,10},{9,11},{10,... | collective-permute-start | bytes 1572872 | tf_op jit(solution)/shard_map/ppermute | solution.py:249
  34.3 19.9 %collective-permute-start.17 = (bf16[256,512]{1,0:T(8,128)(2,1)S(1)}, bf16[256,512]{1,0:T(8,128)(2,1)S(1)}, u32[]{:S(2)}, u32[]{:S(2)}) collective-permute-start(bf16[256,512]{1,0:T(8,128)(2,1)S(1)} %get-tuple-element.135), channel_id=1, source_target_pairs={{0,2},{1,3},{2,0},{3,1},{4,6},{5,7},{6,4},{7,5},{8,10},{9,11},{10,... | collective-permute-start | bytes 786440 | tf_op jit(solution)/shard_map/ppermute | solution.py:249
  37.2 11.1 %collective-permute-start.14 = (bf16[256,512]{1,0:T(8,128)(2,1)S(1)}, bf16[256,512]{1,0:T(8,128)(2,1)S(1)}, u32[]{:S(2)}, u32[]{:S(2)}) collective-permute-start(bf16[256,512]{1,0:T(8,128)(2,1)S(1)} %collective-permute-done.11.refs_9_), channel_id=1, source_target_pairs={{0,16},{16,0},{1,17},{17,1},{2,18},{18,2},{3,19},{19,3},{4,20},{20... | collective-permute-start | bytes 786440 | tf_op jit(solution)/shard_map/ppermute | solution.py:249
  38.9 5.4 %collective-permute-start.15 = (bf16[16,5120]{1,0:T(8,128)(2,1)S(1)}, bf16[16,5120]{1,0:T(8,128)(2,1)S(1)}, u32[]{:S(2)}, u32[]{:S(2)}) collective-permute-start(bf16[16,5120]{1,0:T(8,128)(2,1)S(1)} %get-tuple-element.123), channel_id=1, source_target_pairs={{0,4},{4,0},{8,12},{12,8},{1,5},{5,1},{9,13},{13,9},{2,6},{6,2},{1... | collective-permute-start | bytes 491528 | tf_op jit(solution)/shard_map/ppermute | solution.py:249
  44.3 9.9 %collective-permute-start.23 = (bf16[16,5120]{1,0:T(8,128)(2,1)S(1)}, bf16[16,5120]{1,0:T(8,128)(2,1)S(1)}, u32[]{:S(2)}, u32[]{:S(2)}) collective-permute-start(bf16[16,5120]{1,0:T(8,128)(2,1)S(1)} %add_convert_fusion.1), channel_id=1, source_target_pairs={{0,8},{4,12},{8,0},{12,4},{1,9},{5,13},{9,1},{13,5},{2,10},{6,14},... | collective-permute-start | bytes 491528 | tf_op jit(solution)/shard_map/ppermute | solution.py:249
  47.0 27.2 %collective-permute-start.20 = (bf16[256,1536]{1,0:T(8,128)(2,1)S(1)}, bf16[256,1536]{1,0:T(8,128)(2,1)S(1)}, u32[]{:S(2)}, u32[]{:S(2)}) collective-permute-start(bf16[256,1536]{1,0:T(8,128)(2,1)S(1)} %get-tuple-element.137), channel_id=1, source_target_pairs={{0,2},{1,3},{2,0},{3,1},{4,6},{5,7},{6,4},{7,5},{8,10},{9,11},{10,... | collective-permute-start | bytes 2359304 | tf_op jit(solution)/shard_map/ppermute | solution.py:249
  48.6 18.6 %collective-permute-start.21 = (bf16[256,1024]{1,0:T(8,128)(2,1)S(1)}, bf16[256,1024]{1,0:T(8,128)(2,1)S(1)}, u32[]{:S(2)}, u32[]{:S(2)}) collective-permute-start(bf16[256,1024]{1,0:T(8,128)(2,1)S(1)} %collective-permute-done.10.refs_7_), channel_id=1, source_target_pairs={{0,16},{16,0},{1,17},{17,1},{2,18},{18,2},{3,19},{19,3},{4,20},{20... | collective-permute-start | bytes 1572872 | tf_op jit(solution)/shard_map/ppermute | solution.py:249
  49.6 20.0 %collective-permute-start.22 = (bf16[256,1024]{1,0:T(8,128)(2,1)S(1)}, bf16[256,1024]{1,0:T(8,128)(2,1)S(1)}, u32[]{:S(2)}, u32[]{:S(2)}) collective-permute-start(bf16[256,1024]{1,0:T(8,128)(2,1)S(1)} %collective-permute-done.10.refs_7_), channel_id=1, source_target_pairs={{0,4},{4,0},{8,12},{12,8},{1,5},{5,1},{9,13},{13,9},{2,6},{6,2},{1... | collective-permute-start | bytes 1572872 | tf_op jit(solution)/shard_map/ppermute | solution.py:249
  54.3 11.8 %collective-permute-start.24 = (bf16[16,5120]{1,0:T(8,128)(2,1)S(1)}, bf16[16,5120]{1,0:T(8,128)(2,1)S(1)}, u32[]{:S(2)}, u32[]{:S(2)}) collective-permute-start(bf16[16,5120]{1,0:T(8,128)(2,1)S(1)} %add_convert_fusion.mine), channel_id=1, source_target_pairs={{0,4},{4,0},{8,12},{12,8},{1,5},{5,1},{9,13},{13,9},{2,6},{6,2},{1... | collective-permute-start | bytes 491528 | tf_op jit(solution)/shard_map/ppermute | solution.py:249
  55.4 14.7 %collective-permute-start.25 = (bf16[256,512]{1,0:T(8,128)(2,1)S(1)}, bf16[256,512]{1,0:T(8,128)(2,1)S(1)}, u32[]{:S(2)}, u32[]{:S(2)}) collective-permute-start(bf16[256,512]{1,0:T(8,128)(2,1)S(1)} %collective-permute-done.17.refs_8_), channel_id=1, source_target_pairs={{0,16},{16,0},{1,17},{17,1},{2,18},{18,2},{3,19},{19,3},{4,20},{20... | collective-permute-start | bytes 786440 | tf_op jit(solution)/shard_map/ppermute | solution.py:249
  66.1 6.4 %collective-permute-start.26 = (bf16[256,512]{1,0:T(8,128)(2,1)S(1)}, bf16[256,512]{1,0:T(8,128)(2,1)S(1)}, u32[]{:S(2)}, u32[]{:S(2)}) collective-permute-start(bf16[256,512]{1,0:T(8,128)(2,1)S(1)} %collective-permute-done.17.refs_8_), channel_id=1, source_target_pairs={{0,4},{4,0},{8,12},{12,8},{1,5},{5,1},{9,13},{13,9},{2,6},{6,2},{1... | collective-permute-start | bytes 786440 | tf_op jit(solution)/shard_map/ppermute | solution.py:249
  67.2 7.7 %collective-permute-start.9 = (bf16[256,512]{1,0:T(8,128)(2,1)S(1)}, bf16[256,512]{1,0:T(8,128)(2,1)S(1)}, u32[]{:S(2)}, u32[]{:S(2)}) collective-permute-start(bf16[256,512]{1,0:T(8,128)(2,1)S(1)} %collective-permute-done.refs_6_), channel_id=1, source_target_pairs={{0,1},{1,0},{2,3},{3,2},{4,5},{5,4},{6,7},{7,6},{8,9},{9,8},{10,11... | collective-permute-start | bytes 786440 | tf_op jit(solution)/shard_map/ppermute | solution.py:249
  69.6 5.8 %collective-permute-start.31 = (bf16[256,512]{1,0:T(8,128)(2,1)S(1)}, bf16[256,512]{1,0:T(8,128)(2,1)S(1)}, u32[]{:S(2)}, u32[]{:S(2)}) collective-permute-start(bf16[256,512]{1,0:T(8,128)(2,1)S(1)} %collective-permute-done.11.refs_9_), channel_id=1, source_target_pairs={{0,1},{1,0},{2,3},{3,2},{4,5},{5,4},{6,7},{7,6},{8,9},{9,8},{10,11... | collective-permute-start | bytes 786440 | tf_op jit(solution)/shard_map/ppermute | solution.py:249
  70.1 4.8 %collective-permute-start.28 = (bf16[256,512]{1,0:T(8,128)(2,1)S(1)}, bf16[256,512]{1,0:T(8,128)(2,1)S(1)}, u32[]{:S(2)}, u32[]{:S(2)}) collective-permute-start(bf16[256,512]{1,0:T(8,128)(2,1)S(1)} %collective-permute-done.12.refs_6_), channel_id=1, source_target_pairs={{0,1},{1,0},{2,3},{3,2},{4,5},{5,4},{6,7},{7,6},{8,9},{9,8},{10,11... | collective-permute-start | bytes 786440 | tf_op jit(solution)/shard_map/ppermute | solution.py:249
  72.6 2.9 %collective-permute-start.18 = (bf16[256,512]{1,0:T(8,128)(2,1)S(1)}, bf16[256,512]{1,0:T(8,128)(2,1)S(1)}, u32[]{:S(2)}, u32[]{:S(2)}) collective-permute-start(bf16[256,512]{1,0:T(8,128)(2,1)S(1)} %collective-permute-done.17.refs_8_), channel_id=1, source_target_pairs={{0,1},{1,0},{2,3},{3,2},{4,5},{5,4},{6,7},{7,6},{8,9},{9,8},{10,11... | collective-permute-start | bytes 786440 | tf_op jit(solution)/shard_map/ppermute | solution.py:249
  74.3 4.0 %collective-permute-start.16 = (bf16[256,1024]{1,0:T(8,128)(2,1)S(1)}, bf16[256,1024]{1,0:T(8,128)(2,1)S(1)}, u32[]{:S(2)}, u32[]{:S(2)}) collective-permute-start(bf16[256,1024]{1,0:T(8,128)(2,1)S(1)} %collective-permute-done.10.refs_7_), channel_id=1, source_target_pairs={{0,1},{1,0},{2,3},{3,2},{4,5},{5,4},{6,7},{7,6},{8,9},{9,8},{10,11... | collective-permute-start | bytes 1572872 | tf_op jit(solution)/shard_map/ppermute | solution.py:249
  74.8 5.3 %collective-permute-start.27 = (bf16[256,1536]{1,0:T(8,128)(2,1)S(1)}, bf16[256,1536]{1,0:T(8,128)(2,1)S(1)}, u32[]{:S(2)}, u32[]{:S(2)}) collective-permute-start(bf16[256,1536]{1,0:T(8,128)(2,1)S(1)} %collective-permute-done.20.refs_7_), channel_id=1, source_target_pairs={{0,1},{1,0},{2,3},{3,2},{4,5},{5,4},{6,7},{7,6},{8,9},{9,8},{10,11... | collective-permute-start | bytes 2359304 | tf_op jit(solution)/shard_map/ppermute | solution.py:249
  74.9 2.9 %collective-permute-start.19 = (bf16[256,512]{1,0:T(8,128)(2,1)S(1)}, bf16[256,512]{1,0:T(8,128)(2,1)S(1)}, u32[]{:S(2)}, u32[]{:S(2)}) collective-permute-start(bf16[256,512]{1,0:T(8,128)(2,1)S(1)} %collective-permute-done.14.refs_6_), channel_id=1, source_target_pairs={{0,1},{1,0},{2,3},{3,2},{4,5},{5,4},{6,7},{7,6},{8,9},{9,8},{10,11... | collective-permute-start | bytes 786440 | tf_op jit(solution)/shard_map/ppermute | solution.py:249
  75.4 4.8 %collective-permute-start.29 = (bf16[256,1024]{1,0:T(8,128)(2,1)S(1)}, bf16[256,1024]{1,0:T(8,128)(2,1)S(1)}, u32[]{:S(2)}, u32[]{:S(2)}) collective-permute-start(bf16[256,1024]{1,0:T(8,128)(2,1)S(1)} %collective-permute-done.21.refs_7_), channel_id=1, source_target_pairs={{0,1},{1,0},{2,3},{3,2},{4,5},{5,4},{6,7},{7,6},{8,9},{9,8},{10,11... | collective-permute-start | bytes 1572872 | tf_op jit(solution)/shard_map/ppermute | solution.py:249
  75.4 4.7 %collective-permute-start.32 = (bf16[256,1024]{1,0:T(8,128)(2,1)S(1)}, bf16[256,1024]{1,0:T(8,128)(2,1)S(1)}, u32[]{:S(2)}, u32[]{:S(2)}) collective-permute-start(bf16[256,1024]{1,0:T(8,128)(2,1)S(1)} %collective-permute-done.22.refs_10_), channel_id=1, source_target_pairs={{0,1},{1,0},{2,3},{3,2},{4,5},{5,4},{6,7},{7,6},{8,9},{9,8},{10,11... | collective-permute-start | bytes 1572872 | tf_op jit(solution)/shard_map/ppermute | solution.py:249
  77.9 2.1 %collective-permute-start.30 = (bf16[256,512]{1,0:T(8,128)(2,1)S(1)}, bf16[256,512]{1,0:T(8,128)(2,1)S(1)}, u32[]{:S(2)}, u32[]{:S(2)}) collective-permute-start(bf16[256,512]{1,0:T(8,128)(2,1)S(1)} %collective-permute-done.25.refs_8_), channel_id=1, source_target_pairs={{0,1},{1,0},{2,3},{3,2},{4,5},{5,4},{6,7},{7,6},{8,9},{9,8},{10,11... | collective-permute-start | bytes 786440 | tf_op jit(solution)/shard_map/ppermute | solution.py:249
  78.2 1.9 %collective-permute-start.33 = (bf16[256,512]{1,0:T(8,128)(2,1)S(1)}, bf16[256,512]{1,0:T(8,128)(2,1)S(1)}, u32[]{:S(2)}, u32[]{:S(2)}) collective-permute-start(bf16[256,512]{1,0:T(8,128)(2,1)S(1)} %collective-permute-done.26.refs_11_), channel_id=1, source_target_pairs={{0,1},{1,0},{2,3},{3,2},{4,5},{5,4},{6,7},{7,6},{8,9},{9,8},{10,11... | collective-permute-start | bytes 786440 | tf_op jit(solution)/shard_map/ppermute | solution.py:249
  (9 other events, 61.9 us)

commit v3 on v2

--- a/solution.py
+++ b/solution.py
@@ -57,6 +57,23 @@
         copy.wait()
 
 
+def pack_kernel(block, cuts, weight, down, up, pack, *refs):
+    outs, sems = refs[: len(cuts)], refs[len(cuts)]
+    width = down.shape[2]
+    moves = [
+        (down.at[0], pack.at[:, pl.ds(0, width)]),
+        (up.at[0], pack.at[:, pl.ds(width, up.shape[2])]),
+    ]
+    for out, (key, start, span) in zip(outs, cuts):
+        row = pl.multiple_of(quarter_row(weight.shape[0], key), block)
+        moves.append((weight.at[pl.ds(row, block), pl.ds(start, span)], out))
+    copies = [pltpu.make_async_copy(a, b, sems.at[i]) for i, (a, b) in enumerate(moves)]
+    for copy in copies:
+        copy.start()
+    for copy in copies:
+        copy.wait()
+
+
 def load_kernel(count, *refs):
     sems = refs[2 * count]
     copies = [
@@ -69,13 +86,13 @@
 
 
 def low_rank_kernel(slots, rank2, width, kv, place, tok, cot, *refs):
-    downs, ups = refs[:slots], refs[slots : 2 * slots]
-    spread_low, spread_grad, down_cat, up_cat, keep, send = refs[2 * slots :]
+    packs = refs[:slots]
+    spread_low, spread_grad, down_cat, up_cat, keep, send = refs[slots:]
     rows = tok.shape[0]
     me = lax.axis_index("fsdp")
     for r in range(slots):
-        down_cat[pl.ds(r * rank2, rank2), :] = downs[r][0]
-        up_cat[pl.ds(r * rank2, rank2), :] = ups[r][0]
+        down_cat[pl.ds(r * rank2, rank2), :] = packs[r][:, :width]
+        up_cat[pl.ds(r * rank2, rank2), :] = packs[r][:, width:]
     pos = me * rows + lax.broadcasted_iota(jnp.int32, (rows, slots * rank2), 0)
     col = lax.broadcasted_iota(jnp.int32, (rows, slots * rank2), 1)
     slot = col // rank2
@@ -112,10 +129,9 @@
         put(r, slice(width, width + kv), part[r * rank2 : (r + 1) * rank2])
 
 
-def low_rank_call(place, tok, cot, downs, ups):
-    slots = len(downs)
-    rank2, width = downs[0].shape[1:]
-    kv = ups[0].shape[2]
+def low_rank_call(place, tok, cot, packs, width, kv):
+    slots = len(packs)
+    rank2 = packs[0].shape[0]
     rows = tok.shape[0]
     half = struct((slots // 2, rank2, width + kv))
     return pl.pallas_call(
@@ -128,12 +144,12 @@
             half,
             half,
         ),
-        in_specs=[SMEM] + [VMEM] * (2 + 2 * slots),
+        in_specs=[SMEM] + [VMEM] * (2 + slots),
         out_specs=(VMEM,) * 6,
         compiler_params=params(),
         cost_estimate=COST,
         name="low_rank",
-    )(place, tok, cot, *downs, *ups)
+    )(place, tok, cot, *packs)
 
 
 def matmul_kernel(plan, block, shard, rank2, kv, first, last, *refs):
@@ -250,7 +266,12 @@
 
 
 PREP_MIB = 54
-SPANS = (4, 8, 4)
+SPANS = (7, 9)
+DIAGONAL_AT = 1
+CORE_AT = 1
+CORE_GATE = False
+DIAGONAL_MM = True
+LATE_FINISH = True
 
 
 def per_device(
@@ -294,28 +315,28 @@
 
     barrier = lambda *values: lax.optimization_barrier(values)
 
-    downs, ups = {0: adapter_down_maps}, {0: adapter_up_maps}
-    for bit in high_bits + [1]:
-        downs[bit], ups[bit] = swap(adapter_down_maps, bit), swap(adapter_up_maps, bit)
-    sibling = swap(key_value_weight, 1)
-
-    span = cols // 4
+    cuts, start = [], 0
     if quartered:
-        cuts, start = [], 0
         for size in SPANS:
             cuts.append(((0, 0), start * cols // 16, size * cols // 16))
             start += size
         start = SPANS[0] * cols // 16
         cuts.append(((1, 1), start, cols - start))
-        sent = local(
-            functools.partial(prep_kernel, block, cuts[:1]),
-            [struct((block, size)) for _, _, size in cuts[:1]],
-            (key_value_weight,),
-            "prep",
-            [pltpu.SemaphoreType.DMA((1,))],
-            [HBM],
-            PREP_MIB,
-        )
+
+    pack, *sent = local(
+        functools.partial(pack_kernel, block, cuts[:1]),
+        [struct((rank2, width + kv))] + [struct((block, size)) for _, _, size in cuts[:1]],
+        (key_value_weight, adapter_down_maps, adapter_up_maps),
+        "prep",
+        [pltpu.SemaphoreType.DMA((2 + len(cuts[:1]),))],
+        [HBM, HBM, HBM],
+        PREP_MIB,
+    )
+    packs = {0: pack}
+    for bit in high_bits + [1]:
+        packs[bit] = swap(pack, bit)
+    sibling = swap(key_value_weight, 1)
+    if quartered:
         direct = [swap(sent[0], 2)]
         sent = list(sent) + list(
             local(
@@ -338,15 +359,17 @@
         [HBM] * len(loads),
     )
     if quartered:
-        direct[0], downs[2], ups[2], tok, second, sibling, *rest = barrier(
-            direct[0], downs[2], ups[2], tok, second, sibling, *rest
+        packs[2], tok, second, sibling, *rest = barrier(
+            packs[2], tok, second, sibling, *rest
         )
     for bit in high_bits:
-        downs[bit], ups[bit], tok = barrier(downs[bit], ups[bit], tok)
-        downs[bit + 1], ups[bit + 1] = swap(downs[bit], 1), swap(ups[bit], 1)
-
+        packs[bit], tok = barrier(packs[bit], tok)
+        packs[bit + 1] = swap(packs[bit], 1)
+
+    if quartered:
+        direct[0], tok, packs[3] = barrier(direct[0], tok, packs[3])
     low, grad, down_cat, up_cat, keep, send = low_rank_call(
-        place, tok, cot, [downs[r] for r in range(slots)], [ups[r] for r in range(slots)]
+        place, tok, cot, [packs[r] for r in range(slots)], width, kv
     )
 
     def matmul(number, sources, prev, last=False):
@@ -422,16 +445,17 @@
 
     core = lambda parts: [swap(c, 1) for c in parts]
     parts = struct((1,) + keep.shape[1:])
+    ahead = core(direct)
     via_y, via_z = [swap_y(direct[0])], [swap_z(direct[0])]
-    keep, recv = after(keep, recv)
+    keep, recv, ahead[0] = after(keep, recv, ahead[0])
     keep, send = local(even_odd_kernel, (parts, parts), (keep, recv), "even_odd")
     keep, send = after(keep, send)
     recv = swap(send, 2)
     low = after(low)
     prev = matmul(0, [((0, None), [weight])], None)
-    second, *rest = after(second, *rest, *prev)[: len(sent) - 1]
-    direct += [swap(c, 2) for c in (second, rest[0])]
-    across = swap(rest[1], 2)
+    rest = list(after(*sent[1:], *prev)[: len(sent) - 1])
+    direct += [swap(c, 2) for c in rest[:-1]]
+    across = swap(rest[-1], 2)
     recv, keep = after(recv, keep)
     mine, other = local(halves_kernel, (half, half), (keep, recv), "halves")
     mine, other = after(mine, other)
@@ -445,13 +469,12 @@
     mine = after(add(mine, recv))
     bit = 2
     recv = xor_swap(mine, "dp", n_dp, bit) if n_dp > 2 else None
-    diagonal[0] = after(diagonal[0])
-    direct[1] = after(direct[1])
-    via_y.append(swap_y(direct[1]))
-    via_z.append(swap_z(direct[1]))
-    direct[2] = after(direct[2])
-    via_y.append(swap_y(direct[2]))
-    via_z.append(swap_z(direct[2]))
+    for i in range(1, len(direct)):
+        direct[i] = after(direct[i])
+        via_y.append(swap_y(direct[i]))
+        via_z.append(swap_z(direct[i]))
+        if i == 1 and DIAGONAL_AT == 1:
+            diagonal[0] = after(diagonal[0])
     while bit < n_dp:
         if bit > 2:
             recv = xor_swap(mine, "dp", n_dp, bit)
@@ -459,19 +482,45 @@
         mine = after(add(mine, recv))
         bit *= 2
     other = swap_z(mine)
-
-    prev = matmul(2, [((2, (0, 0)), direct)], prev)
+    if DIAGONAL_AT == 2:
+        diagonal[0] = after(diagonal[0])
+
+    if CORE_AT == 1:
+        ahead[1:] = ready(ahead[:1] + core(direct[1:]))[1:]
+    sources = [((2, (0, 0)), direct)]
+    if CORE_AT == 1:
+        sources.append(((3, (0, 0)), ahead))
+    prev = matmul(2, sources, prev)
     prev = after(*prev)
-    mine, other = after(mine, other)
-    grad_down, grad_up = after(*finish(mine, other))
-    via_y[1], via_z[1] = after(via_y[1], via_z[1])
-    via_y[2], via_z[2] = after(via_y[2], via_z[2])
-    prev = matmul(3, [((2, (1, 0)), via_y), ((2, (0, 1)), via_z)], prev)
-    prev = after(*prev)
+    if not LATE_FINISH:
+        mine, other = after(mine, other)
+        grad_down, grad_up = after(*finish(mine, other))
+    if DIAGONAL_AT == 3:
+        diagonal[0] = after(diagonal[0])
     diagonal.append(after(across))
-    crossed = [core(p) for p in (direct, diagonal, via_y, via_z)]
-    prev = matmul(4, [((2, (1, 1)), diagonal)], prev)
-    keys = ((0, 0), (1, 1), (1, 0), (0, 1))
+    if DIAGONAL_MM:
+        prev = matmul(3, [((2, (1, 1)), diagonal)], prev)
+        prev = after(*prev)
+    for i in range(1, len(direct)):
+        via_y[i], via_z[i] = after(via_y[i], via_z[i])
+    groups = [diagonal, via_y, via_z]
+    if CORE_AT != 1:
+        groups.append(direct)
+    if CORE_GATE:
+        flat = iter(after(*[p for group in groups for p in group]))
+        groups = [[next(flat) for _ in group] for group in groups]
+    crossed = [core(p) for p in groups[:3]]
+    if CORE_AT != 1:
+        crossed.append(ahead + core(groups[3][1:]))
+    sources = [((2, (1, 0)), via_y), ((2, (0, 1)), via_z)]
+    if not DIAGONAL_MM:
+        sources.append(((2, (1, 1)), diagonal))
+    prev = matmul(4, sources, prev)
+    if LATE_FINISH:
+        prev = after(*prev)
+        mine, other = after(mine, other)
+        grad_down, grad_up = after(*finish(mine, other))
+    keys = ((1, 1), (1, 0), (0, 1), (0, 0))
     sources = [((3, key), p) for key, p in zip(keys, crossed)]
     prev = matmul(5, sources, prev, True)
     return prev[0], prev[1], grad_down, grad_up

time: 84.8 us -> 80.5 us (0.949)
  starting transfers between devices: 29.2 us -> 20.8 us
  waiting for transfers between devices: 34.1 us -> 36.7 us
  local copies, waits for them, and re-layouts: 0.18 us -> 1.83 us
    ppermute x34 -> x25, starting transfers between devices: 29.2 us -> 20.8 us  [xor_swap(): return lax.ppermute(value, axis, [(i, i ^ bit) for i in range(size)])]
    ppermute x34 -> x25, waiting for transfers between devices: 34.1 us -> 36.7 us  [xor_swap(): return lax.ppermute(value, axis, [(i, i ^ bit) for i in range(size)])]
    unnamed x15 -> x13, local copies, waits for them, and re-layouts: 0.18 us -> 1.83 us
  transfers between devices with their start and end apart: 34 -> 25, of which waited for: 13 -> 11; matrix products, arithmetic and copies ran while one was open for 0% -> 0% of each run, Pallas kernels for 16% -> 18%
where the time goes in v3:
time: 80.5 us; the launch traced here: 80.3 us
  waiting for transfers between devices  36.7 us (46%)
  starting transfers between devices  20.8 us (26%)
  Pallas kernels  20.1 us (25%)
  local copies, waits for them, and re-layouts  1.83 us (2%)
    ppermute x25, waiting for transfers between devices, xor_swap(): return lax.ppermute(value, axis, [(i, i ^ bit) for i in range(size)])  36.7 us
    ppermute x25, starting transfers between devices, xor_swap(): return lax.ppermute(value, axis, [(i, i ^ bit) for i in range(size)])  20.8 us
    pallas_call x6, Pallas kernels, matmul_call(): pl.pallas_call(functools.partial(matmul_kernel, plan, block, shard, rank2...  13.9 us
    pallas_call x6, Pallas kernels, local(): pl.pallas_call(kernel, out_shape=tuple(outs), in_specs=spaces, out_specs=...  4.05 us
    pallas_call x1, Pallas kernels, low_rank_call(): pl.pallas_call(functools.partial(low_rank_kernel, slots, rank2, width, kv...  2.1 us
    unnamed x13, local copies, waits for them, and re-layouts  1.83 us
  transfers between devices with their start and end apart: 25, of which 11 were waited for; matrix products, arithmetic and copies ran while one was open for 0% of the time, Pallas kernels for 18%

profile of v3, /device:TPU:0, one launch (start us, length us, event | category | flops | bytes accessed | tf_op | source)
XLA Modules:
  0.0 80.3 jit_solution(4811998508598396244)
XLA Ops:
  1.2 2.3 %prep.1 = (bf16[32,5120]{1,0:T(8,128)(2,1)}, bf16[256,896]{1,0:T(8,128)(2,1)}) custom-call(bf16[1024,2048]{1,0:T(8,128)(2,1)} %weight.3, bf16[1,32,4096]{2,1,0:T(8,128)(2,1)} %down.1, bf16[1,32,1024]{2,1,0:T(8,128)(2,1)} %up.1), custom_call_target="tpu_custom_call" | custom-call | flops 1 | bytes 1 | tf_op jit(solution)/shard_map/prep/pallas_call | solution.py:305
  3.5 2.5 %collective-permute-start.1 = (bf16[32,5120]{1,0:T(8,128)(2,1)}, bf16[32,5120]{1,0:T(8,128)(2,1)S(1)}, u32[]{:S(2)}, u32[]{:S(2)}) collective-permute-start(bf16[32,5120]{1,0:T(8,128)(2,1)} %get-tuple-element.82.refs_0_), channel_id=1, source_target_pairs={{0,2},{1,3},{2,0},{3,1},{4,6},{5,7},{6,4},{7,5},{8,10},{9,11},{10,... | collective-permute-start | bytes 983048 | tf_op jit(solution)/shard_map/ppermute | solution.py:265
  6.2 1.3 %copy-done.1 = bf16[256,4096]{1,0:T(8,128)(2,1)S(1)} copy-done((bf16[256,4096]{1,0:T(8,128)(2,1)S(1)}, bf16[256,4096]{1,0:T(8,128)(2,1)}, u32[]{:S(2)}) %copy-start.1) | copy-done | bytes 2097176
  8.3 6.4 %collective-permute-done.1.refs_2_ = bf16[32,5120]{1,0:T(8,128)(2,1)S(1)} collective-permute-done((bf16[32,5120]{1,0:T(8,128)(2,1)}, bf16[32,5120]{1,0:T(8,128)(2,1)S(1)}, u32[]{:S(2)}, u32[]{:S(2)}) %collective-permute-start.1) | collective-permute-done | bytes 327712 | tf_op jit(solution)/shard_map/ppermute | solution.py:265
  15.3 9.2 %collective-permute-done.refs_6_ = bf16[256,896]{1,0:T(8,128)(2,1)S(1)} collective-permute-done((bf16[256,896]{1,0:T(8,128)(2,1)}, bf16[256,896]{1,0:T(8,128)(2,1)S(1)}, u32[]{:S(2)}, u32[]{:S(2)}) %collective-permute-start) | collective-permute-done | bytes 458784 | tf_op jit(solution)/shard_map/ppermute | solution.py:265
  24.5 2.1 %low_rank.1 = (bf16[256,128]{1,0:T(8,128)(2,1)S(1)}, bf16[256,128]{1,0:T(8,128)(2,1)S(1)}, bf16[128,4096]{1,0:T(8,128)(2,1)S(1)}, bf16[128,1024]{1,0:T(8,128)(2,...) custom-call(s32[8]{0:T(128)S(1)} %pad_add_fusion.place, ...), custom_call_target="tpu_custom_call" | custom-call | flops 1 | bytes 1 | tf_op jit(solution)/shard_map/low_rank/pallas_call | solution.py:137
  27.2 1.9 %collective-permute-start.7 = (bf16[256,896]{1,0:T(8,128)(2,1)S(1)}, bf16[256,896]{1,0:T(8,128)(2,1)S(1)}, u32[]{:S(2)}, u32[]{:S(2)}) collective-permute-start(bf16[256,896]{1,0:T(8,128)(2,1)S(1)} %collective-permute-done.refs_6_), channel_id=1, source_target_pairs={{0,4},{4,0},{8,12},{12,8},{1,5},{5,1},{9,13},{13,9},{2,6},{6,2},{1... | collective-permute-start | bytes 1376264 | tf_op jit(solution)/shard_map/ppermute | solution.py:265
  29.0 1.5 %collective-permute-start.8 = (bf16[256,896]{1,0:T(8,128)(2,1)S(1)}, bf16[256,896]{1,0:T(8,128)(2,1)S(1)}, u32[]{:S(2)}, u32[]{:S(2)}) collective-permute-start(bf16[256,896]{1,0:T(8,128)(2,1)S(1)} %collective-permute-done.refs_6_), channel_id=1, source_target_pairs={{0,16},{16,0},{1,17},{17,1},{2,18},{18,2},{3,19},{19,3},{4,20},{20... | collective-permute-start | bytes 1376264 | tf_op jit(solution)/shard_map/ppermute | solution.py:265
  30.7 1.6 %collective-permute-start.9 = (bf16[1,32,5120]{2,1,0:T(8,128)(2,1)S(1)}, bf16[1,32,5120]{2,1,0:T(8,128)(2,1)S(1)}, u32[]{:S(2)}, u32[]{:S(2)}) collective-permute-start(bf16[1,32,5120]{2,1,0:T(8,128)(2,1)S(1)} %get-tuple-element.106), channel_id=1, source_target_pairs={{0,2},{1,3},{2,0},{3,1},{4,6},{5,7},{6,4},{7,5},{8,10},{9,11},{10,... | collective-permute-start | bytes 983048 | tf_op jit(solution)/shard_map/ppermute | solution.py:265
  32.3 2.7 %matmul_0.1 = (f32[256,2048]{1,0:T(8,128)S(1)}, bf16[256,4096]{1,0:T(8,128)(2,1)}) custom-call(bf16[256,4096]{1,0:T(8,128)(2,1)S(1)} %get-tuple-element.90.tok.refs_0_, bf16[256,2048]{1,0:T(8,128)(2,1)S(1)} %get-tuple-element.91.cot.refs_1_, bf16[256,128]{1,0:T(8,128)(2,1)S(1)} %get-tuple-element.102.refs_2_, ...), custom_call_target="tpu_custom_call" | custom-call | flops 2147483648 | bytes 1 | tf_op jit(solution)/shard_map/matmul_0/pallas_call | solution.py:228
  35.0 0.6 collective-permute-start.11
  35.6 5.8 %collective-permute-done.9.recv = bf16[1,32,5120]{2,1,0:T(8,128)(2,1)S(1)} collective-permute-done((bf16[1,32,5120]{2,1,0:T(8,128)(2,1)S(1)}, bf16[1,32,5120]{2,1,0:T(8,128)(2,1)S(1)}, u32[]{:S(2)}, u32[]{:S(2)}) %collective-permute-start.9) | collective-permute-done | bytes 327712 | tf_op jit(solution)/shard_map/ppermute | solution.py:265
  41.5 1.3 %collective-permute-start.10 = (bf16[256,896]{1,0:T(8,128)(2,1)S(1)}, bf16[256,896]{1,0:T(8,128)(2,1)S(1)}, u32[]{:S(2)}, u32[]{:S(2)}) collective-permute-start(bf16[256,896]{1,0:T(8,128)(2,1)S(1)} %collective-permute-done.7.refs_8_), channel_id=1, source_target_pairs={{0,16},{16,0},{1,17},{17,1},{2,18},{18,2},{3,19},{19,3},{4,20},{20... | collective-permute-start | bytes 1376264 | tf_op jit(solution)/shard_map/ppermute | solution.py:265
  43.0 1.0 %collective-permute-start.12 = (bf16[16,5120]{1,0:T(8,128)(2,1)S(1)}, bf16[16,5120]{1,0:T(8,128)(2,1)S(1)}, u32[]{:S(2)}, u32[]{:S(2)}) collective-permute-start(bf16[16,5120]{1,0:T(8,128)(2,1)S(1)} %get-tuple-element.117), channel_id=1, source_target_pairs={{0,4},{4,0},{8,12},{12,8},{1,5},{5,1},{9,13},{13,9},{2,6},{6,2},{1... | collective-permute-start | bytes 491528 | tf_op jit(solution)/shard_map/ppermute | solution.py:265
  44.0 2.7 %matmul_1.1 = (f32[256,2048]{1,0:T(8,128)S(1)}, bf16[256,4096]{1,0:T(8,128)(2,1)}) custom-call(bf16[256,4096]{1,0:T(8,128)(2,1)S(1)} %get-tuple-element.90.tok.refs_0_, bf16[256,2048]{1,0:T(8,128)(2,1)S(1)} %get-tuple-element.91.cot.refs_1_, bf16[256,128]{1,0:T(8,128)(2,1)S(1)} %get-tuple-element.102.refs_2_, ...), custom_call_target="tpu_custom_call", output_to_operand_aliasing={{1}: (8, {}), {0}: (7, {})} | custom-call | flops 2147483648 | bytes 1 | tf_op jit(solution)/shard_map/matmul_1/pallas_call | solution.py:228
  46.7 1.7 %collective-permute-done.12 = bf16[16,5120]{1,0:T(8,128)(2,1)S(1)} collective-permute-done((bf16[16,5120]{1,0:T(8,128)(2,1)S(1)}, bf16[16,5120]{1,0:T(8,128)(2,1)S(1)}, u32[]{:S(2)}, u32[]{:S(2)}) %collective-permute-start.12) | collective-permute-done | bytes 163872 | tf_op jit(solution)/shard_map/ppermute | solution.py:265
  48.4 3.2 %collective-permute-start.16 = (bf16[16,5120]{1,0:T(8,128)(2,1)S(1)}, bf16[16,5120]{1,0:T(8,128)(2,1)S(1)}, u32[]{:S(2)}, u32[]{:S(2)}) collective-permute-start(bf16[16,5120]{1,0:T(8,128)(2,1)S(1)} %add_convert_fusion.1), channel_id=1, source_target_pairs={{0,8},{4,12},{8,0},{12,4},{1,9},{5,13},{9,1},{13,5},{2,10},{6,14},... | collective-permute-start | bytes 491528 | tf_op jit(solution)/shard_map/ppermute | solution.py:265
  51.7 1.5 %collective-permute-start.14 = (bf16[256,1152]{1,0:T(8,128)(2,1)S(1)}, bf16[256,1152]{1,0:T(8,128)(2,1)S(1)}, u32[]{:S(2)}, u32[]{:S(2)}) collective-permute-start(bf16[256,1152]{1,0:T(8,128)(2,1)S(1)} %get-tuple-element.129), channel_id=1, source_target_pairs={{0,2},{1,3},{2,0},{3,1},{4,6},{5,7},{6,4},{7,5},{8,10},{9,11},{10,... | collective-permute-start | bytes 1769480 | tf_op jit(solution)/shard_map/ppermute | solution.py:265
  53.2 0.7 collective-permute-done.11.refs_7_
  53.9 1.0 %collective-permute-start.19 = (bf16[256,1152]{1,0:T(8,128)(2,1)S(1)}, bf16[256,1152]{1,0:T(8,128)(2,1)S(1)}, u32[]{:S(2)}, u32[]{:S(2)}) collective-permute-start(bf16[256,1152]{1,0:T(8,128)(2,1)S(1)} %collective-permute-done.11.refs_7_), channel_id=1, source_target_pairs={{0,16},{16,0},{1,17},{17,1},{2,18},{18,2},{3,19},{19,3},{4,20},{20... | collective-permute-start | bytes 1769480 | tf_op jit(solution)/shard_map/ppermute | solution.py:265
  54.9 1.9 %collective-permute-done.16 = bf16[16,5120]{1,0:T(8,128)(2,1)S(1)} collective-permute-done((bf16[16,5120]{1,0:T(8,128)(2,1)S(1)}, bf16[16,5120]{1,0:T(8,128)(2,1)S(1)}, u32[]{:S(2)}, u32[]{:S(2)}) %collective-permute-start.16) | collective-permute-done | bytes 163872 | tf_op jit(solution)/shard_map/ppermute | solution.py:265
  56.9 2.1 %collective-permute-start.24 = (bf16[16,5120]{1,0:T(8,128)(2,1)S(1)}, bf16[16,5120]{1,0:T(8,128)(2,1)S(1)}, u32[]{:S(2)}, u32[]{:S(2)}) collective-permute-start(bf16[16,5120]{1,0:T(8,128)(2,1)S(1)} %add_convert_fusion.mine), channel_id=1, source_target_pairs={{0,4},{4,0},{8,12},{12,8},{1,5},{5,1},{9,13},{13,9},{2,6},{6,2},{1... | collective-permute-start | bytes 491528 | tf_op jit(solution)/shard_map/ppermute | solution.py:265
  58.9 1.7 %matmul_2.1 = (f32[256,2048]{1,0:T(8,128)S(1)}, bf16[256,4096]{1,0:T(8,128)(2,1)}) custom-call(bf16[256,4096]{1,0:T(8,128)(2,1)S(1)} %get-tuple-element.90.tok.refs_0_, bf16[256,2048]{1,0:T(8,128)(2,1)S(1)} %get-tuple-element.91.cot.refs_1_, bf16[256,128]{1,0:T(8,128)(2,1)S(1)} %get-tuple-element.102.refs_2_, ...), custom_call_target="tpu_custom_call", output_to_operand_aliasing={{1}: (11, {}), {0}: (10, {})} | custom-call | flops 1073741824 | bytes 1 | tf_op jit(solution)/shard_map/matmul_2/pallas_call | solution.py:228
  60.6 4.6 %collective-permute-done.14.refs_7_ = bf16[256,1152]{1,0:T(8,128)(2,1)S(1)} collective-permute-done((bf16[256,1152]{1,0:T(8,128)(2,1)S(1)}, bf16[256,1152]{1,0:T(8,128)(2,1)S(1)}, u32[]{:S(2)}, u32[]{:S(2)}) %collective-permute-start.14) | collective-permute-done | bytes 589856 | tf_op jit(solution)/shard_map/ppermute | solution.py:265
  65.2 1.7 %matmul_3.1 = (f32[256,2048]{1,0:T(8,128)S(1)}, bf16[256,4096]{1,0:T(8,128)(2,1)}) custom-call(bf16[256,4096]{1,0:T(8,128)(2,1)S(1)} %get-tuple-element.90.tok.refs_0_, bf16[256,2048]{1,0:T(8,128)(2,1)S(1)} %get-tuple-element.91.cot.refs_1_, bf16[256,128]{1,0:T(8,128)(2,1)S(1)} %get-tuple-element.102.refs_2_, ...), custom_call_target="tpu_custom_call", output_to_operand_aliasing={{1}: (9, {}), {0}: (8, {})} | custom-call | flops 536870912 | bytes 1 | tf_op jit(solution)/shard_map/matmul_3/pallas_call | solution.py:228
  66.9 2.7 %collective-permute-done.19.refs_7_ = bf16[256,1152]{1,0:T(8,128)(2,1)S(1)} collective-permute-done((bf16[256,1152]{1,0:T(8,128)(2,1)S(1)}, bf16[256,1152]{1,0:T(8,128)(2,1)S(1)}, u32[]{:S(2)}, u32[]{:S(2)}) %collective-permute-start.19) | collective-permute-done | bytes 589856 | tf_op jit(solution)/shard_map/ppermute | solution.py:265
  69.6 2.3 %collective-permute-done.20.refs_9_ = bf16[256,1152]{1,0:T(8,128)(2,1)S(1)} collective-permute-done((bf16[256,1152]{1,0:T(8,128)(2,1)S(1)}, bf16[256,1152]{1,0:T(8,128)(2,1)S(1)}, u32[]{:S(2)}, u32[]{:S(2)}) %collective-permute-start.20) | collective-permute-done | bytes 589856 | tf_op jit(solution)/shard_map/ppermute | solution.py:265
  72.9 0.7 collective-permute-done.24.recv
  73.6 1.7 %matmul_4.1 = (f32[256,2048]{1,0:T(8,128)S(1)}, bf16[256,4096]{1,0:T(8,128)(2,1)}) custom-call(bf16[256,4096]{1,0:T(8,128)(2,1)S(1)} %get-tuple-element.90.tok.refs_0_, bf16[256,2048]{1,0:T(8,128)(2,1)S(1)} %get-tuple-element.91.cot.refs_1_, bf16[256,128]{1,0:T(8,128)(2,1)S(1)} %get-tuple-element.102.refs_2_, ...), custom_call_target="tpu_custom_call", output_to_operand_aliasing={{1}: (11, {}), {0}: (10, {})} | custom-call | flops 1073741824 | bytes 1 | tf_op jit(solution)/shard_map/matmul_4/pallas_call | solution.py:228
  75.3 0.9 %finish.1 = (f32[1,32,4096]{2,1,0:T(8,128)}, f32[1,32,1024]{2,1,0:T(8,128)}) custom-call(bf16[16,5120]{1,0:T(8,128)(2,1)S(1)} %add_convert_fusion.mine, bf16[16,5120]{1,0:T(8,128)(2,1)S(1)} %collective-permute-done.24.recv), custom_call_target="tpu_custom_call" | custom-call | flops 1 | bytes 1 | tf_op jit(solution)/shard_map/finish/pallas_call | solution.py:305
  76.2 0.7 collective-permute-done.13.refs_6_
  76.9 3.5 %matmul_5.1 = (bf16[256,2048]{1,0:T(8,128)(2,1)}, bf16[256,4096]{1,0:T(8,128)(2,1)}) custom-call(bf16[256,4096]{1,0:T(8,128)(2,1)S(1)} %get-tuple-element.90.tok.refs_0_, bf16[256,2048]{1,0:T(8,128)(2,1)S(1)} %get-tuple-element.91.cot.refs_1_, bf16[256,128]{1,0:T(8,128)(2,1)S(1)} %get-tuple-element.102.refs_2_, ...), custom_call_target="tpu_custom_call", output_to_operand_aliasing={{1}: (13, {})} | custom-call | flops 1610612736 | bytes 1 | tf_op jit(solution)/shard_map/matmul_5/pallas_call | solution.py:228
  (47 shorter events, 4.3 us)
Async XLA Ops:
  0.6 5.4 %copy-start = (bf16[1024,2048]{1,0:T(8,128)(2,1)S(1)}, bf16[1024,2048]{1,0:T(8,128)(2,1)}, u32[]{:S(2)}) copy-start(bf16[1024,2048]{1,0:T(8,128)(2,1)} %weight.3) | copy-start | bytes 12582916
  0.6 14.0 %collective-permute-start.2 = (bf16[1024,2048]{1,0:T(8,128)(2,1)}, bf16[1024,2048]{1,0:T(8,128)(2,1)S(1)}, u32[]{:S(2)}, u32[]{:S(2)}) collective-permute-start(bf16[1024,2048]{1,0:T(8,128)(2,1)} %weight.3), channel_id=1, source_target_pairs={{0,1},{1,0},{2,3},{3,2},{4,5},{5,4},{6,7},{7,6},{8,9},{9,8},{10,11... | collective-permute-start | bytes 12582920 | tf_op jit(solution)/shard_map/ppermute | solution.py:265
  3.5 11.2 %collective-permute-start.1 = (bf16[32,5120]{1,0:T(8,128)(2,1)}, bf16[32,5120]{1,0:T(8,128)(2,1)S(1)}, u32[]{:S(2)}, u32[]{:S(2)}) collective-permute-start(bf16[32,5120]{1,0:T(8,128)(2,1)} %get-tuple-element.82.refs_0_), channel_id=1, source_target_pairs={{0,2},{1,3},{2,0},{3,1},{4,6},{5,7},{6,4},{7,5},{8,10},{9,11},{10,... | collective-permute-start | bytes 983048 | tf_op jit(solution)/shard_map/ppermute | solution.py:265
  5.9 1.6 %copy-start.1 = (bf16[256,4096]{1,0:T(8,128)(2,1)S(1)}, bf16[256,4096]{1,0:T(8,128)(2,1)}, u32[]{:S(2)}) copy-start(bf16[256,4096]{1,0:T(8,128)(2,1)} %refs_0_.1) | copy-start | bytes 6291460
  5.9 1.9 %copy-start.2 = (bf16[256,2048]{1,0:T(8,128)(2,1)S(1)}, bf16[256,2048]{1,0:T(8,128)(2,1)}, u32[]{:S(2)}) copy-start(bf16[256,2048]{1,0:T(8,128)(2,1)} %refs_1_.1) | copy-start | bytes 3145732
  5.9 18.6 %collective-permute-start = (bf16[256,896]{1,0:T(8,128)(2,1)}, bf16[256,896]{1,0:T(8,128)(2,1)S(1)}, u32[]{:S(2)}, u32[]{:S(2)}) collective-permute-start(bf16[256,896]{1,0:T(8,128)(2,1)} %get-tuple-element.81), channel_id=1, source_target_pairs={{0,2},{1,3},{2,0},{3,1},{4,6},{5,7},{6,4},{7,5},{8,10},{9,11},{10,... | collective-permute-start | bytes 1376264 | tf_op jit(solution)/shard_map/ppermute | solution.py:265
  7.8 7.1 %copy-start.3 = (bf16[32,5120]{1,0:T(8,128)(2,1)S(1)}, bf16[32,5120]{1,0:T(8,128)(2,1)}, u32[]{:S(2)}) copy-start(bf16[32,5120]{1,0:T(8,128)(2,1)} %get-tuple-element.82.refs_0_) | copy-start | bytes 983044
  7.8 7.4 %copy-start.4 = (s32[4]{0:T(128)S(1)}, s32[4]{0:T(128)}, u32[]{:S(2)}) copy-start(s32[4]{0:T(128)} %param.12) | copy-start | bytes 52
  7.8 7.4 %copy-start.5 = (s32[1,4]{1,0:T(1,128)S(1)}, s32[1,4]{1,0:T(1,128)}, u32[]{:S(2)}) copy-start(s32[1,4]{1,0:T(1,128)} %param.11) | copy-start | bytes 52
  14.7 9.8 %collective-permute-start.3 = (bf16[32,5120]{1,0:T(8,128)(2,1)S(1)}, bf16[32,5120]{1,0:T(8,128)(2,1)S(1)}, u32[]{:S(2)}, u32[]{:S(2)}) collective-permute-start(bf16[32,5120]{1,0:T(8,128)(2,1)S(1)} %collective-permute-done.1.refs_2_), channel_id=1, source_target_pairs={{0,1},{1,0},{2,3},{3,2},{4,5},{5,4},{6,7},{7,6},{8,9},{9,8},{10,11... | collective-permute-start | bytes 983048 | tf_op jit(solution)/shard_map/ppermute | solution.py:265
  14.8 9.7 %collective-permute-start.4 = (bf16[32,5120]{1,0:T(8,128)(2,1)S(1)}, bf16[32,5120]{1,0:T(8,128)(2,1)S(1)}, u32[]{:S(2)}, u32[]{:S(2)}) collective-permute-start(bf16[32,5120]{1,0:T(8,128)(2,1)S(1)} %copy-done.3), channel_id=1, source_target_pairs={{0,1},{1,0},{2,3},{3,2},{4,5},{5,4},{6,7},{7,6},{8,9},{9,8},{10,11... | collective-permute-start | bytes 983048 | tf_op jit(solution)/shard_map/ppermute | solution.py:265
  26.6 4.0 %collective-permute-start.5 = (bf16[2,32,5120]{2,1,0:T(8,128)(2,1)S(1)}, bf16[2,32,5120]{2,1,0:T(8,128)(2,1)S(1)}, u32[]{:S(2)}, u32[]{:S(2)}) collective-permute-start(bf16[2,32,5120]{2,1,0:T(8,128)(2,1)S(1)} %get-tuple-element.95), channel_id=1, source_target_pairs={{0,1},{1,0},{2,3},{3,2},{4,5},{5,4},{6,7},{7,6},{8,9},{9,8},{10,11... | collective-permute-start | bytes 1966088 | tf_op jit(solution)/shard_map/ppermute | solution.py:265
  26.8 3.8 %collective-permute-start.6 = (bf16[256,896]{1,0:T(8,128)(2,1)S(1)}, bf16[256,896]{1,0:T(8,128)(2,1)S(1)}, u32[]{:S(2)}, u32[]{:S(2)}) collective-permute-start(bf16[256,896]{1,0:T(8,128)(2,1)S(1)} %collective-permute-done.refs_6_), channel_id=1, source_target_pairs={{0,1},{1,0},{2,3},{3,2},{4,5},{5,4},{6,7},{7,6},{8,9},{9,8},{10,11... | collective-permute-start | bytes 1376264 | tf_op jit(solution)/shard_map/ppermute | solution.py:265
  27.2 14.3 %collective-permute-start.7 = (bf16[256,896]{1,0:T(8,128)(2,1)S(1)}, bf16[256,896]{1,0:T(8,128)(2,1)S(1)}, u32[]{:S(2)}, u32[]{:S(2)}) collective-permute-start(bf16[256,896]{1,0:T(8,128)(2,1)S(1)} %collective-permute-done.refs_6_), channel_id=1, source_target_pairs={{0,4},{4,0},{8,12},{12,8},{1,5},{5,1},{9,13},{13,9},{2,6},{6,2},{1... | collective-permute-start | bytes 1376264 | tf_op jit(solution)/shard_map/ppermute | solution.py:265
  29.0 12.5 %collective-permute-start.8 = (bf16[256,896]{1,0:T(8,128)(2,1)S(1)}, bf16[256,896]{1,0:T(8,128)(2,1)S(1)}, u32[]{:S(2)}, u32[]{:S(2)}) collective-permute-start(bf16[256,896]{1,0:T(8,128)(2,1)S(1)} %collective-permute-done.refs_6_), channel_id=1, source_target_pairs={{0,16},{16,0},{1,17},{17,1},{2,18},{18,2},{3,19},{19,3},{4,20},{20... | collective-permute-start | bytes 1376264 | tf_op jit(solution)/shard_map/ppermute | solution.py:265
  30.7 10.7 %collective-permute-start.9 = (bf16[1,32,5120]{2,1,0:T(8,128)(2,1)S(1)}, bf16[1,32,5120]{2,1,0:T(8,128)(2,1)S(1)}, u32[]{:S(2)}, u32[]{:S(2)}) collective-permute-start(bf16[1,32,5120]{2,1,0:T(8,128)(2,1)S(1)} %get-tuple-element.106), channel_id=1, source_target_pairs={{0,2},{1,3},{2,0},{3,1},{4,6},{5,7},{6,4},{7,5},{8,10},{9,11},{10,... | collective-permute-start | bytes 983048 | tf_op jit(solution)/shard_map/ppermute | solution.py:265
  35.0 18.8 %collective-permute-start.11 = (bf16[256,1152]{1,0:T(8,128)(2,1)S(1)}, bf16[256,1152]{1,0:T(8,128)(2,1)S(1)}, u32[]{:S(2)}, u32[]{:S(2)}) collective-permute-start(bf16[256,1152]{1,0:T(8,128)(2,1)S(1)} %get-tuple-element.110), channel_id=1, source_target_pairs={{0,2},{1,3},{2,0},{3,1},{4,6},{5,7},{6,4},{7,5},{8,10},{9,11},{10,... | collective-permute-start | bytes 1769480 | tf_op jit(solution)/shard_map/ppermute | solution.py:265
  41.5 12.3 %collective-permute-start.10 = (bf16[256,896]{1,0:T(8,128)(2,1)S(1)}, bf16[256,896]{1,0:T(8,128)(2,1)S(1)}, u32[]{:S(2)}, u32[]{:S(2)}) collective-permute-start(bf16[256,896]{1,0:T(8,128)(2,1)S(1)} %collective-permute-done.7.refs_8_), channel_id=1, source_target_pairs={{0,16},{16,0},{1,17},{17,1},{2,18},{18,2},{3,19},{19,3},{4,20},{20... | collective-permute-start | bytes 1376264 | tf_op jit(solution)/shard_map/ppermute | solution.py:265
  43.0 5.4 %collective-permute-start.12 = (bf16[16,5120]{1,0:T(8,128)(2,1)S(1)}, bf16[16,5120]{1,0:T(8,128)(2,1)S(1)}, u32[]{:S(2)}, u32[]{:S(2)}) collective-permute-start(bf16[16,5120]{1,0:T(8,128)(2,1)S(1)} %get-tuple-element.117), channel_id=1, source_target_pairs={{0,4},{4,0},{8,12},{12,8},{1,5},{5,1},{9,13},{13,9},{2,6},{6,2},{1... | collective-permute-start | bytes 491528 | tf_op jit(solution)/shard_map/ppermute | solution.py:265
  48.4 8.4 %collective-permute-start.16 = (bf16[16,5120]{1,0:T(8,128)(2,1)S(1)}, bf16[16,5120]{1,0:T(8,128)(2,1)S(1)}, u32[]{:S(2)}, u32[]{:S(2)}) collective-permute-start(bf16[16,5120]{1,0:T(8,128)(2,1)S(1)} %add_convert_fusion.1), channel_id=1, source_target_pairs={{0,8},{4,12},{8,0},{12,4},{1,9},{5,13},{9,1},{13,5},{2,10},{6,14},... | collective-permute-start | bytes 491528 | tf_op jit(solution)/shard_map/ppermute | solution.py:265
  51.7 13.5 %collective-permute-start.14 = (bf16[256,1152]{1,0:T(8,128)(2,1)S(1)}, bf16[256,1152]{1,0:T(8,128)(2,1)S(1)}, u32[]{:S(2)}, u32[]{:S(2)}) collective-permute-start(bf16[256,1152]{1,0:T(8,128)(2,1)S(1)} %get-tuple-element.129), channel_id=1, source_target_pairs={{0,2},{1,3},{2,0},{3,1},{4,6},{5,7},{6,4},{7,5},{8,10},{9,11},{10,... | collective-permute-start | bytes 1769480 | tf_op jit(solution)/shard_map/ppermute | solution.py:265
  53.1 19.2 %collective-permute-start.18 = (bf16[256,896]{1,0:T(8,128)(2,1)S(1)}, bf16[256,896]{1,0:T(8,128)(2,1)S(1)}, u32[]{:S(2)}, u32[]{:S(2)}) collective-permute-start(bf16[256,896]{1,0:T(8,128)(2,1)S(1)} %collective-permute-done.8.refs_6_), channel_id=1, source_target_pairs={{0,1},{1,0},{2,3},{3,2},{4,5},{5,4},{6,7},{7,6},{8,9},{9,8},{10,11... | collective-permute-start | bytes 1376264 | tf_op jit(solution)/shard_map/ppermute | solution.py:265
  53.9 3.0 %collective-permute-start.15 = (bf16[256,1152]{1,0:T(8,128)(2,1)S(1)}, bf16[256,1152]{1,0:T(8,128)(2,1)S(1)}, u32[]{:S(2)}, u32[]{:S(2)}) collective-permute-start(bf16[256,1152]{1,0:T(8,128)(2,1)S(1)} %collective-permute-done.11.refs_7_), channel_id=1, source_target_pairs={{0,1},{1,0},{2,3},{3,2},{4,5},{5,4},{6,7},{7,6},{8,9},{9,8},{10,11... | collective-permute-start | bytes 1769480 | tf_op jit(solution)/shard_map/ppermute | solution.py:265
  53.9 15.7 %collective-permute-start.19 = (bf16[256,1152]{1,0:T(8,128)(2,1)S(1)}, bf16[256,1152]{1,0:T(8,128)(2,1)S(1)}, u32[]{:S(2)}, u32[]{:S(2)}) collective-permute-start(bf16[256,1152]{1,0:T(8,128)(2,1)S(1)} %collective-permute-done.11.refs_7_), channel_id=1, source_target_pairs={{0,16},{16,0},{1,17},{17,1},{2,18},{18,2},{3,19},{19,3},{4,20},{20... | collective-permute-start | bytes 1769480 | tf_op jit(solution)/shard_map/ppermute | solution.py:265
  56.8 15.1 %collective-permute-start.20 = (bf16[256,1152]{1,0:T(8,128)(2,1)S(1)}, bf16[256,1152]{1,0:T(8,128)(2,1)S(1)}, u32[]{:S(2)}, u32[]{:S(2)}) collective-permute-start(bf16[256,1152]{1,0:T(8,128)(2,1)S(1)} %collective-permute-done.11.refs_7_), channel_id=1, source_target_pairs={{0,4},{4,0},{8,12},{12,8},{1,5},{5,1},{9,13},{13,9},{2,6},{6,2},{1... | collective-permute-start | bytes 1769480 | tf_op jit(solution)/shard_map/ppermute | solution.py:265
  56.9 16.8 %collective-permute-start.24 = (bf16[16,5120]{1,0:T(8,128)(2,1)S(1)}, bf16[16,5120]{1,0:T(8,128)(2,1)S(1)}, u32[]{:S(2)}, u32[]{:S(2)}) collective-permute-start(bf16[16,5120]{1,0:T(8,128)(2,1)S(1)} %add_convert_fusion.mine), channel_id=1, source_target_pairs={{0,4},{4,0},{8,12},{12,8},{1,5},{5,1},{9,13},{13,9},{2,6},{6,2},{1... | collective-permute-start | bytes 491528 | tf_op jit(solution)/shard_map/ppermute | solution.py:265
  71.9 5.0 %collective-permute-start.21 = (bf16[256,1152]{1,0:T(8,128)(2,1)S(1)}, bf16[256,1152]{1,0:T(8,128)(2,1)S(1)}, u32[]{:S(2)}, u32[]{:S(2)}) collective-permute-start(bf16[256,1152]{1,0:T(8,128)(2,1)S(1)} %collective-permute-done.19.refs_7_), channel_id=1, source_target_pairs={{0,1},{1,0},{2,3},{3,2},{4,5},{5,4},{6,7},{7,6},{8,9},{9,8},{10,11... | collective-permute-start | bytes 1769480 | tf_op jit(solution)/shard_map/ppermute | solution.py:265
  71.9 5.0 %collective-permute-start.23 = (bf16[256,1152]{1,0:T(8,128)(2,1)S(1)}, bf16[256,1152]{1,0:T(8,128)(2,1)S(1)}, u32[]{:S(2)}, u32[]{:S(2)}) collective-permute-start(bf16[256,1152]{1,0:T(8,128)(2,1)S(1)} %collective-permute-done.20.refs_9_), channel_id=1, source_target_pairs={{0,1},{1,0},{2,3},{3,2},{4,5},{5,4},{6,7},{7,6},{8,9},{9,8},{10,11... | collective-permute-start | bytes 1769480 | tf_op jit(solution)/shard_map/ppermute | solution.py:265
  72.4 4.5 %collective-permute-start.17 = (bf16[256,1152]{1,0:T(8,128)(2,1)S(1)}, bf16[256,1152]{1,0:T(8,128)(2,1)S(1)}, u32[]{:S(2)}, u32[]{:S(2)}) collective-permute-start(bf16[256,1152]{1,0:T(8,128)(2,1)S(1)} %collective-permute-done.14.refs_7_), channel_id=1, source_target_pairs={{0,1},{1,0},{2,3},{3,2},{4,5},{5,4},{6,7},{7,6},{8,9},{9,8},{10,11... | collective-permute-start | bytes 1769480 | tf_op jit(solution)/shard_map/ppermute | solution.py:265
  72.4 3.8 %collective-permute-start.22 = (bf16[256,896]{1,0:T(8,128)(2,1)S(1)}, bf16[256,896]{1,0:T(8,128)(2,1)S(1)}, u32[]{:S(2)}, u32[]{:S(2)}) collective-permute-start(bf16[256,896]{1,0:T(8,128)(2,1)S(1)} %collective-permute-done.7.refs_8_), channel_id=1, source_target_pairs={{0,1},{1,0},{2,3},{3,2},{4,5},{5,4},{6,7},{7,6},{8,9},{9,8},{10,11... | collective-permute-start | bytes 1376264 | tf_op jit(solution)/shard_map/ppermute | solution.py:265
  73.6 3.2 %collective-permute-start.13 = (bf16[256,896]{1,0:T(8,128)(2,1)S(1)}, bf16[256,896]{1,0:T(8,128)(2,1)S(1)}, u32[]{:S(2)}, u32[]{:S(2)}) collective-permute-start(bf16[256,896]{1,0:T(8,128)(2,1)S(1)} %collective-permute-done.10.refs_6_), channel_id=1, source_target_pairs={{0,1},{1,0},{2,3},{3,2},{4,5},{5,4},{6,7},{7,6},{8,9},{9,8},{10,11... | collective-permute-start | bytes 1376264 | tf_op jit(solution)/shard_map/ppermute | solution.py:265

commit v4 on v3

--- a/solution.py
+++ b/solution.py
@@ -155,7 +155,9 @@
 def matmul_kernel(plan, block, shard, rank2, kv, first, last, *refs):
     refs = list(refs)
     tok, cot, low, grad, down, up = (refs.pop(0) for _ in range(6))
-    sources = [[refs.pop(0) for _ in range(count)] for count, _, _ in plan]
+    sources = [
+        [refs.pop(0) if i is None else refs.pop(0).at[i] for i in picks] for picks, _, _ in plan
+    ]
     if not first:
         acc_in = refs.pop(0)
         refs.pop(0)
@@ -208,12 +210,20 @@
     rows, width = tok.shape
     cols = cot.shape[1]
     kv = up.shape[1]
-    block = min(512, min(parts[0].shape[0] for _, parts in sources))
-    plan = tuple((len(parts), entry, parts[0].shape[0]) for entry, parts in sources)
+    sources = [
+        (entry, [p if isinstance(p, tuple) else (p, None) for p in parts])
+        for entry, parts in sources
+    ]
+    tall = [parts[0][0].shape[-2] for _, parts in sources]
+    block = min(512, min(tall))
+    plan = tuple(
+        (tuple(i for _, i in parts), entry, total)
+        for (entry, parts), total in zip(sources, tall)
+    )
     flops = 4 * rows * cols * sum(total for _, _, total in plan)
     cost = pl.CostEstimate(flops=flops, bytes_accessed=1, transcendentals=0)
     count = sum(total // block for _, _, total in plan)
-    arrays = [part for _, parts in sources for part in parts]
+    arrays = [part for _, parts in sources for part, _ in parts]
     args = [tok, cot, low, grad, down, up] + arrays
     in_specs = [VMEM] * (6 + len(arrays))
     first = prev is None
@@ -238,6 +248,11 @@
     )(*args)
 
 
+def stack_kernel(*refs):
+    for i, ref in enumerate(refs[:-1]):
+        refs[-1][i] = ref[...]
+
+
 def even_odd_kernel(keep, recv, even, odd):
     for i in range(even.shape[0]):
         for out, j in ((even, 2 * i), (odd, 2 * i + 1)):
@@ -267,11 +282,6 @@
 
 PREP_MIB = 54
 SPANS = (7, 9)
-DIAGONAL_AT = 1
-CORE_AT = 1
-CORE_GATE = False
-DIAGONAL_MM = True
-LATE_FINISH = True
 
 
 def per_device(
@@ -473,7 +483,7 @@
         direct[i] = after(direct[i])
         via_y.append(swap_y(direct[i]))
         via_z.append(swap_z(direct[i]))
-        if i == 1 and DIAGONAL_AT == 1:
+        if i == 1:
             diagonal[0] = after(diagonal[0])
     while bit < n_dp:
         if bit > 2:
@@ -482,48 +492,26 @@
         mine = after(add(mine, recv))
         bit *= 2
     other = swap_z(mine)
-    if DIAGONAL_AT == 2:
-        diagonal[0] = after(diagonal[0])
-
-    if CORE_AT == 1:
-        ahead[1:] = ready(ahead[:1] + core(direct[1:]))[1:]
-    sources = [((2, (0, 0)), direct)]
-    if CORE_AT == 1:
-        sources.append(((3, (0, 0)), ahead))
-    prev = matmul(2, sources, prev)
+
+    ahead[1:] = ready(ahead[:1] + core(direct[1:]))[1:]
+    early = (via_y[0], via_z[0], diagonal[0])
+    (stacked,) = local(stack_kernel, (struct((3,) + early[0].shape),), early, "stack")
+    stacked = after(stacked)
+    crossed = swap(stacked, 1)
+    prev = matmul(2, [((2, (0, 0)), direct), ((3, (0, 0)), ahead)], prev)
     prev = after(*prev)
-    if not LATE_FINISH:
-        mine, other = after(mine, other)
-        grad_down, grad_up = after(*finish(mine, other))
-    if DIAGONAL_AT == 3:
-        diagonal[0] = after(diagonal[0])
     diagonal.append(after(across))
-    if DIAGONAL_MM:
-        prev = matmul(3, [((2, (1, 1)), diagonal)], prev)
-        prev = after(*prev)
-    for i in range(1, len(direct)):
-        via_y[i], via_z[i] = after(via_y[i], via_z[i])
-    groups = [diagonal, via_y, via_z]
-    if CORE_AT != 1:
-        groups.append(direct)
-    if CORE_GATE:
-        flat = iter(after(*[p for group in groups for p in group]))
-        groups = [[next(flat) for _ in group] for group in groups]
-    crossed = [core(p) for p in groups[:3]]
-    if CORE_AT != 1:
-        crossed.append(ahead + core(groups[3][1:]))
-    sources = [((2, (1, 0)), via_y), ((2, (0, 1)), via_z)]
-    if not DIAGONAL_MM:
-        sources.append(((2, (1, 1)), diagonal))
-    prev = matmul(4, sources, prev)
-    if LATE_FINISH:
-        prev = after(*prev)
-        mine, other = after(mine, other)
-        grad_down, grad_up = after(*finish(mine, other))
-    keys = ((1, 1), (1, 0), (0, 1), (0, 0))
-    sources = [((3, key), p) for key, p in zip(keys, crossed)]
-    prev = matmul(5, sources, prev, True)
-    return prev[0], prev[1], grad_down, grad_up
+    prev = matmul(3, [((2, (1, 1)), diagonal)], prev)
+    prev = after(*prev)
+    via_y[1], via_z[1] = after(via_y[1], via_z[1])
+    late = core((via_y[1], via_z[1], diagonal[1]))
+    prev = matmul(4, [((2, (1, 0)), via_y), ((2, (0, 1)), via_z)], prev)
+    keys = ((1, 0), (0, 1), (1, 1))
+    sources = [((3, key), [(crossed, i), late[i]]) for i, key in enumerate(keys)]
+    out, grad_x = matmul(5, sources, prev, True)
+    out, mine, other = barrier(out, mine, other)
+    grad_down, grad_up = finish(mine, other)
+    return out, grad_x, grad_down, grad_up
 
 
 def solution(mesh):

time: 80.5 us -> 78.4 us (0.974)
  waiting for transfers between devices: 36.7 us -> 34.2 us
    ppermute x25 -> x23, waiting for transfers between devices: 36.7 us -> 34.2 us  [xor_swap(): return lax.ppermute(value, axis, [(i, i ^ bit) for i in range(size)])]
    ppermute x25 -> x23, starting transfers between devices: 20.8 us -> 21.2 us  [xor_swap(): return lax.ppermute(value, axis, [(i, i ^ bit) for i in range(size)])]
    pallas_call x6 -> x7, Pallas kernels: 4.05 us -> 4.16 us  [local(): pl.pallas_call(kernel, out_shape=tuple(outs), in_specs=spaces, out_specs=...]
  transfers between devices with their start and end apart: 25 -> 23, of which waited for: 11 -> 9; matrix products, arithmetic and copies ran while one was open for 0% -> 0% of each run, Pallas kernels for 18% -> 22%
where the time goes in v4:
time: 78.4 us; the launch traced here: 78.3 us
  waiting for transfers between devices  34.2 us (44%)
  starting transfers between devices  21.2 us (27%)
  Pallas kernels  20.1 us (26%)
  local copies, waits for them, and re-layouts  1.76 us (2%)
  between operations  0.84 us (1%)
    ppermute x23, waiting for transfers between devices, xor_swap(): return lax.ppermute(value, axis, [(i, i ^ bit) for i in range(size)])  34.2 us
    ppermute x23, starting transfers between devices, xor_swap(): return lax.ppermute(value, axis, [(i, i ^ bit) for i in range(size)])  21.2 us
    pallas_call x6, Pallas kernels, matmul_call(): pl.pallas_call(functools.partial(matmul_kernel, plan, block, shard, rank2...  13.9 us
    pallas_call x7, Pallas kernels, local(): pl.pallas_call(kernel, out_shape=tuple(outs), in_specs=spaces, out_specs=...  4.16 us
    pallas_call x1, Pallas kernels, low_rank_call(): pl.pallas_call(functools.partial(low_rank_kernel, slots, rank2, width, kv...  2.09 us
    unnamed x13, local copies, waits for them, and re-layouts  1.76 us
  transfers between devices with their start and end apart: 23, of which 9 were waited for; matrix products, arithmetic and copies ran while one was open for 0% of the time, Pallas kernels for 22%

profile of v4, /device:TPU:0, one launch (start us, length us, event | category | flops | bytes accessed | tf_op | source)
XLA Modules:
  0.0 78.3 jit_solution(9904682264956412643)
XLA Ops:
  0.6 0.5 collective-permute-start.2
  1.2 2.3 %prep.1 = (bf16[32,5120]{1,0:T(8,128)(2,1)}, bf16[256,896]{1,0:T(8,128)(2,1)}) custom-call(bf16[1024,2048]{1,0:T(8,128)(2,1)} %weight.3, bf16[1,32,4096]{2,1,0:T(8,128)(2,1)} %down.1, bf16[1,32,1024]{2,1,0:T(8,128)(2,1)} %up.1), custom_call_target="tpu_custom_call" | custom-call | flops 1 | bytes 1 | tf_op jit(solution)/shard_map/prep/pallas_call | solution.py:315
  3.5 2.5 %collective-permute-start.1 = (bf16[32,5120]{1,0:T(8,128)(2,1)}, bf16[32,5120]{1,0:T(8,128)(2,1)S(1)}, u32[]{:S(2)}, u32[]{:S(2)}) collective-permute-start(bf16[32,5120]{1,0:T(8,128)(2,1)} %get-tuple-element.81.refs_0_), channel_id=1, source_target_pairs={{0,2},{1,3},{2,0},{3,1},{4,6},{5,7},{6,4},{7,5},{8,10},{9,11},{10,... | collective-permute-start | bytes 983048 | tf_op jit(solution)/shard_map/ppermute | solution.py:280
  6.2 1.3 %copy-done.1 = bf16[256,4096]{1,0:T(8,128)(2,1)S(1)} copy-done((bf16[256,4096]{1,0:T(8,128)(2,1)S(1)}, bf16[256,4096]{1,0:T(8,128)(2,1)}, u32[]{:S(2)}) %copy-start.1) | copy-done | bytes 2097176
  7.8 0.5 load.1
  8.3 6.4 %collective-permute-done.1.refs_2_ = bf16[32,5120]{1,0:T(8,128)(2,1)S(1)} collective-permute-done((bf16[32,5120]{1,0:T(8,128)(2,1)}, bf16[32,5120]{1,0:T(8,128)(2,1)S(1)}, u32[]{:S(2)}, u32[]{:S(2)}) %collective-permute-start.1) | collective-permute-done | bytes 327712 | tf_op jit(solution)/shard_map/ppermute | solution.py:280
  15.3 9.2 %collective-permute-done.refs_6_ = bf16[256,896]{1,0:T(8,128)(2,1)S(1)} collective-permute-done((bf16[256,896]{1,0:T(8,128)(2,1)}, bf16[256,896]{1,0:T(8,128)(2,1)S(1)}, u32[]{:S(2)}, u32[]{:S(2)}) %collective-permute-start) | collective-permute-done | bytes 458784 | tf_op jit(solution)/shard_map/ppermute | solution.py:280
  24.5 2.1 %low_rank.1 = (bf16[256,128]{1,0:T(8,128)(2,1)S(1)}, bf16[256,128]{1,0:T(8,128)(2,1)S(1)}, bf16[128,4096]{1,0:T(8,128)(2,1)S(1)}, bf16[128,1024]{1,0:T(8,128)(2,...) custom-call(s32[8]{0:T(128)S(1)} %pad_add_fusion.place, ...), custom_call_target="tpu_custom_call" | custom-call | flops 1 | bytes 1 | tf_op jit(solution)/shard_map/low_rank/pallas_call | solution.py:137
  27.2 1.9 %collective-permute-start.7 = (bf16[256,896]{1,0:T(8,128)(2,1)S(1)}, bf16[256,896]{1,0:T(8,128)(2,1)S(1)}, u32[]{:S(2)}, u32[]{:S(2)}) collective-permute-start(bf16[256,896]{1,0:T(8,128)(2,1)S(1)} %collective-permute-done.refs_6_), channel_id=1, source_target_pairs={{0,4},{4,0},{8,12},{12,8},{1,5},{5,1},{9,13},{13,9},{2,6},{6,2},{1... | collective-permute-start | bytes 1376264 | tf_op jit(solution)/shard_map/ppermute | solution.py:280
  29.0 1.5 %collective-permute-start.8 = (bf16[256,896]{1,0:T(8,128)(2,1)S(1)}, bf16[256,896]{1,0:T(8,128)(2,1)S(1)}, u32[]{:S(2)}, u32[]{:S(2)}) collective-permute-start(bf16[256,896]{1,0:T(8,128)(2,1)S(1)} %collective-permute-done.refs_6_), channel_id=1, source_target_pairs={{0,16},{16,0},{1,17},{17,1},{2,18},{18,2},{3,19},{19,3},{4,20},{20... | collective-permute-start | bytes 1376264 | tf_op jit(solution)/shard_map/ppermute | solution.py:280
  30.7 1.6 %collective-permute-start.9 = (bf16[1,32,5120]{2,1,0:T(8,128)(2,1)S(1)}, bf16[1,32,5120]{2,1,0:T(8,128)(2,1)S(1)}, u32[]{:S(2)}, u32[]{:S(2)}) collective-permute-start(bf16[1,32,5120]{2,1,0:T(8,128)(2,1)S(1)} %get-tuple-element.105), channel_id=1, source_target_pairs={{0,2},{1,3},{2,0},{3,1},{4,6},{5,7},{6,4},{7,5},{8,10},{9,11},{10,... | collective-permute-start | bytes 983048 | tf_op jit(solution)/shard_map/ppermute | solution.py:280
  32.3 2.8 %matmul_0.1 = (f32[256,2048]{1,0:T(8,128)S(1)}, bf16[256,4096]{1,0:T(8,128)(2,1)}) custom-call(bf16[256,4096]{1,0:T(8,128)(2,1)S(1)} %get-tuple-element.89.tok.refs_0_, bf16[256,2048]{1,0:T(8,128)(2,1)S(1)} %get-tuple-element.90.cot.refs_1_, bf16[256,128]{1,0:T(8,128)(2,1)S(1)} %get-tuple-element.101.refs_2_, ...), custom_call_target="tpu_custom_call" | custom-call | flops 2147483648 | bytes 1 | tf_op jit(solution)/shard_map/matmul_0/pallas_call | solution.py:238
  35.0 0.6 collective-permute-start.11
  35.6 5.8 %collective-permute-done.9.recv = bf16[1,32,5120]{2,1,0:T(8,128)(2,1)S(1)} collective-permute-done((bf16[1,32,5120]{2,1,0:T(8,128)(2,1)S(1)}, bf16[1,32,5120]{2,1,0:T(8,128)(2,1)S(1)}, u32[]{:S(2)}, u32[]{:S(2)}) %collective-permute-start.9) | collective-permute-done | bytes 327712 | tf_op jit(solution)/shard_map/ppermute | solution.py:280
  41.5 1.3 %collective-permute-start.10 = (bf16[256,896]{1,0:T(8,128)(2,1)S(1)}, bf16[256,896]{1,0:T(8,128)(2,1)S(1)}, u32[]{:S(2)}, u32[]{:S(2)}) collective-permute-start(bf16[256,896]{1,0:T(8,128)(2,1)S(1)} %collective-permute-done.7.refs_1_.refs_8_), channel_id=1, source_target_pairs={{0,16},{16,0},{1,17},{17,1},{2,18},{18,2},{3,19},{19,3},{4,20},{20... | collective-permute-start | bytes 1376264 | tf_op jit(solution)/shard_map/ppermute | solution.py:280
  42.9 1.0 %collective-permute-start.12 = (bf16[16,5120]{1,0:T(8,128)(2,1)S(1)}, bf16[16,5120]{1,0:T(8,128)(2,1)S(1)}, u32[]{:S(2)}, u32[]{:S(2)}) collective-permute-start(bf16[16,5120]{1,0:T(8,128)(2,1)S(1)} %get-tuple-element.117), channel_id=1, source_target_pairs={{0,4},{4,0},{8,12},{12,8},{1,5},{5,1},{9,13},{13,9},{2,6},{6,2},{1... | collective-permute-start | bytes 491528 | tf_op jit(solution)/shard_map/ppermute | solution.py:280
  44.0 2.7 %matmul_1.1 = (f32[256,2048]{1,0:T(8,128)S(1)}, bf16[256,4096]{1,0:T(8,128)(2,1)}) custom-call(bf16[256,4096]{1,0:T(8,128)(2,1)S(1)} %get-tuple-element.89.tok.refs_0_, bf16[256,2048]{1,0:T(8,128)(2,1)S(1)} %get-tuple-element.90.cot.refs_1_, bf16[256,128]{1,0:T(8,128)(2,1)S(1)} %get-tuple-element.101.refs_2_, ...), custom_call_target="tpu_custom_call", output_to_operand_aliasing={{1}: (8, {}), {0}: (7, {})} | custom-call | flops 2147483648 | bytes 1 | tf_op jit(solution)/shard_map/matmul_1/pallas_call | solution.py:238
  46.6 1.7 %collective-permute-done.12 = bf16[16,5120]{1,0:T(8,128)(2,1)S(1)} collective-permute-done((bf16[16,5120]{1,0:T(8,128)(2,1)S(1)}, bf16[16,5120]{1,0:T(8,128)(2,1)S(1)}, u32[]{:S(2)}, u32[]{:S(2)}) %collective-permute-start.12) | collective-permute-done | bytes 163872 | tf_op jit(solution)/shard_map/ppermute | solution.py:280
  48.4 3.2 %collective-permute-start.18 = (bf16[16,5120]{1,0:T(8,128)(2,1)S(1)}, bf16[16,5120]{1,0:T(8,128)(2,1)S(1)}, u32[]{:S(2)}, u32[]{:S(2)}) collective-permute-start(bf16[16,5120]{1,0:T(8,128)(2,1)S(1)} %add_convert_fusion.1), channel_id=1, source_target_pairs={{0,8},{4,12},{8,0},{12,4},{1,9},{5,13},{9,1},{13,5},{2,10},{6,14},... | collective-permute-start | bytes 491528 | tf_op jit(solution)/shard_map/ppermute | solution.py:280
  51.6 1.5 %collective-permute-start.16 = (bf16[256,1152]{1,0:T(8,128)(2,1)S(1)}, bf16[256,1152]{1,0:T(8,128)(2,1)S(1)}, u32[]{:S(2)}, u32[]{:S(2)}) collective-permute-start(bf16[256,1152]{1,0:T(8,128)(2,1)S(1)} %get-tuple-element.129), channel_id=1, source_target_pairs={{0,2},{1,3},{2,0},{3,1},{4,6},{5,7},{6,4},{7,5},{8,10},{9,11},{10,... | collective-permute-start | bytes 1769480 | tf_op jit(solution)/shard_map/ppermute | solution.py:280
  53.1 0.9 %collective-permute-done.11.refs_7_ = bf16[256,1152]{1,0:T(8,128)(2,1)S(1)} collective-permute-done((bf16[256,1152]{1,0:T(8,128)(2,1)S(1)}, bf16[256,1152]{1,0:T(8,128)(2,1)S(1)}, u32[]{:S(2)}, u32[]{:S(2)}) %collective-permute-start.11) | collective-permute-done | bytes 589856 | tf_op jit(solution)/shard_map/ppermute | solution.py:280
  53.9 0.7 collective-permute-start.14
  54.7 1.6 %collective-permute-start.15 = (bf16[256,1152]{1,0:T(8,128)(2,1)S(1)}, bf16[256,1152]{1,0:T(8,128)(2,1)S(1)}, u32[]{:S(2)}, u32[]{:S(2)}) collective-permute-start(bf16[256,1152]{1,0:T(8,128)(2,1)S(1)} %collective-permute-done.11.refs_7_), channel_id=1, source_target_pairs={{0,4},{4,0},{8,12},{12,8},{1,5},{5,1},{9,13},{13,9},{2,6},{6,2},{1... | collective-permute-start | bytes 1769480 | tf_op jit(solution)/shard_map/ppermute | solution.py:280
  57.0 1.7 %matmul_2.1 = (f32[256,2048]{1,0:T(8,128)S(1)}, bf16[256,4096]{1,0:T(8,128)(2,1)}) custom-call(bf16[256,4096]{1,0:T(8,128)(2,1)S(1)} %get-tuple-element.89.tok.refs_0_, bf16[256,2048]{1,0:T(8,128)(2,1)S(1)} %get-tuple-element.90.cot.refs_1_, bf16[256,128]{1,0:T(8,128)(2,1)S(1)} %get-tuple-element.101.refs_2_, ...), custom_call_target="tpu_custom_call", output_to_operand_aliasing={{1}: (11, {}), {0}: (10, {})} | custom-call | flops 1073741824 | bytes 1 | tf_op jit(solution)/shard_map/matmul_2/pallas_call | solution.py:238
  58.7 6.5 %collective-permute-done.16.refs_7_ = bf16[256,1152]{1,0:T(8,128)(2,1)S(1)} collective-permute-done((bf16[256,1152]{1,0:T(8,128)(2,1)S(1)}, bf16[256,1152]{1,0:T(8,128)(2,1)S(1)}, u32[]{:S(2)}, u32[]{:S(2)}) %collective-permute-start.16) | collective-permute-done | bytes 589856 | tf_op jit(solution)/shard_map/ppermute | solution.py:280
  65.2 1.7 %matmul_3.1 = (f32[256,2048]{1,0:T(8,128)S(1)}, bf16[256,4096]{1,0:T(8,128)(2,1)}) custom-call(bf16[256,4096]{1,0:T(8,128)(2,1)S(1)} %get-tuple-element.89.tok.refs_0_, bf16[256,2048]{1,0:T(8,128)(2,1)S(1)} %get-tuple-element.90.cot.refs_1_, bf16[256,128]{1,0:T(8,128)(2,1)S(1)} %get-tuple-element.101.refs_2_, ...), custom_call_target="tpu_custom_call", output_to_operand_aliasing={{1}: (9, {}), {0}: (8, {})} | custom-call | flops 536870912 | bytes 1 | tf_op jit(solution)/shard_map/matmul_3/pallas_call | solution.py:238
  66.9 2.8 %collective-permute-done.14.refs_7_ = bf16[256,1152]{1,0:T(8,128)(2,1)S(1)} collective-permute-done((bf16[256,1152]{1,0:T(8,128)(2,1)S(1)}, bf16[256,1152]{1,0:T(8,128)(2,1)S(1)}, u32[]{:S(2)}, u32[]{:S(2)}) %collective-permute-start.14) | collective-permute-done | bytes 589856 | tf_op jit(solution)/shard_map/ppermute | solution.py:280
  70.1 0.5 collective-permute-start.20
  70.6 1.6 %collective-permute-start.22 = (bf16[16,5120]{1,0:T(8,128)(2,1)S(1)}, bf16[16,5120]{1,0:T(8,128)(2,1)S(1)}, u32[]{:S(2)}, u32[]{:S(2)}) collective-permute-start(bf16[16,5120]{1,0:T(8,128)(2,1)S(1)} %add_convert_fusion.mine), channel_id=1, source_target_pairs={{0,4},{4,0},{8,12},{12,8},{1,5},{5,1},{9,13},{13,9},{2,6},{6,2},{1... | collective-permute-start | bytes 491528 | tf_op jit(solution)/shard_map/ppermute | solution.py:280
  72.2 1.7 %matmul_4.1 = (f32[256,2048]{1,0:T(8,128)S(1)}, bf16[256,4096]{1,0:T(8,128)(2,1)}) custom-call(bf16[256,4096]{1,0:T(8,128)(2,1)S(1)} %get-tuple-element.89.tok.refs_0_, bf16[256,2048]{1,0:T(8,128)(2,1)S(1)} %get-tuple-element.90.cot.refs_1_, bf16[256,128]{1,0:T(8,128)(2,1)S(1)} %get-tuple-element.101.refs_2_, ...), custom_call_target="tpu_custom_call", output_to_operand_aliasing={{1}: (11, {}), {0}: (10, {})} | custom-call | flops 1073741824 | bytes 1 | tf_op jit(solution)/shard_map/matmul_4/pallas_call | solution.py:238
  73.9 3.4 %matmul_5.1 = (bf16[256,2048]{1,0:T(8,128)(2,1)}, bf16[256,4096]{1,0:T(8,128)(2,1)}) custom-call(bf16[256,4096]{1,0:T(8,128)(2,1)S(1)} %get-tuple-element.89.tok.refs_0_, bf16[256,2048]{1,0:T(8,128)(2,1)S(1)} %get-tuple-element.90.cot.refs_1_, bf16[256,128]{1,0:T(8,128)(2,1)S(1)} %get-tuple-element.101.refs_2_, ...), custom_call_target="tpu_custom_call", output_to_operand_aliasing={{1}: (13, {})} | custom-call | flops 1610612736 | bytes 1 | tf_op jit(solution)/shard_map/matmul_5/pallas_call | solution.py:238
  77.4 0.9 %finish.1 = (f32[1,32,4096]{2,1,0:T(8,128)}, f32[1,32,1024]{2,1,0:T(8,128)}) custom-call(bf16[16,5120]{1,0:T(8,128)(2,1)S(1)} %add_convert_fusion.mine, bf16[16,5120]{1,0:T(8,128)(2,1)S(1)} %collective-permute-done.22.recv), custom_call_target="tpu_custom_call" | custom-call | flops 1 | bytes 1 | tf_op jit(solution)/shard_map/finish/pallas_call | solution.py:315
  (44 shorter events, 3.3 us)
Async XLA Ops:
  0.6 5.4 %copy-start = (bf16[1024,2048]{1,0:T(8,128)(2,1)S(1)}, bf16[1024,2048]{1,0:T(8,128)(2,1)}, u32[]{:S(2)}) copy-start(bf16[1024,2048]{1,0:T(8,128)(2,1)} %weight.3) | copy-start | bytes 12582916
  0.6 14.0 %collective-permute-start.2 = (bf16[1024,2048]{1,0:T(8,128)(2,1)}, bf16[1024,2048]{1,0:T(8,128)(2,1)S(1)}, u32[]{:S(2)}, u32[]{:S(2)}) collective-permute-start(bf16[1024,2048]{1,0:T(8,128)(2,1)} %weight.3), channel_id=1, source_target_pairs={{0,1},{1,0},{2,3},{3,2},{4,5},{5,4},{6,7},{7,6},{8,9},{9,8},{10,11... | collective-permute-start | bytes 12582920 | tf_op jit(solution)/shard_map/ppermute | solution.py:280
  3.5 11.2 %collective-permute-start.1 = (bf16[32,5120]{1,0:T(8,128)(2,1)}, bf16[32,5120]{1,0:T(8,128)(2,1)S(1)}, u32[]{:S(2)}, u32[]{:S(2)}) collective-permute-start(bf16[32,5120]{1,0:T(8,128)(2,1)} %get-tuple-element.81.refs_0_), channel_id=1, source_target_pairs={{0,2},{1,3},{2,0},{3,1},{4,6},{5,7},{6,4},{7,5},{8,10},{9,11},{10,... | collective-permute-start | bytes 983048 | tf_op jit(solution)/shard_map/ppermute | solution.py:280
  5.9 1.6 %copy-start.1 = (bf16[256,4096]{1,0:T(8,128)(2,1)S(1)}, bf16[256,4096]{1,0:T(8,128)(2,1)}, u32[]{:S(2)}) copy-start(bf16[256,4096]{1,0:T(8,128)(2,1)} %refs_0_.1) | copy-start | bytes 6291460
  5.9 1.9 %copy-start.2 = (bf16[256,2048]{1,0:T(8,128)(2,1)S(1)}, bf16[256,2048]{1,0:T(8,128)(2,1)}, u32[]{:S(2)}) copy-start(bf16[256,2048]{1,0:T(8,128)(2,1)} %refs_1_.1) | copy-start | bytes 3145732
  5.9 18.6 %collective-permute-start = (bf16[256,896]{1,0:T(8,128)(2,1)}, bf16[256,896]{1,0:T(8,128)(2,1)S(1)}, u32[]{:S(2)}, u32[]{:S(2)}) collective-permute-start(bf16[256,896]{1,0:T(8,128)(2,1)} %get-tuple-element.80), channel_id=1, source_target_pairs={{0,2},{1,3},{2,0},{3,1},{4,6},{5,7},{6,4},{7,5},{8,10},{9,11},{10,... | collective-permute-start | bytes 1376264 | tf_op jit(solution)/shard_map/ppermute | solution.py:280
  7.8 7.1 %copy-start.3 = (bf16[32,5120]{1,0:T(8,128)(2,1)S(1)}, bf16[32,5120]{1,0:T(8,128)(2,1)}, u32[]{:S(2)}) copy-start(bf16[32,5120]{1,0:T(8,128)(2,1)} %get-tuple-element.81.refs_0_) | copy-start | bytes 983044
  7.8 7.4 %copy-start.4 = (s32[4]{0:T(128)S(1)}, s32[4]{0:T(128)}, u32[]{:S(2)}) copy-start(s32[4]{0:T(128)} %param.12) | copy-start | bytes 52
  7.8 7.4 %copy-start.5 = (s32[1,4]{1,0:T(1,128)S(1)}, s32[1,4]{1,0:T(1,128)}, u32[]{:S(2)}) copy-start(s32[1,4]{1,0:T(1,128)} %param.11) | copy-start | bytes 52
  14.7 9.8 %collective-permute-start.3 = (bf16[32,5120]{1,0:T(8,128)(2,1)S(1)}, bf16[32,5120]{1,0:T(8,128)(2,1)S(1)}, u32[]{:S(2)}, u32[]{:S(2)}) collective-permute-start(bf16[32,5120]{1,0:T(8,128)(2,1)S(1)} %collective-permute-done.1.refs_2_), channel_id=1, source_target_pairs={{0,1},{1,0},{2,3},{3,2},{4,5},{5,4},{6,7},{7,6},{8,9},{9,8},{10,11... | collective-permute-start | bytes 983048 | tf_op jit(solution)/shard_map/ppermute | solution.py:280
  14.8 9.7 %collective-permute-start.4 = (bf16[32,5120]{1,0:T(8,128)(2,1)S(1)}, bf16[32,5120]{1,0:T(8,128)(2,1)S(1)}, u32[]{:S(2)}, u32[]{:S(2)}) collective-permute-start(bf16[32,5120]{1,0:T(8,128)(2,1)S(1)} %copy-done.3), channel_id=1, source_target_pairs={{0,1},{1,0},{2,3},{3,2},{4,5},{5,4},{6,7},{7,6},{8,9},{9,8},{10,11... | collective-permute-start | bytes 983048 | tf_op jit(solution)/shard_map/ppermute | solution.py:280
  26.6 4.0 %collective-permute-start.5 = (bf16[2,32,5120]{2,1,0:T(8,128)(2,1)S(1)}, bf16[2,32,5120]{2,1,0:T(8,128)(2,1)S(1)}, u32[]{:S(2)}, u32[]{:S(2)}) collective-permute-start(bf16[2,32,5120]{2,1,0:T(8,128)(2,1)S(1)} %get-tuple-element.94), channel_id=1, source_target_pairs={{0,1},{1,0},{2,3},{3,2},{4,5},{5,4},{6,7},{7,6},{8,9},{9,8},{10,11... | collective-permute-start | bytes 1966088 | tf_op jit(solution)/shard_map/ppermute | solution.py:280
  26.8 3.8 %collective-permute-start.6 = (bf16[256,896]{1,0:T(8,128)(2,1)S(1)}, bf16[256,896]{1,0:T(8,128)(2,1)S(1)}, u32[]{:S(2)}, u32[]{:S(2)}) collective-permute-start(bf16[256,896]{1,0:T(8,128)(2,1)S(1)} %collective-permute-done.refs_6_), channel_id=1, source_target_pairs={{0,1},{1,0},{2,3},{3,2},{4,5},{5,4},{6,7},{7,6},{8,9},{9,8},{10,11... | collective-permute-start | bytes 1376264 | tf_op jit(solution)/shard_map/ppermute | solution.py:280
  27.2 14.3 %collective-permute-start.7 = (bf16[256,896]{1,0:T(8,128)(2,1)S(1)}, bf16[256,896]{1,0:T(8,128)(2,1)S(1)}, u32[]{:S(2)}, u32[]{:S(2)}) collective-permute-start(bf16[256,896]{1,0:T(8,128)(2,1)S(1)} %collective-permute-done.refs_6_), channel_id=1, source_target_pairs={{0,4},{4,0},{8,12},{12,8},{1,5},{5,1},{9,13},{13,9},{2,6},{6,2},{1... | collective-permute-start | bytes 1376264 | tf_op jit(solution)/shard_map/ppermute | solution.py:280
  29.0 12.5 %collective-permute-start.8 = (bf16[256,896]{1,0:T(8,128)(2,1)S(1)}, bf16[256,896]{1,0:T(8,128)(2,1)S(1)}, u32[]{:S(2)}, u32[]{:S(2)}) collective-permute-start(bf16[256,896]{1,0:T(8,128)(2,1)S(1)} %collective-permute-done.refs_6_), channel_id=1, source_target_pairs={{0,16},{16,0},{1,17},{17,1},{2,18},{18,2},{3,19},{19,3},{4,20},{20... | collective-permute-start | bytes 1376264 | tf_op jit(solution)/shard_map/ppermute | solution.py:280
  30.7 10.7 %collective-permute-start.9 = (bf16[1,32,5120]{2,1,0:T(8,128)(2,1)S(1)}, bf16[1,32,5120]{2,1,0:T(8,128)(2,1)S(1)}, u32[]{:S(2)}, u32[]{:S(2)}) collective-permute-start(bf16[1,32,5120]{2,1,0:T(8,128)(2,1)S(1)} %get-tuple-element.105), channel_id=1, source_target_pairs={{0,2},{1,3},{2,0},{3,1},{4,6},{5,7},{6,4},{7,5},{8,10},{9,11},{10,... | collective-permute-start | bytes 983048 | tf_op jit(solution)/shard_map/ppermute | solution.py:280
  35.0 18.9 %collective-permute-start.11 = (bf16[256,1152]{1,0:T(8,128)(2,1)S(1)}, bf16[256,1152]{1,0:T(8,128)(2,1)S(1)}, u32[]{:S(2)}, u32[]{:S(2)}) collective-permute-start(bf16[256,1152]{1,0:T(8,128)(2,1)S(1)} %get-tuple-element.109), channel_id=1, source_target_pairs={{0,2},{1,3},{2,0},{3,1},{4,6},{5,7},{6,4},{7,5},{8,10},{9,11},{10,... | collective-permute-start | bytes 1769480 | tf_op jit(solution)/shard_map/ppermute | solution.py:280
  41.5 13.1 %collective-permute-start.10 = (bf16[256,896]{1,0:T(8,128)(2,1)S(1)}, bf16[256,896]{1,0:T(8,128)(2,1)S(1)}, u32[]{:S(2)}, u32[]{:S(2)}) collective-permute-start(bf16[256,896]{1,0:T(8,128)(2,1)S(1)} %collective-permute-done.7.refs_1_.refs_8_), channel_id=1, source_target_pairs={{0,16},{16,0},{1,17},{17,1},{2,18},{18,2},{3,19},{19,3},{4,20},{20... | collective-permute-start | bytes 1376264 | tf_op jit(solution)/shard_map/ppermute | solution.py:280
  42.9 5.4 %collective-permute-start.12 = (bf16[16,5120]{1,0:T(8,128)(2,1)S(1)}, bf16[16,5120]{1,0:T(8,128)(2,1)S(1)}, u32[]{:S(2)}, u32[]{:S(2)}) collective-permute-start(bf16[16,5120]{1,0:T(8,128)(2,1)S(1)} %get-tuple-element.117), channel_id=1, source_target_pairs={{0,4},{4,0},{8,12},{12,8},{1,5},{5,1},{9,13},{13,9},{2,6},{6,2},{1... | collective-permute-start | bytes 491528 | tf_op jit(solution)/shard_map/ppermute | solution.py:280
  48.4 8.4 %collective-permute-start.18 = (bf16[16,5120]{1,0:T(8,128)(2,1)S(1)}, bf16[16,5120]{1,0:T(8,128)(2,1)S(1)}, u32[]{:S(2)}, u32[]{:S(2)}) collective-permute-start(bf16[16,5120]{1,0:T(8,128)(2,1)S(1)} %add_convert_fusion.1), channel_id=1, source_target_pairs={{0,8},{4,12},{8,0},{12,4},{1,9},{5,13},{9,1},{13,5},{2,10},{6,14},... | collective-permute-start | bytes 491528 | tf_op jit(solution)/shard_map/ppermute | solution.py:280
  51.6 13.6 %collective-permute-start.16 = (bf16[256,1152]{1,0:T(8,128)(2,1)S(1)}, bf16[256,1152]{1,0:T(8,128)(2,1)S(1)}, u32[]{:S(2)}, u32[]{:S(2)}) collective-permute-start(bf16[256,1152]{1,0:T(8,128)(2,1)S(1)} %get-tuple-element.129), channel_id=1, source_target_pairs={{0,2},{1,3},{2,0},{3,1},{4,6},{5,7},{6,4},{7,5},{8,10},{9,11},{10,... | collective-permute-start | bytes 1769480 | tf_op jit(solution)/shard_map/ppermute | solution.py:280
  53.9 3.0 %collective-permute-start.17 = (bf16[256,1152]{1,0:T(8,128)(2,1)S(1)}, bf16[256,1152]{1,0:T(8,128)(2,1)S(1)}, u32[]{:S(2)}, u32[]{:S(2)}) collective-permute-start(bf16[256,1152]{1,0:T(8,128)(2,1)S(1)} %collective-permute-done.11.refs_7_), channel_id=1, source_target_pairs={{0,1},{1,0},{2,3},{3,2},{4,5},{5,4},{6,7},{7,6},{8,9},{9,8},{10,11... | collective-permute-start | bytes 1769480 | tf_op jit(solution)/shard_map/ppermute | solution.py:280
  53.9 15.7 %collective-permute-start.14 = (bf16[256,1152]{1,0:T(8,128)(2,1)S(1)}, bf16[256,1152]{1,0:T(8,128)(2,1)S(1)}, u32[]{:S(2)}, u32[]{:S(2)}) collective-permute-start(bf16[256,1152]{1,0:T(8,128)(2,1)S(1)} %collective-permute-done.11.refs_7_), channel_id=1, source_target_pairs={{0,16},{16,0},{1,17},{17,1},{2,18},{18,2},{3,19},{19,3},{4,20},{20... | collective-permute-start | bytes 1769480 | tf_op jit(solution)/shard_map/ppermute | solution.py:280
  54.7 15.5 %collective-permute-start.15 = (bf16[256,1152]{1,0:T(8,128)(2,1)S(1)}, bf16[256,1152]{1,0:T(8,128)(2,1)S(1)}, u32[]{:S(2)}, u32[]{:S(2)}) collective-permute-start(bf16[256,1152]{1,0:T(8,128)(2,1)S(1)} %collective-permute-done.11.refs_7_), channel_id=1, source_target_pairs={{0,4},{4,0},{8,12},{12,8},{1,5},{5,1},{9,13},{13,9},{2,6},{6,2},{1... | collective-permute-start | bytes 1769480 | tf_op jit(solution)/shard_map/ppermute | solution.py:280
  56.8 17.1 %collective-permute-start.13 = (bf16[3,256,896]{2,1,0:T(8,128)(2,1)S(1)}, bf16[3,256,896]{2,1,0:T(8,128)(2,1)S(1)}, u32[]{:S(2)}, u32[]{:S(2)}) collective-permute-start(bf16[3,256,896]{2,1,0:T(8,128)(2,1)S(1)} %stack.1), channel_id=1, source_target_pairs={{0,1},{1,0},{2,3},{3,2},{4,5},{5,4},{6,7},{7,6},{8,9},{9,8},{10,11... | collective-permute-start | bytes 4128776 | tf_op jit(solution)/shard_map/ppermute | solution.py:280
  70.1 3.8 %collective-permute-start.19 = (bf16[256,1152]{1,0:T(8,128)(2,1)S(1)}, bf16[256,1152]{1,0:T(8,128)(2,1)S(1)}, u32[]{:S(2)}, u32[]{:S(2)}) collective-permute-start(bf16[256,1152]{1,0:T(8,128)(2,1)S(1)} %collective-permute-done.14.refs_7_), channel_id=1, source_target_pairs={{0,1},{1,0},{2,3},{3,2},{4,5},{5,4},{6,7},{7,6},{8,9},{9,8},{10,11... | collective-permute-start | bytes 1769480 | tf_op jit(solution)/shard_map/ppermute | solution.py:280
  70.1 3.8 %collective-permute-start.20 = (bf16[256,1152]{1,0:T(8,128)(2,1)S(1)}, bf16[256,1152]{1,0:T(8,128)(2,1)S(1)}, u32[]{:S(2)}, u32[]{:S(2)}) collective-permute-start(bf16[256,1152]{1,0:T(8,128)(2,1)S(1)} %collective-permute-done.15.refs_9_), channel_id=1, source_target_pairs={{0,1},{1,0},{2,3},{3,2},{4,5},{5,4},{6,7},{7,6},{8,9},{9,8},{10,11... | collective-permute-start | bytes 1769480 | tf_op jit(solution)/shard_map/ppermute | solution.py:280
  70.6 3.3 %collective-permute-start.21 = (bf16[256,1152]{1,0:T(8,128)(2,1)S(1)}, bf16[256,1152]{1,0:T(8,128)(2,1)S(1)}, u32[]{:S(2)}, u32[]{:S(2)}) collective-permute-start(bf16[256,1152]{1,0:T(8,128)(2,1)S(1)} %collective-permute-done.16.refs_7_), channel_id=1, source_target_pairs={{0,1},{1,0},{2,3},{3,2},{4,5},{5,4},{6,7},{7,6},{8,9},{9,8},{10,11... | collective-permute-start | bytes 1769480 | tf_op jit(solution)/shard_map/ppermute | solution.py:280
  70.6 6.7 %collective-permute-start.22 = (bf16[16,5120]{1,0:T(8,128)(2,1)S(1)}, bf16[16,5120]{1,0:T(8,128)(2,1)S(1)}, u32[]{:S(2)}, u32[]{:S(2)}) collective-permute-start(bf16[16,5120]{1,0:T(8,128)(2,1)S(1)} %add_convert_fusion.mine), channel_id=1, source_target_pairs={{0,4},{4,0},{8,12},{12,8},{1,5},{5,1},{9,13},{13,9},{2,6},{6,2},{1... | collective-permute-start | bytes 491528 | tf_op jit(solution)/shard_map/ppermute | solution.py:280

commit v5 on v4

--- a/solution.py
+++ b/solution.py
@@ -163,6 +163,7 @@
         refs.pop(0)
     out, gx = refs.pop(0), refs.pop(0)
     stage, sems = refs.pop(0), refs.pop(0)
+    held = refs.pop(0) if last else None
     acc = out
     if first:
         col = lax.broadcasted_iota(jnp.int32, low.shape, 1)
@@ -199,7 +200,11 @@
             inner = slice(low_edge - span.start, edge - span.start)
             total += dot(tok[:, where], chunk[pl.ds(at, block), inner])
         if last:
-            out[:, cols] = total.astype(BF16)
+            number = len(copies)
+            held[:, cols] = total.astype(BF16)
+            copy = pltpu.make_async_copy(held.at[:, cols], out.at[:, cols], sems.at[number])
+            copy.start()
+            copies.append(copy)
         else:
             out[:, cols] = total
     for copy in copies:
@@ -234,12 +239,16 @@
         aliases = {len(args) - 1: 1}
         if not last:
             aliases[len(args) - 2] = 0
-    scratch = [pltpu.VMEM((count, rows, block), BF16), pltpu.SemaphoreType.DMA((count,))]
+    widths = sum(len(parts) for _, parts in sources)
+    sems = count + (widths if last else 0)
+    scratch = [pltpu.VMEM((count, rows, block), BF16), pltpu.SemaphoreType.DMA((sems,))]
+    if last:
+        scratch.append(pltpu.VMEM((rows, cols), BF16))
     return pl.pallas_call(
         functools.partial(matmul_kernel, plan, block, shard, rank2, kv, first, last),
         out_shape=(struct((rows, cols), BF16 if last else F32), struct((rows, width))),
         in_specs=in_specs,
-        out_specs=(VMEM, HBM),
+        out_specs=(HBM if last else VMEM, HBM),
         scratch_shapes=scratch,
         input_output_aliases=aliases,
         compiler_params=params(),

time: 78.4 us -> 78.3 us (level)
  transfers between devices with their start and end apart: 23 -> 23, of which waited for: 9 -> 10; matrix products, arithmetic and copies ran while one was open for 0% -> 0% of each run, Pallas kernels for 22% -> 21%
where the time goes in v5:
time: 78.3 us; the launch traced here: 78.1 us
  waiting for transfers between devices  34.5 us (44%)
  starting transfers between devices  21.2 us (27%)
  Pallas kernels  19.7 us (25%)
  local copies, waits for them, and re-layouts  1.76 us (2%)
  between operations  0.84 us (1%)
    ppermute x23, waiting for transfers between devices, xor_swap(): return lax.ppermute(value, axis, [(i, i ^ bit) for i in range(size)])  34.5 us
    ppermute x23, starting transfers between devices, xor_swap(): return lax.ppermute(value, axis, [(i, i ^ bit) for i in range(size)])  21.2 us
    pallas_call x6, Pallas kernels, matmul_call(): pl.pallas_call(functools.partial(matmul_kernel, plan, block, shard, rank2...  13.5 us
    pallas_call x7, Pallas kernels, local(): pl.pallas_call(kernel, out_shape=tuple(outs), in_specs=spaces, out_specs=...  4.15 us
    pallas_call x1, Pallas kernels, low_rank_call(): pl.pallas_call(functools.partial(low_rank_kernel, slots, rank2, width, kv...  2.09 us
    unnamed x13, local copies, waits for them, and re-layouts  1.76 us
  transfers between devices with their start and end apart: 23, of which 10 were waited for; matrix products, arithmetic and copies ran while one was open for 0% of the time, Pallas kernels for 21%

profile of v5, /device:TPU:0, one launch (start us, length us, event | category | flops | bytes accessed | tf_op | source)
XLA Modules:
  0.0 78.1 jit_solution(6227192775616546295)
XLA Ops:
  0.6 0.5 collective-permute-start.2
  1.2 2.3 %prep.1 = (bf16[32,5120]{1,0:T(8,128)(2,1)}, bf16[256,896]{1,0:T(8,128)(2,1)}) custom-call(bf16[1024,2048]{1,0:T(8,128)(2,1)} %weight.3, bf16[1,32,4096]{2,1,0:T(8,128)(2,1)} %down.1, bf16[1,32,1024]{2,1,0:T(8,128)(2,1)} %up.1), custom_call_target="tpu_custom_call" | custom-call | flops 1 | bytes 1 | tf_op jit(solution)/shard_map/prep/pallas_call | solution.py:324
  3.5 2.5 %collective-permute-start.1 = (bf16[32,5120]{1,0:T(8,128)(2,1)}, bf16[32,5120]{1,0:T(8,128)(2,1)S(1)}, u32[]{:S(2)}, u32[]{:S(2)}) collective-permute-start(bf16[32,5120]{1,0:T(8,128)(2,1)} %get-tuple-element.81.refs_0_), channel_id=1, source_target_pairs={{0,2},{1,3},{2,0},{3,1},{4,6},{5,7},{6,4},{7,5},{8,10},{9,11},{10,... | collective-permute-start | bytes 983048 | tf_op jit(solution)/shard_map/ppermute | solution.py:289
  6.2 1.3 %copy-done.1 = bf16[256,4096]{1,0:T(8,128)(2,1)S(1)} copy-done((bf16[256,4096]{1,0:T(8,128)(2,1)S(1)}, bf16[256,4096]{1,0:T(8,128)(2,1)}, u32[]{:S(2)}) %copy-start.1) | copy-done | bytes 2097176
  7.8 0.5 load.1
  8.3 6.4 %collective-permute-done.1.refs_2_ = bf16[32,5120]{1,0:T(8,128)(2,1)S(1)} collective-permute-done((bf16[32,5120]{1,0:T(8,128)(2,1)}, bf16[32,5120]{1,0:T(8,128)(2,1)S(1)}, u32[]{:S(2)}, u32[]{:S(2)}) %collective-permute-start.1) | collective-permute-done | bytes 327712 | tf_op jit(solution)/shard_map/ppermute | solution.py:289
  15.3 9.2 %collective-permute-done.refs_6_ = bf16[256,896]{1,0:T(8,128)(2,1)S(1)} collective-permute-done((bf16[256,896]{1,0:T(8,128)(2,1)}, bf16[256,896]{1,0:T(8,128)(2,1)S(1)}, u32[]{:S(2)}, u32[]{:S(2)}) %collective-permute-start) | collective-permute-done | bytes 458784 | tf_op jit(solution)/shard_map/ppermute | solution.py:289
  24.5 2.1 %low_rank.1 = (bf16[256,128]{1,0:T(8,128)(2,1)S(1)}, bf16[256,128]{1,0:T(8,128)(2,1)S(1)}, bf16[128,4096]{1,0:T(8,128)(2,1)S(1)}, bf16[128,1024]{1,0:T(8,128)(2,...) custom-call(s32[8]{0:T(128)S(1)} %pad_add_fusion.place, ...), custom_call_target="tpu_custom_call" | custom-call | flops 1 | bytes 1 | tf_op jit(solution)/shard_map/low_rank/pallas_call | solution.py:137
  27.2 1.9 %collective-permute-start.7 = (bf16[256,896]{1,0:T(8,128)(2,1)S(1)}, bf16[256,896]{1,0:T(8,128)(2,1)S(1)}, u32[]{:S(2)}, u32[]{:S(2)}) collective-permute-start(bf16[256,896]{1,0:T(8,128)(2,1)S(1)} %collective-permute-done.refs_6_), channel_id=1, source_target_pairs={{0,4},{4,0},{8,12},{12,8},{1,5},{5,1},{9,13},{13,9},{2,6},{6,2},{1... | collective-permute-start | bytes 1376264 | tf_op jit(solution)/shard_map/ppermute | solution.py:289
  29.0 1.5 %collective-permute-start.8 = (bf16[256,896]{1,0:T(8,128)(2,1)S(1)}, bf16[256,896]{1,0:T(8,128)(2,1)S(1)}, u32[]{:S(2)}, u32[]{:S(2)}) collective-permute-start(bf16[256,896]{1,0:T(8,128)(2,1)S(1)} %collective-permute-done.refs_6_), channel_id=1, source_target_pairs={{0,16},{16,0},{1,17},{17,1},{2,18},{18,2},{3,19},{19,3},{4,20},{20... | collective-permute-start | bytes 1376264 | tf_op jit(solution)/shard_map/ppermute | solution.py:289
  30.7 1.6 %collective-permute-start.9 = (bf16[1,32,5120]{2,1,0:T(8,128)(2,1)S(1)}, bf16[1,32,5120]{2,1,0:T(8,128)(2,1)S(1)}, u32[]{:S(2)}, u32[]{:S(2)}) collective-permute-start(bf16[1,32,5120]{2,1,0:T(8,128)(2,1)S(1)} %get-tuple-element.105), channel_id=1, source_target_pairs={{0,2},{1,3},{2,0},{3,1},{4,6},{5,7},{6,4},{7,5},{8,10},{9,11},{10,... | collective-permute-start | bytes 983048 | tf_op jit(solution)/shard_map/ppermute | solution.py:289
  32.3 2.8 %matmul_0.1 = (f32[256,2048]{1,0:T(8,128)S(1)}, bf16[256,4096]{1,0:T(8,128)(2,1)}) custom-call(bf16[256,4096]{1,0:T(8,128)(2,1)S(1)} %get-tuple-element.89.tok.refs_0_, bf16[256,2048]{1,0:T(8,128)(2,1)S(1)} %get-tuple-element.90.cot.refs_1_, bf16[256,128]{1,0:T(8,128)(2,1)S(1)} %get-tuple-element.101.refs_2_, ...), custom_call_target="tpu_custom_call" | custom-call | flops 2147483648 | bytes 1 | tf_op jit(solution)/shard_map/matmul_0/pallas_call | solution.py:247
  35.0 0.6 collective-permute-start.11
  35.6 5.8 %collective-permute-done.9.recv = bf16[1,32,5120]{2,1,0:T(8,128)(2,1)S(1)} collective-permute-done((bf16[1,32,5120]{2,1,0:T(8,128)(2,1)S(1)}, bf16[1,32,5120]{2,1,0:T(8,128)(2,1)S(1)}, u32[]{:S(2)}, u32[]{:S(2)}) %collective-permute-start.9) | collective-permute-done | bytes 327712 | tf_op jit(solution)/shard_map/ppermute | solution.py:289
  41.5 1.3 %collective-permute-start.10 = (bf16[256,896]{1,0:T(8,128)(2,1)S(1)}, bf16[256,896]{1,0:T(8,128)(2,1)S(1)}, u32[]{:S(2)}, u32[]{:S(2)}) collective-permute-start(bf16[256,896]{1,0:T(8,128)(2,1)S(1)} %collective-permute-done.7.refs_1_.refs_8_), channel_id=1, source_target_pairs={{0,16},{16,0},{1,17},{17,1},{2,18},{18,2},{3,19},{19,3},{4,20},{20... | collective-permute-start | bytes 1376264 | tf_op jit(solution)/shard_map/ppermute | solution.py:289
  42.9 1.0 %collective-permute-start.12 = (bf16[16,5120]{1,0:T(8,128)(2,1)S(1)}, bf16[16,5120]{1,0:T(8,128)(2,1)S(1)}, u32[]{:S(2)}, u32[]{:S(2)}) collective-permute-start(bf16[16,5120]{1,0:T(8,128)(2,1)S(1)} %get-tuple-element.117), channel_id=1, source_target_pairs={{0,4},{4,0},{8,12},{12,8},{1,5},{5,1},{9,13},{13,9},{2,6},{6,2},{1... | collective-permute-start | bytes 491528 | tf_op jit(solution)/shard_map/ppermute | solution.py:289
  44.0 2.7 %matmul_1.1 = (f32[256,2048]{1,0:T(8,128)S(1)}, bf16[256,4096]{1,0:T(8,128)(2,1)}) custom-call(bf16[256,4096]{1,0:T(8,128)(2,1)S(1)} %get-tuple-element.89.tok.refs_0_, bf16[256,2048]{1,0:T(8,128)(2,1)S(1)} %get-tuple-element.90.cot.refs_1_, bf16[256,128]{1,0:T(8,128)(2,1)S(1)} %get-tuple-element.101.refs_2_, ...), custom_call_target="tpu_custom_call", output_to_operand_aliasing={{1}: (8, {}), {0}: (7, {})} | custom-call | flops 2147483648 | bytes 1 | tf_op jit(solution)/shard_map/matmul_1/pallas_call | solution.py:247
  46.6 1.7 %collective-permute-done.12 = bf16[16,5120]{1,0:T(8,128)(2,1)S(1)} collective-permute-done((bf16[16,5120]{1,0:T(8,128)(2,1)S(1)}, bf16[16,5120]{1,0:T(8,128)(2,1)S(1)}, u32[]{:S(2)}, u32[]{:S(2)}) %collective-permute-start.12) | collective-permute-done | bytes 163872 | tf_op jit(solution)/shard_map/ppermute | solution.py:289
  48.4 3.2 %collective-permute-start.18 = (bf16[16,5120]{1,0:T(8,128)(2,1)S(1)}, bf16[16,5120]{1,0:T(8,128)(2,1)S(1)}, u32[]{:S(2)}, u32[]{:S(2)}) collective-permute-start(bf16[16,5120]{1,0:T(8,128)(2,1)S(1)} %add_convert_fusion.1), channel_id=1, source_target_pairs={{0,8},{4,12},{8,0},{12,4},{1,9},{5,13},{9,1},{13,5},{2,10},{6,14},... | collective-permute-start | bytes 491528 | tf_op jit(solution)/shard_map/ppermute | solution.py:289
  51.6 1.5 %collective-permute-start.16 = (bf16[256,1152]{1,0:T(8,128)(2,1)S(1)}, bf16[256,1152]{1,0:T(8,128)(2,1)S(1)}, u32[]{:S(2)}, u32[]{:S(2)}) collective-permute-start(bf16[256,1152]{1,0:T(8,128)(2,1)S(1)} %get-tuple-element.129), channel_id=1, source_target_pairs={{0,2},{1,3},{2,0},{3,1},{4,6},{5,7},{6,4},{7,5},{8,10},{9,11},{10,... | collective-permute-start | bytes 1769480 | tf_op jit(solution)/shard_map/ppermute | solution.py:289
  53.1 0.9 %collective-permute-done.11.refs_7_ = bf16[256,1152]{1,0:T(8,128)(2,1)S(1)} collective-permute-done((bf16[256,1152]{1,0:T(8,128)(2,1)S(1)}, bf16[256,1152]{1,0:T(8,128)(2,1)S(1)}, u32[]{:S(2)}, u32[]{:S(2)}) %collective-permute-start.11) | collective-permute-done | bytes 589856 | tf_op jit(solution)/shard_map/ppermute | solution.py:289
  53.9 0.7 collective-permute-start.14
  54.7 1.6 %collective-permute-start.15 = (bf16[256,1152]{1,0:T(8,128)(2,1)S(1)}, bf16[256,1152]{1,0:T(8,128)(2,1)S(1)}, u32[]{:S(2)}, u32[]{:S(2)}) collective-permute-start(bf16[256,1152]{1,0:T(8,128)(2,1)S(1)} %collective-permute-done.11.refs_7_), channel_id=1, source_target_pairs={{0,4},{4,0},{8,12},{12,8},{1,5},{5,1},{9,13},{13,9},{2,6},{6,2},{1... | collective-permute-start | bytes 1769480 | tf_op jit(solution)/shard_map/ppermute | solution.py:289
  57.0 1.7 %matmul_2.1 = (f32[256,2048]{1,0:T(8,128)S(1)}, bf16[256,4096]{1,0:T(8,128)(2,1)}) custom-call(bf16[256,4096]{1,0:T(8,128)(2,1)S(1)} %get-tuple-element.89.tok.refs_0_, bf16[256,2048]{1,0:T(8,128)(2,1)S(1)} %get-tuple-element.90.cot.refs_1_, bf16[256,128]{1,0:T(8,128)(2,1)S(1)} %get-tuple-element.101.refs_2_, ...), custom_call_target="tpu_custom_call", output_to_operand_aliasing={{1}: (11, {}), {0}: (10, {})} | custom-call | flops 1073741824 | bytes 1 | tf_op jit(solution)/shard_map/matmul_2/pallas_call | solution.py:247
  58.7 6.5 %collective-permute-done.16.refs_7_ = bf16[256,1152]{1,0:T(8,128)(2,1)S(1)} collective-permute-done((bf16[256,1152]{1,0:T(8,128)(2,1)S(1)}, bf16[256,1152]{1,0:T(8,128)(2,1)S(1)}, u32[]{:S(2)}, u32[]{:S(2)}) %collective-permute-start.16) | collective-permute-done | bytes 589856 | tf_op jit(solution)/shard_map/ppermute | solution.py:289
  65.2 1.7 %matmul_3.1 = (f32[256,2048]{1,0:T(8,128)S(1)}, bf16[256,4096]{1,0:T(8,128)(2,1)}) custom-call(bf16[256,4096]{1,0:T(8,128)(2,1)S(1)} %get-tuple-element.89.tok.refs_0_, bf16[256,2048]{1,0:T(8,128)(2,1)S(1)} %get-tuple-element.90.cot.refs_1_, bf16[256,128]{1,0:T(8,128)(2,1)S(1)} %get-tuple-element.101.refs_2_, ...), custom_call_target="tpu_custom_call", output_to_operand_aliasing={{1}: (9, {}), {0}: (8, {})} | custom-call | flops 536870912 | bytes 1 | tf_op jit(solution)/shard_map/matmul_3/pallas_call | solution.py:247
  66.9 2.8 %collective-permute-done.14.refs_7_ = bf16[256,1152]{1,0:T(8,128)(2,1)S(1)} collective-permute-done((bf16[256,1152]{1,0:T(8,128)(2,1)S(1)}, bf16[256,1152]{1,0:T(8,128)(2,1)S(1)}, u32[]{:S(2)}, u32[]{:S(2)}) %collective-permute-start.14) | collective-permute-done | bytes 589856 | tf_op jit(solution)/shard_map/ppermute | solution.py:289
  70.1 0.5 collective-permute-start.20
  70.6 1.6 %collective-permute-start.22 = (bf16[16,5120]{1,0:T(8,128)(2,1)S(1)}, bf16[16,5120]{1,0:T(8,128)(2,1)S(1)}, u32[]{:S(2)}, u32[]{:S(2)}) collective-permute-start(bf16[16,5120]{1,0:T(8,128)(2,1)S(1)} %add_convert_fusion.mine), channel_id=1, source_target_pairs={{0,4},{4,0},{8,12},{12,8},{1,5},{5,1},{9,13},{13,9},{2,6},{6,2},{1... | collective-permute-start | bytes 491528 | tf_op jit(solution)/shard_map/ppermute | solution.py:289
  72.2 1.7 %matmul_4.1 = (f32[256,2048]{1,0:T(8,128)S(1)}, bf16[256,4096]{1,0:T(8,128)(2,1)}) custom-call(bf16[256,4096]{1,0:T(8,128)(2,1)S(1)} %get-tuple-element.89.tok.refs_0_, bf16[256,2048]{1,0:T(8,128)(2,1)S(1)} %get-tuple-element.90.cot.refs_1_, bf16[256,128]{1,0:T(8,128)(2,1)S(1)} %get-tuple-element.101.refs_2_, ...), custom_call_target="tpu_custom_call", output_to_operand_aliasing={{1}: (11, {}), {0}: (10, {})} | custom-call | flops 1073741824 | bytes 1 | tf_op jit(solution)/shard_map/matmul_4/pallas_call | solution.py:247
  73.9 3.1 %matmul_5.1 = (bf16[256,2048]{1,0:T(8,128)(2,1)}, bf16[256,4096]{1,0:T(8,128)(2,1)}) custom-call(bf16[256,4096]{1,0:T(8,128)(2,1)S(1)} %get-tuple-element.89.tok.refs_0_, bf16[256,2048]{1,0:T(8,128)(2,1)S(1)} %get-tuple-element.90.cot.refs_1_, bf16[256,128]{1,0:T(8,128)(2,1)S(1)} %get-tuple-element.101.refs_2_, ...), custom_call_target="tpu_custom_call", output_to_operand_aliasing={{1}: (13, {})} | custom-call | flops 1610612736 | bytes 1 | tf_op jit(solution)/shard_map/matmul_5/pallas_call | solution.py:247
  77.2 0.9 %finish.1 = (f32[1,32,4096]{2,1,0:T(8,128)}, f32[1,32,1024]{2,1,0:T(8,128)}) custom-call(bf16[16,5120]{1,0:T(8,128)(2,1)S(1)} %add_convert_fusion.mine, bf16[16,5120]{1,0:T(8,128)(2,1)S(1)} %collective-permute-done.22.recv), custom_call_target="tpu_custom_call" | custom-call | flops 1 | bytes 1 | tf_op jit(solution)/shard_map/finish/pallas_call | solution.py:324
  (44 shorter events, 3.5 us)
Async XLA Ops:
  0.6 5.4 %copy-start = (bf16[1024,2048]{1,0:T(8,128)(2,1)S(1)}, bf16[1024,2048]{1,0:T(8,128)(2,1)}, u32[]{:S(2)}) copy-start(bf16[1024,2048]{1,0:T(8,128)(2,1)} %weight.3) | copy-start | bytes 12582916
  0.6 14.0 %collective-permute-start.2 = (bf16[1024,2048]{1,0:T(8,128)(2,1)}, bf16[1024,2048]{1,0:T(8,128)(2,1)S(1)}, u32[]{:S(2)}, u32[]{:S(2)}) collective-permute-start(bf16[1024,2048]{1,0:T(8,128)(2,1)} %weight.3), channel_id=1, source_target_pairs={{0,1},{1,0},{2,3},{3,2},{4,5},{5,4},{6,7},{7,6},{8,9},{9,8},{10,11... | collective-permute-start | bytes 12582920 | tf_op jit(solution)/shard_map/ppermute | solution.py:289
  3.5 11.2 %collective-permute-start.1 = (bf16[32,5120]{1,0:T(8,128)(2,1)}, bf16[32,5120]{1,0:T(8,128)(2,1)S(1)}, u32[]{:S(2)}, u32[]{:S(2)}) collective-permute-start(bf16[32,5120]{1,0:T(8,128)(2,1)} %get-tuple-element.81.refs_0_), channel_id=1, source_target_pairs={{0,2},{1,3},{2,0},{3,1},{4,6},{5,7},{6,4},{7,5},{8,10},{9,11},{10,... | collective-permute-start | bytes 983048 | tf_op jit(solution)/shard_map/ppermute | solution.py:289
  5.9 1.6 %copy-start.1 = (bf16[256,4096]{1,0:T(8,128)(2,1)S(1)}, bf16[256,4096]{1,0:T(8,128)(2,1)}, u32[]{:S(2)}) copy-start(bf16[256,4096]{1,0:T(8,128)(2,1)} %refs_0_.1) | copy-start | bytes 6291460
  5.9 1.9 %copy-start.2 = (bf16[256,2048]{1,0:T(8,128)(2,1)S(1)}, bf16[256,2048]{1,0:T(8,128)(2,1)}, u32[]{:S(2)}) copy-start(bf16[256,2048]{1,0:T(8,128)(2,1)} %refs_1_.1) | copy-start | bytes 3145732
  5.9 18.6 %collective-permute-start = (bf16[256,896]{1,0:T(8,128)(2,1)}, bf16[256,896]{1,0:T(8,128)(2,1)S(1)}, u32[]{:S(2)}, u32[]{:S(2)}) collective-permute-start(bf16[256,896]{1,0:T(8,128)(2,1)} %get-tuple-element.80), channel_id=1, source_target_pairs={{0,2},{1,3},{2,0},{3,1},{4,6},{5,7},{6,4},{7,5},{8,10},{9,11},{10,... | collective-permute-start | bytes 1376264 | tf_op jit(solution)/shard_map/ppermute | solution.py:289
  7.8 7.1 %copy-start.3 = (bf16[32,5120]{1,0:T(8,128)(2,1)S(1)}, bf16[32,5120]{1,0:T(8,128)(2,1)}, u32[]{:S(2)}) copy-start(bf16[32,5120]{1,0:T(8,128)(2,1)} %get-tuple-element.81.refs_0_) | copy-start | bytes 983044
  7.8 7.4 %copy-start.4 = (s32[4]{0:T(128)S(1)}, s32[4]{0:T(128)}, u32[]{:S(2)}) copy-start(s32[4]{0:T(128)} %param.12) | copy-start | bytes 52
  7.8 7.4 %copy-start.5 = (s32[1,4]{1,0:T(1,128)S(1)}, s32[1,4]{1,0:T(1,128)}, u32[]{:S(2)}) copy-start(s32[1,4]{1,0:T(1,128)} %param.11) | copy-start | bytes 52
  14.7 9.8 %collective-permute-start.3 = (bf16[32,5120]{1,0:T(8,128)(2,1)S(1)}, bf16[32,5120]{1,0:T(8,128)(2,1)S(1)}, u32[]{:S(2)}, u32[]{:S(2)}) collective-permute-start(bf16[32,5120]{1,0:T(8,128)(2,1)S(1)} %collective-permute-done.1.refs_2_), channel_id=1, source_target_pairs={{0,1},{1,0},{2,3},{3,2},{4,5},{5,4},{6,7},{7,6},{8,9},{9,8},{10,11... | collective-permute-start | bytes 983048 | tf_op jit(solution)/shard_map/ppermute | solution.py:289
  14.8 9.7 %collective-permute-start.4 = (bf16[32,5120]{1,0:T(8,128)(2,1)S(1)}, bf16[32,5120]{1,0:T(8,128)(2,1)S(1)}, u32[]{:S(2)}, u32[]{:S(2)}) collective-permute-start(bf16[32,5120]{1,0:T(8,128)(2,1)S(1)} %copy-done.3), channel_id=1, source_target_pairs={{0,1},{1,0},{2,3},{3,2},{4,5},{5,4},{6,7},{7,6},{8,9},{9,8},{10,11... | collective-permute-start | bytes 983048 | tf_op jit(solution)/shard_map/ppermute | solution.py:289
  26.6 4.0 %collective-permute-start.5 = (bf16[2,32,5120]{2,1,0:T(8,128)(2,1)S(1)}, bf16[2,32,5120]{2,1,0:T(8,128)(2,1)S(1)}, u32[]{:S(2)}, u32[]{:S(2)}) collective-permute-start(bf16[2,32,5120]{2,1,0:T(8,128)(2,1)S(1)} %get-tuple-element.94), channel_id=1, source_target_pairs={{0,1},{1,0},{2,3},{3,2},{4,5},{5,4},{6,7},{7,6},{8,9},{9,8},{10,11... | collective-permute-start | bytes 1966088 | tf_op jit(solution)/shard_map/ppermute | solution.py:289
  26.8 3.8 %collective-permute-start.6 = (bf16[256,896]{1,0:T(8,128)(2,1)S(1)}, bf16[256,896]{1,0:T(8,128)(2,1)S(1)}, u32[]{:S(2)}, u32[]{:S(2)}) collective-permute-start(bf16[256,896]{1,0:T(8,128)(2,1)S(1)} %collective-permute-done.refs_6_), channel_id=1, source_target_pairs={{0,1},{1,0},{2,3},{3,2},{4,5},{5,4},{6,7},{7,6},{8,9},{9,8},{10,11... | collective-permute-start | bytes 1376264 | tf_op jit(solution)/shard_map/ppermute | solution.py:289
  27.2 14.3 %collective-permute-start.7 = (bf16[256,896]{1,0:T(8,128)(2,1)S(1)}, bf16[256,896]{1,0:T(8,128)(2,1)S(1)}, u32[]{:S(2)}, u32[]{:S(2)}) collective-permute-start(bf16[256,896]{1,0:T(8,128)(2,1)S(1)} %collective-permute-done.refs_6_), channel_id=1, source_target_pairs={{0,4},{4,0},{8,12},{12,8},{1,5},{5,1},{9,13},{13,9},{2,6},{6,2},{1... | collective-permute-start | bytes 1376264 | tf_op jit(solution)/shard_map/ppermute | solution.py:289
  29.0 12.5 %collective-permute-start.8 = (bf16[256,896]{1,0:T(8,128)(2,1)S(1)}, bf16[256,896]{1,0:T(8,128)(2,1)S(1)}, u32[]{:S(2)}, u32[]{:S(2)}) collective-permute-start(bf16[256,896]{1,0:T(8,128)(2,1)S(1)} %collective-permute-done.refs_6_), channel_id=1, source_target_pairs={{0,16},{16,0},{1,17},{17,1},{2,18},{18,2},{3,19},{19,3},{4,20},{20... | collective-permute-start | bytes 1376264 | tf_op jit(solution)/shard_map/ppermute | solution.py:289
  30.7 10.7 %collective-permute-start.9 = (bf16[1,32,5120]{2,1,0:T(8,128)(2,1)S(1)}, bf16[1,32,5120]{2,1,0:T(8,128)(2,1)S(1)}, u32[]{:S(2)}, u32[]{:S(2)}) collective-permute-start(bf16[1,32,5120]{2,1,0:T(8,128)(2,1)S(1)} %get-tuple-element.105), channel_id=1, source_target_pairs={{0,2},{1,3},{2,0},{3,1},{4,6},{5,7},{6,4},{7,5},{8,10},{9,11},{10,... | collective-permute-start | bytes 983048 | tf_op jit(solution)/shard_map/ppermute | solution.py:289
  35.0 18.9 %collective-permute-start.11 = (bf16[256,1152]{1,0:T(8,128)(2,1)S(1)}, bf16[256,1152]{1,0:T(8,128)(2,1)S(1)}, u32[]{:S(2)}, u32[]{:S(2)}) collective-permute-start(bf16[256,1152]{1,0:T(8,128)(2,1)S(1)} %get-tuple-element.109), channel_id=1, source_target_pairs={{0,2},{1,3},{2,0},{3,1},{4,6},{5,7},{6,4},{7,5},{8,10},{9,11},{10,... | collective-permute-start | bytes 1769480 | tf_op jit(solution)/shard_map/ppermute | solution.py:289
  41.5 13.1 %collective-permute-start.10 = (bf16[256,896]{1,0:T(8,128)(2,1)S(1)}, bf16[256,896]{1,0:T(8,128)(2,1)S(1)}, u32[]{:S(2)}, u32[]{:S(2)}) collective-permute-start(bf16[256,896]{1,0:T(8,128)(2,1)S(1)} %collective-permute-done.7.refs_1_.refs_8_), channel_id=1, source_target_pairs={{0,16},{16,0},{1,17},{17,1},{2,18},{18,2},{3,19},{19,3},{4,20},{20... | collective-permute-start | bytes 1376264 | tf_op jit(solution)/shard_map/ppermute | solution.py:289
  42.9 5.4 %collective-permute-start.12 = (bf16[16,5120]{1,0:T(8,128)(2,1)S(1)}, bf16[16,5120]{1,0:T(8,128)(2,1)S(1)}, u32[]{:S(2)}, u32[]{:S(2)}) collective-permute-start(bf16[16,5120]{1,0:T(8,128)(2,1)S(1)} %get-tuple-element.117), channel_id=1, source_target_pairs={{0,4},{4,0},{8,12},{12,8},{1,5},{5,1},{9,13},{13,9},{2,6},{6,2},{1... | collective-permute-start | bytes 491528 | tf_op jit(solution)/shard_map/ppermute | solution.py:289
  48.4 8.4 %collective-permute-start.18 = (bf16[16,5120]{1,0:T(8,128)(2,1)S(1)}, bf16[16,5120]{1,0:T(8,128)(2,1)S(1)}, u32[]{:S(2)}, u32[]{:S(2)}) collective-permute-start(bf16[16,5120]{1,0:T(8,128)(2,1)S(1)} %add_convert_fusion.1), channel_id=1, source_target_pairs={{0,8},{4,12},{8,0},{12,4},{1,9},{5,13},{9,1},{13,5},{2,10},{6,14},... | collective-permute-start | bytes 491528 | tf_op jit(solution)/shard_map/ppermute | solution.py:289
  51.6 13.6 %collective-permute-start.16 = (bf16[256,1152]{1,0:T(8,128)(2,1)S(1)}, bf16[256,1152]{1,0:T(8,128)(2,1)S(1)}, u32[]{:S(2)}, u32[]{:S(2)}) collective-permute-start(bf16[256,1152]{1,0:T(8,128)(2,1)S(1)} %get-tuple-element.129), channel_id=1, source_target_pairs={{0,2},{1,3},{2,0},{3,1},{4,6},{5,7},{6,4},{7,5},{8,10},{9,11},{10,... | collective-permute-start | bytes 1769480 | tf_op jit(solution)/shard_map/ppermute | solution.py:289
  53.9 3.0 %collective-permute-start.17 = (bf16[256,1152]{1,0:T(8,128)(2,1)S(1)}, bf16[256,1152]{1,0:T(8,128)(2,1)S(1)}, u32[]{:S(2)}, u32[]{:S(2)}) collective-permute-start(bf16[256,1152]{1,0:T(8,128)(2,1)S(1)} %collective-permute-done.11.refs_7_), channel_id=1, source_target_pairs={{0,1},{1,0},{2,3},{3,2},{4,5},{5,4},{6,7},{7,6},{8,9},{9,8},{10,11... | collective-permute-start | bytes 1769480 | tf_op jit(solution)/shard_map/ppermute | solution.py:289
  53.9 15.7 %collective-permute-start.14 = (bf16[256,1152]{1,0:T(8,128)(2,1)S(1)}, bf16[256,1152]{1,0:T(8,128)(2,1)S(1)}, u32[]{:S(2)}, u32[]{:S(2)}) collective-permute-start(bf16[256,1152]{1,0:T(8,128)(2,1)S(1)} %collective-permute-done.11.refs_7_), channel_id=1, source_target_pairs={{0,16},{16,0},{1,17},{17,1},{2,18},{18,2},{3,19},{19,3},{4,20},{20... | collective-permute-start | bytes 1769480 | tf_op jit(solution)/shard_map/ppermute | solution.py:289
  54.7 15.5 %collective-permute-start.15 = (bf16[256,1152]{1,0:T(8,128)(2,1)S(1)}, bf16[256,1152]{1,0:T(8,128)(2,1)S(1)}, u32[]{:S(2)}, u32[]{:S(2)}) collective-permute-start(bf16[256,1152]{1,0:T(8,128)(2,1)S(1)} %collective-permute-done.11.refs_7_), channel_id=1, source_target_pairs={{0,4},{4,0},{8,12},{12,8},{1,5},{5,1},{9,13},{13,9},{2,6},{6,2},{1... | collective-permute-start | bytes 1769480 | tf_op jit(solution)/shard_map/ppermute | solution.py:289
  56.8 17.1 %collective-permute-start.13 = (bf16[3,256,896]{2,1,0:T(8,128)(2,1)S(1)}, bf16[3,256,896]{2,1,0:T(8,128)(2,1)S(1)}, u32[]{:S(2)}, u32[]{:S(2)}) collective-permute-start(bf16[3,256,896]{2,1,0:T(8,128)(2,1)S(1)} %stack.1), channel_id=1, source_target_pairs={{0,1},{1,0},{2,3},{3,2},{4,5},{5,4},{6,7},{7,6},{8,9},{9,8},{10,11... | collective-permute-start | bytes 4128776 | tf_op jit(solution)/shard_map/ppermute | solution.py:289
  70.1 3.8 %collective-permute-start.19 = (bf16[256,1152]{1,0:T(8,128)(2,1)S(1)}, bf16[256,1152]{1,0:T(8,128)(2,1)S(1)}, u32[]{:S(2)}, u32[]{:S(2)}) collective-permute-start(bf16[256,1152]{1,0:T(8,128)(2,1)S(1)} %collective-permute-done.14.refs_7_), channel_id=1, source_target_pairs={{0,1},{1,0},{2,3},{3,2},{4,5},{5,4},{6,7},{7,6},{8,9},{9,8},{10,11... | collective-permute-start | bytes 1769480 | tf_op jit(solution)/shard_map/ppermute | solution.py:289
  70.1 3.8 %collective-permute-start.20 = (bf16[256,1152]{1,0:T(8,128)(2,1)S(1)}, bf16[256,1152]{1,0:T(8,128)(2,1)S(1)}, u32[]{:S(2)}, u32[]{:S(2)}) collective-permute-start(bf16[256,1152]{1,0:T(8,128)(2,1)S(1)} %collective-permute-done.15.refs_9_), channel_id=1, source_target_pairs={{0,1},{1,0},{2,3},{3,2},{4,5},{5,4},{6,7},{7,6},{8,9},{9,8},{10,11... | collective-permute-start | bytes 1769480 | tf_op jit(solution)/shard_map/ppermute | solution.py:289
  70.6 3.3 %collective-permute-start.21 = (bf16[256,1152]{1,0:T(8,128)(2,1)S(1)}, bf16[256,1152]{1,0:T(8,128)(2,1)S(1)}, u32[]{:S(2)}, u32[]{:S(2)}) collective-permute-start(bf16[256,1152]{1,0:T(8,128)(2,1)S(1)} %collective-permute-done.16.refs_7_), channel_id=1, source_target_pairs={{0,1},{1,0},{2,3},{3,2},{4,5},{5,4},{6,7},{7,6},{8,9},{9,8},{10,11... | collective-permute-start | bytes 1769480 | tf_op jit(solution)/shard_map/ppermute | solution.py:289
  70.6 6.6 %collective-permute-start.22 = (bf16[16,5120]{1,0:T(8,128)(2,1)S(1)}, bf16[16,5120]{1,0:T(8,128)(2,1)S(1)}, u32[]{:S(2)}, u32[]{:S(2)}) collective-permute-start(bf16[16,5120]{1,0:T(8,128)(2,1)S(1)} %add_convert_fusion.mine), channel_id=1, source_target_pairs={{0,4},{4,0},{8,12},{12,8},{1,5},{5,1},{9,13},{13,9},{2,6},{6,2},{1... | collective-permute-start | bytes 491528 | tf_op jit(solution)/shard_map/ppermute | solution.py:289

commit v6 on v5

--- a/solution.py
+++ b/solution.py
@@ -290,7 +290,7 @@
 
 
 PREP_MIB = 54
-SPANS = (7, 9)
+SPANS = (8, 8)
 
 
 def per_device(

time: 78.3 us -> 79 us (level)
  waiting for transfers between devices: 34.5 us -> 37.7 us
  starting transfers between devices: 21.2 us -> 18.4 us
    ppermute x23, waiting for transfers between devices: 34.5 us -> 37.7 us  [xor_swap(): return lax.ppermute(value, axis, [(i, i ^ bit) for i in range(size)])]
    ppermute x23, starting transfers between devices: 21.2 us -> 18.4 us  [xor_swap(): return lax.ppermute(value, axis, [(i, i ^ bit) for i in range(size)])]
  transfers between devices with their start and end apart: 23 -> 23, of which waited for: 10 -> 12; matrix products, arithmetic and copies ran while one was open for 0% -> 0% of each run, Pallas kernels for 21% -> 22%
where the time goes in v6:
time: 79 us; the launch traced here: 78.8 us
  waiting for transfers between devices  37.7 us (48%)
  Pallas kernels  20 us (25%)
  starting transfers between devices  18.4 us (23%)
  local copies, waits for them, and re-layouts  1.78 us (2%)
  between operations  0.81 us (1%)
    ppermute x23, waiting for transfers between devices, xor_swap(): return lax.ppermute(value, axis, [(i, i ^ bit) for i in range(size)])  37.7 us
    ppermute x23, starting transfers between devices, xor_swap(): return lax.ppermute(value, axis, [(i, i ^ bit) for i in range(size)])  18.4 us
    pallas_call x6, Pallas kernels, matmul_call(): pl.pallas_call(functools.partial(matmul_kernel, plan, block, shard, rank2...  13.7 us
    pallas_call x7, Pallas kernels, local(): pl.pallas_call(kernel, out_shape=tuple(outs), in_specs=spaces, out_specs=...  4.18 us
    pallas_call x1, Pallas kernels, low_rank_call(): pl.pallas_call(functools.partial(low_rank_kernel, slots, rank2, width, kv...  2.09 us
    unnamed x13, local copies, waits for them, and re-layouts  1.78 us
  transfers between devices with their start and end apart: 23, of which 12 were waited for; matrix products, arithmetic and copies ran while one was open for 0% of the time, Pallas kernels for 22%

profile of v6, /device:TPU:0, one launch (start us, length us, event | category | flops | bytes accessed | tf_op | source)
XLA Modules:
  0.0 78.8 jit_solution(10952807791211470762)
XLA Ops:
  0.6 0.5 collective-permute-start.2
  1.2 2.3 %prep.1 = (bf16[32,5120]{1,0:T(8,128)(2,1)}, bf16[256,1024]{1,0:T(8,128)(2,1)}) custom-call(bf16[1024,2048]{1,0:T(8,128)(2,1)} %weight.3, bf16[1,32,4096]{2,1,0:T(8,128)(2,1)} %down.1, bf16[1,32,1024]{2,1,0:T(8,128)(2,1)} %up.1), custom_call_target="tpu_custom_call" | custom-call | flops 1 | bytes 1 | tf_op jit(solution)/shard_map/prep/pallas_call | solution.py:324
  3.5 2.5 %collective-permute-start.1 = (bf16[32,5120]{1,0:T(8,128)(2,1)}, bf16[32,5120]{1,0:T(8,128)(2,1)S(1)}, u32[]{:S(2)}, u32[]{:S(2)}) collective-permute-start(bf16[32,5120]{1,0:T(8,128)(2,1)} %get-tuple-element.81.refs_0_), channel_id=1, source_target_pairs={{0,2},{1,3},{2,0},{3,1},{4,6},{5,7},{6,4},{7,5},{8,10},{9,11},{10,... | collective-permute-start | bytes 983048 | tf_op jit(solution)/shard_map/ppermute | solution.py:289
  6.2 1.4 %copy-done.1 = bf16[256,4096]{1,0:T(8,128)(2,1)S(1)} copy-done((bf16[256,4096]{1,0:T(8,128)(2,1)S(1)}, bf16[256,4096]{1,0:T(8,128)(2,1)}, u32[]{:S(2)}) %copy-start.1) | copy-done | bytes 2097176
  7.8 0.5 load.1
  8.3 6.4 %collective-permute-done.1.refs_2_ = bf16[32,5120]{1,0:T(8,128)(2,1)S(1)} collective-permute-done((bf16[32,5120]{1,0:T(8,128)(2,1)}, bf16[32,5120]{1,0:T(8,128)(2,1)S(1)}, u32[]{:S(2)}, u32[]{:S(2)}) %collective-permute-start.1) | collective-permute-done | bytes 327712 | tf_op jit(solution)/shard_map/ppermute | solution.py:289
  15.3 10.6 %collective-permute-done.refs_6_ = bf16[256,1024]{1,0:T(8,128)(2,1)S(1)} collective-permute-done((bf16[256,1024]{1,0:T(8,128)(2,1)}, bf16[256,1024]{1,0:T(8,128)(2,1)S(1)}, u32[]{:S(2)}, u32[]{:S(2)}) %collective-permute-start) | collective-permute-done | bytes 524320 | tf_op jit(solution)/shard_map/ppermute | solution.py:289
  26.0 2.1 %low_rank.1 = (bf16[256,128]{1,0:T(8,128)(2,1)S(1)}, bf16[256,128]{1,0:T(8,128)(2,1)S(1)}, bf16[128,4096]{1,0:T(8,128)(2,1)S(1)}, bf16[128,1024]{1,0:T(8,128)(2,...) custom-call(s32[8]{0:T(128)S(1)} %pad_add_fusion.place, ...), custom_call_target="tpu_custom_call" | custom-call | flops 1 | bytes 1 | tf_op jit(solution)/shard_map/low_rank/pallas_call | solution.py:137
  28.6 1.9 %collective-permute-start.7 = (bf16[256,1024]{1,0:T(8,128)(2,1)S(1)}, bf16[256,1024]{1,0:T(8,128)(2,1)S(1)}, u32[]{:S(2)}, u32[]{:S(2)}) collective-permute-start(bf16[256,1024]{1,0:T(8,128)(2,1)S(1)} %collective-permute-done.refs_6_), channel_id=1, source_target_pairs={{0,4},{4,0},{8,12},{12,8},{1,5},{5,1},{9,13},{13,9},{2,6},{6,2},{1... | collective-permute-start | bytes 1572872 | tf_op jit(solution)/shard_map/ppermute | solution.py:289
  30.5 1.5 %collective-permute-start.8 = (bf16[256,1024]{1,0:T(8,128)(2,1)S(1)}, bf16[256,1024]{1,0:T(8,128)(2,1)S(1)}, u32[]{:S(2)}, u32[]{:S(2)}) collective-permute-start(bf16[256,1024]{1,0:T(8,128)(2,1)S(1)} %collective-permute-done.refs_6_), channel_id=1, source_target_pairs={{0,16},{16,0},{1,17},{17,1},{2,18},{18,2},{3,19},{19,3},{4,20},{20... | collective-permute-start | bytes 1572872 | tf_op jit(solution)/shard_map/ppermute | solution.py:289
  32.2 1.6 %collective-permute-start.9 = (bf16[1,32,5120]{2,1,0:T(8,128)(2,1)S(1)}, bf16[1,32,5120]{2,1,0:T(8,128)(2,1)S(1)}, u32[]{:S(2)}, u32[]{:S(2)}) collective-permute-start(bf16[1,32,5120]{2,1,0:T(8,128)(2,1)S(1)} %get-tuple-element.105), channel_id=1, source_target_pairs={{0,2},{1,3},{2,0},{3,1},{4,6},{5,7},{6,4},{7,5},{8,10},{9,11},{10,... | collective-permute-start | bytes 983048 | tf_op jit(solution)/shard_map/ppermute | solution.py:289
  33.7 2.8 %matmul_0.1 = (f32[256,2048]{1,0:T(8,128)S(1)}, bf16[256,4096]{1,0:T(8,128)(2,1)}) custom-call(bf16[256,4096]{1,0:T(8,128)(2,1)S(1)} %get-tuple-element.89.tok.refs_0_, bf16[256,2048]{1,0:T(8,128)(2,1)S(1)} %get-tuple-element.90.cot.refs_1_, bf16[256,128]{1,0:T(8,128)(2,1)S(1)} %get-tuple-element.101.refs_2_, ...), custom_call_target="tpu_custom_call" | custom-call | flops 2147483648 | bytes 1 | tf_op jit(solution)/shard_map/matmul_0/pallas_call | solution.py:247
  36.5 0.6 collective-permute-start.11
  37.1 5.8 %collective-permute-done.9.recv = bf16[1,32,5120]{2,1,0:T(8,128)(2,1)S(1)} collective-permute-done((bf16[1,32,5120]{2,1,0:T(8,128)(2,1)S(1)}, bf16[1,32,5120]{2,1,0:T(8,128)(2,1)S(1)}, u32[]{:S(2)}, u32[]{:S(2)}) %collective-permute-start.9) | collective-permute-done | bytes 327712 | tf_op jit(solution)/shard_map/ppermute | solution.py:289
  43.0 1.1 %collective-permute-done.8.refs_0_.refs_6_ = bf16[256,1024]{1,0:T(8,128)(2,1)S(1)} collective-permute-done((bf16[256,1024]{1,0:T(8,128)(2,1)S(1)}, bf16[256,1024]{1,0:T(8,128)(2,1)S(1)}, u32[]{:S(2)}, u32[]{:S(2)}) %collective-permute-start.8) | collective-permute-done | bytes 524320 | tf_op jit(solution)/shard_map/ppermute | solution.py:289
  44.1 1.5 %collective-permute-start.10 = (bf16[256,1024]{1,0:T(8,128)(2,1)S(1)}, bf16[256,1024]{1,0:T(8,128)(2,1)S(1)}, u32[]{:S(2)}, u32[]{:S(2)}) collective-permute-start(bf16[256,1024]{1,0:T(8,128)(2,1)S(1)} %collective-permute-done.7.refs_1_.refs_8_), channel_id=1, source_target_pairs={{0,16},{16,0},{1,17},{17,1},{2,18},{18,2},{3,19},{19,3},{4,20},{20... | collective-permute-start | bytes 1572872 | tf_op jit(solution)/shard_map/ppermute | solution.py:289
  46.3 2.7 %matmul_1.1 = (f32[256,2048]{1,0:T(8,128)S(1)}, bf16[256,4096]{1,0:T(8,128)(2,1)}) custom-call(bf16[256,4096]{1,0:T(8,128)(2,1)S(1)} %get-tuple-element.89.tok.refs_0_, bf16[256,2048]{1,0:T(8,128)(2,1)S(1)} %get-tuple-element.90.cot.refs_1_, bf16[256,128]{1,0:T(8,128)(2,1)S(1)} %get-tuple-element.101.refs_2_, ...), custom_call_target="tpu_custom_call", output_to_operand_aliasing={{1}: (8, {}), {0}: (7, {})} | custom-call | flops 2147483648 | bytes 1 | tf_op jit(solution)/shard_map/matmul_1/pallas_call | solution.py:247
  49.0 2.2 %collective-permute-done.12 = bf16[16,5120]{1,0:T(8,128)(2,1)S(1)} collective-permute-done((bf16[16,5120]{1,0:T(8,128)(2,1)S(1)}, bf16[16,5120]{1,0:T(8,128)(2,1)S(1)}, u32[]{:S(2)}, u32[]{:S(2)}) %collective-permute-start.12) | collective-permute-done | bytes 163872 | tf_op jit(solution)/shard_map/ppermute | solution.py:289
  51.2 3.2 %collective-permute-start.18 = (bf16[16,5120]{1,0:T(8,128)(2,1)S(1)}, bf16[16,5120]{1,0:T(8,128)(2,1)S(1)}, u32[]{:S(2)}, u32[]{:S(2)}) collective-permute-start(bf16[16,5120]{1,0:T(8,128)(2,1)S(1)} %add_convert_fusion.1), channel_id=1, source_target_pairs={{0,8},{4,12},{8,0},{12,4},{1,9},{5,13},{9,1},{13,5},{2,10},{6,14},... | collective-permute-start | bytes 491528 | tf_op jit(solution)/shard_map/ppermute | solution.py:289
  54.5 1.5 %collective-permute-start.16 = (bf16[256,1024]{1,0:T(8,128)(2,1)S(1)}, bf16[256,1024]{1,0:T(8,128)(2,1)S(1)}, u32[]{:S(2)}, u32[]{:S(2)}) collective-permute-start(bf16[256,1024]{1,0:T(8,128)(2,1)S(1)} %get-tuple-element.129), channel_id=1, source_target_pairs={{0,2},{1,3},{2,0},{3,1},{4,6},{5,7},{6,4},{7,5},{8,10},{9,11},{10,... | collective-permute-start | bytes 1572872 | tf_op jit(solution)/shard_map/ppermute | solution.py:289
  56.9 0.6 collective-permute-start.15
  57.5 2.1 %collective-permute-done.18 = bf16[16,5120]{1,0:T(8,128)(2,1)S(1)} collective-permute-done((bf16[16,5120]{1,0:T(8,128)(2,1)S(1)}, bf16[16,5120]{1,0:T(8,128)(2,1)S(1)}, u32[]{:S(2)}, u32[]{:S(2)}) %collective-permute-start.18) | collective-permute-done | bytes 163872 | tf_op jit(solution)/shard_map/ppermute | solution.py:289
  59.9 1.9 %matmul_2.1 = (f32[256,2048]{1,0:T(8,128)S(1)}, bf16[256,4096]{1,0:T(8,128)(2,1)}) custom-call(bf16[256,4096]{1,0:T(8,128)(2,1)S(1)} %get-tuple-element.89.tok.refs_0_, bf16[256,2048]{1,0:T(8,128)(2,1)S(1)} %get-tuple-element.90.cot.refs_1_, bf16[256,128]{1,0:T(8,128)(2,1)S(1)} %get-tuple-element.101.refs_2_, ...), custom_call_target="tpu_custom_call", output_to_operand_aliasing={{1}: (11, {}), {0}: (10, {})} | custom-call | flops 1073741824 | bytes 1 | tf_op jit(solution)/shard_map/matmul_2/pallas_call | solution.py:247
  61.8 3.4 %collective-permute-done.16.refs_7_ = bf16[256,1024]{1,0:T(8,128)(2,1)S(1)} collective-permute-done((bf16[256,1024]{1,0:T(8,128)(2,1)S(1)}, bf16[256,1024]{1,0:T(8,128)(2,1)S(1)}, u32[]{:S(2)}, u32[]{:S(2)}) %collective-permute-start.16) | collective-permute-done | bytes 524320 | tf_op jit(solution)/shard_map/ppermute | solution.py:289
  65.2 1.5 %matmul_3.1 = (f32[256,2048]{1,0:T(8,128)S(1)}, bf16[256,4096]{1,0:T(8,128)(2,1)}) custom-call(bf16[256,4096]{1,0:T(8,128)(2,1)S(1)} %get-tuple-element.89.tok.refs_0_, bf16[256,2048]{1,0:T(8,128)(2,1)S(1)} %get-tuple-element.90.cot.refs_1_, bf16[256,128]{1,0:T(8,128)(2,1)S(1)} %get-tuple-element.101.refs_2_, ...), custom_call_target="tpu_custom_call", output_to_operand_aliasing={{1}: (9, {}), {0}: (8, {})} | custom-call | flops 536870912 | bytes 1 | tf_op jit(solution)/shard_map/matmul_3/pallas_call | solution.py:247
  66.7 3.6 %collective-permute-done.14.refs_7_ = bf16[256,1024]{1,0:T(8,128)(2,1)S(1)} collective-permute-done((bf16[256,1024]{1,0:T(8,128)(2,1)S(1)}, bf16[256,1024]{1,0:T(8,128)(2,1)S(1)}, u32[]{:S(2)}, u32[]{:S(2)}) %collective-permute-start.14) | collective-permute-done | bytes 524320 | tf_op jit(solution)/shard_map/ppermute | solution.py:289
  70.3 0.5 collective-permute-done.15.refs_9_
  71.6 1.9 %matmul_4.1 = (f32[256,2048]{1,0:T(8,128)S(1)}, bf16[256,4096]{1,0:T(8,128)(2,1)}) custom-call(bf16[256,4096]{1,0:T(8,128)(2,1)S(1)} %get-tuple-element.89.tok.refs_0_, bf16[256,2048]{1,0:T(8,128)(2,1)S(1)} %get-tuple-element.90.cot.refs_1_, bf16[256,128]{1,0:T(8,128)(2,1)S(1)} %get-tuple-element.101.refs_2_, ...), custom_call_target="tpu_custom_call", output_to_operand_aliasing={{1}: (11, {}), {0}: (10, {})} | custom-call | flops 1073741824 | bytes 1 | tf_op jit(solution)/shard_map/matmul_4/pallas_call | solution.py:247
  73.5 0.7 collective-permute-done.21.refs_11_
  74.2 2.9 %matmul_5.1 = (bf16[256,2048]{1,0:T(8,128)(2,1)}, bf16[256,4096]{1,0:T(8,128)(2,1)}) custom-call(bf16[256,4096]{1,0:T(8,128)(2,1)S(1)} %get-tuple-element.89.tok.refs_0_, bf16[256,2048]{1,0:T(8,128)(2,1)S(1)} %get-tuple-element.90.cot.refs_1_, bf16[256,128]{1,0:T(8,128)(2,1)S(1)} %get-tuple-element.101.refs_2_, ...), custom_call_target="tpu_custom_call", output_to_operand_aliasing={{1}: (13, {})} | custom-call | flops 1610612736 | bytes 1 | tf_op jit(solution)/shard_map/matmul_5/pallas_call | solution.py:247
  77.2 0.8 collective-permute-done.22.recv
  78.0 0.9 %finish.1 = (f32[1,32,4096]{2,1,0:T(8,128)}, f32[1,32,1024]{2,1,0:T(8,128)}) custom-call(bf16[16,5120]{1,0:T(8,128)(2,1)S(1)} %add_convert_fusion.mine, bf16[16,5120]{1,0:T(8,128)(2,1)S(1)} %collective-permute-done.22.recv), custom_call_target="tpu_custom_call" | custom-call | flops 1 | bytes 1 | tf_op jit(solution)/shard_map/finish/pallas_call | solution.py:324
  (44 shorter events, 4.5 us)
Async XLA Ops:
  0.6 5.4 %copy-start = (bf16[1024,2048]{1,0:T(8,128)(2,1)S(1)}, bf16[1024,2048]{1,0:T(8,128)(2,1)}, u32[]{:S(2)}) copy-start(bf16[1024,2048]{1,0:T(8,128)(2,1)} %weight.3) | copy-start | bytes 12582916
  0.6 14.1 %collective-permute-start.2 = (bf16[1024,2048]{1,0:T(8,128)(2,1)}, bf16[1024,2048]{1,0:T(8,128)(2,1)S(1)}, u32[]{:S(2)}, u32[]{:S(2)}) collective-permute-start(bf16[1024,2048]{1,0:T(8,128)(2,1)} %weight.3), channel_id=1, source_target_pairs={{0,1},{1,0},{2,3},{3,2},{4,5},{5,4},{6,7},{7,6},{8,9},{9,8},{10,11... | collective-permute-start | bytes 12582920 | tf_op jit(solution)/shard_map/ppermute | solution.py:289
  3.5 11.2 %collective-permute-start.1 = (bf16[32,5120]{1,0:T(8,128)(2,1)}, bf16[32,5120]{1,0:T(8,128)(2,1)S(1)}, u32[]{:S(2)}, u32[]{:S(2)}) collective-permute-start(bf16[32,5120]{1,0:T(8,128)(2,1)} %get-tuple-element.81.refs_0_), channel_id=1, source_target_pairs={{0,2},{1,3},{2,0},{3,1},{4,6},{5,7},{6,4},{7,5},{8,10},{9,11},{10,... | collective-permute-start | bytes 983048 | tf_op jit(solution)/shard_map/ppermute | solution.py:289
  6.0 1.6 %copy-start.1 = (bf16[256,4096]{1,0:T(8,128)(2,1)S(1)}, bf16[256,4096]{1,0:T(8,128)(2,1)}, u32[]{:S(2)}) copy-start(bf16[256,4096]{1,0:T(8,128)(2,1)} %refs_0_.1) | copy-start | bytes 6291460
  6.0 1.9 %copy-start.2 = (bf16[256,2048]{1,0:T(8,128)(2,1)S(1)}, bf16[256,2048]{1,0:T(8,128)(2,1)}, u32[]{:S(2)}) copy-start(bf16[256,2048]{1,0:T(8,128)(2,1)} %refs_1_.1) | copy-start | bytes 3145732
  6.0 20.0 %collective-permute-start = (bf16[256,1024]{1,0:T(8,128)(2,1)}, bf16[256,1024]{1,0:T(8,128)(2,1)S(1)}, u32[]{:S(2)}, u32[]{:S(2)}) collective-permute-start(bf16[256,1024]{1,0:T(8,128)(2,1)} %get-tuple-element.80), channel_id=1, source_target_pairs={{0,2},{1,3},{2,0},{3,1},{4,6},{5,7},{6,4},{7,5},{8,10},{9,11},{10,... | collective-permute-start | bytes 1572872 | tf_op jit(solution)/shard_map/ppermute | solution.py:289
  7.8 7.1 %copy-start.3 = (bf16[32,5120]{1,0:T(8,128)(2,1)S(1)}, bf16[32,5120]{1,0:T(8,128)(2,1)}, u32[]{:S(2)}) copy-start(bf16[32,5120]{1,0:T(8,128)(2,1)} %get-tuple-element.81.refs_0_) | copy-start | bytes 983044
  7.8 7.4 %copy-start.4 = (s32[4]{0:T(128)S(1)}, s32[4]{0:T(128)}, u32[]{:S(2)}) copy-start(s32[4]{0:T(128)} %param.12) | copy-start | bytes 52
  7.8 7.4 %copy-start.5 = (s32[1,4]{1,0:T(1,128)S(1)}, s32[1,4]{1,0:T(1,128)}, u32[]{:S(2)}) copy-start(s32[1,4]{1,0:T(1,128)} %param.11) | copy-start | bytes 52
  14.7 11.2 %collective-permute-start.3 = (bf16[32,5120]{1,0:T(8,128)(2,1)S(1)}, bf16[32,5120]{1,0:T(8,128)(2,1)S(1)}, u32[]{:S(2)}, u32[]{:S(2)}) collective-permute-start(bf16[32,5120]{1,0:T(8,128)(2,1)S(1)} %collective-permute-done.1.refs_2_), channel_id=1, source_target_pairs={{0,1},{1,0},{2,3},{3,2},{4,5},{5,4},{6,7},{7,6},{8,9},{9,8},{10,11... | collective-permute-start | bytes 983048 | tf_op jit(solution)/shard_map/ppermute | solution.py:289
  14.9 11.1 %collective-permute-start.4 = (bf16[32,5120]{1,0:T(8,128)(2,1)S(1)}, bf16[32,5120]{1,0:T(8,128)(2,1)S(1)}, u32[]{:S(2)}, u32[]{:S(2)}) collective-permute-start(bf16[32,5120]{1,0:T(8,128)(2,1)S(1)} %copy-done.3), channel_id=1, source_target_pairs={{0,1},{1,0},{2,3},{3,2},{4,5},{5,4},{6,7},{7,6},{8,9},{9,8},{10,11... | collective-permute-start | bytes 983048 | tf_op jit(solution)/shard_map/ppermute | solution.py:289
  28.0 4.0 %collective-permute-start.5 = (bf16[2,32,5120]{2,1,0:T(8,128)(2,1)S(1)}, bf16[2,32,5120]{2,1,0:T(8,128)(2,1)S(1)}, u32[]{:S(2)}, u32[]{:S(2)}) collective-permute-start(bf16[2,32,5120]{2,1,0:T(8,128)(2,1)S(1)} %get-tuple-element.94), channel_id=1, source_target_pairs={{0,1},{1,0},{2,3},{3,2},{4,5},{5,4},{6,7},{7,6},{8,9},{9,8},{10,11... | collective-permute-start | bytes 1966088 | tf_op jit(solution)/shard_map/ppermute | solution.py:289
  28.2 3.8 %collective-permute-start.6 = (bf16[256,1024]{1,0:T(8,128)(2,1)S(1)}, bf16[256,1024]{1,0:T(8,128)(2,1)S(1)}, u32[]{:S(2)}, u32[]{:S(2)}) collective-permute-start(bf16[256,1024]{1,0:T(8,128)(2,1)S(1)} %collective-permute-done.refs_6_), channel_id=1, source_target_pairs={{0,1},{1,0},{2,3},{3,2},{4,5},{5,4},{6,7},{7,6},{8,9},{9,8},{10,11... | collective-permute-start | bytes 1572872 | tf_op jit(solution)/shard_map/ppermute | solution.py:289
  28.6 14.4 %collective-permute-start.7 = (bf16[256,1024]{1,0:T(8,128)(2,1)S(1)}, bf16[256,1024]{1,0:T(8,128)(2,1)S(1)}, u32[]{:S(2)}, u32[]{:S(2)}) collective-permute-start(bf16[256,1024]{1,0:T(8,128)(2,1)S(1)} %collective-permute-done.refs_6_), channel_id=1, source_target_pairs={{0,4},{4,0},{8,12},{12,8},{1,5},{5,1},{9,13},{13,9},{2,6},{6,2},{1... | collective-permute-start | bytes 1572872 | tf_op jit(solution)/shard_map/ppermute | solution.py:289
  30.5 13.6 %collective-permute-start.8 = (bf16[256,1024]{1,0:T(8,128)(2,1)S(1)}, bf16[256,1024]{1,0:T(8,128)(2,1)S(1)}, u32[]{:S(2)}, u32[]{:S(2)}) collective-permute-start(bf16[256,1024]{1,0:T(8,128)(2,1)S(1)} %collective-permute-done.refs_6_), channel_id=1, source_target_pairs={{0,16},{16,0},{1,17},{17,1},{2,18},{18,2},{3,19},{19,3},{4,20},{20... | collective-permute-start | bytes 1572872 | tf_op jit(solution)/shard_map/ppermute | solution.py:289
  32.2 10.7 %collective-permute-start.9 = (bf16[1,32,5120]{2,1,0:T(8,128)(2,1)S(1)}, bf16[1,32,5120]{2,1,0:T(8,128)(2,1)S(1)}, u32[]{:S(2)}, u32[]{:S(2)}) collective-permute-start(bf16[1,32,5120]{2,1,0:T(8,128)(2,1)S(1)} %get-tuple-element.105), channel_id=1, source_target_pairs={{0,2},{1,3},{2,0},{3,1},{4,6},{5,7},{6,4},{7,5},{8,10},{9,11},{10,... | collective-permute-start | bytes 983048 | tf_op jit(solution)/shard_map/ppermute | solution.py:289
  36.5 19.4 %collective-permute-start.11 = (bf16[256,1024]{1,0:T(8,128)(2,1)S(1)}, bf16[256,1024]{1,0:T(8,128)(2,1)S(1)}, u32[]{:S(2)}, u32[]{:S(2)}) collective-permute-start(bf16[256,1024]{1,0:T(8,128)(2,1)S(1)} %get-tuple-element.109), channel_id=1, source_target_pairs={{0,2},{1,3},{2,0},{3,1},{4,6},{5,7},{6,4},{7,5},{8,10},{9,11},{10,... | collective-permute-start | bytes 1572872 | tf_op jit(solution)/shard_map/ppermute | solution.py:289
  44.1 12.7 %collective-permute-start.10 = (bf16[256,1024]{1,0:T(8,128)(2,1)S(1)}, bf16[256,1024]{1,0:T(8,128)(2,1)S(1)}, u32[]{:S(2)}, u32[]{:S(2)}) collective-permute-start(bf16[256,1024]{1,0:T(8,128)(2,1)S(1)} %collective-permute-done.7.refs_1_.refs_8_), channel_id=1, source_target_pairs={{0,16},{16,0},{1,17},{17,1},{2,18},{18,2},{3,19},{19,3},{4,20},{20... | collective-permute-start | bytes 1572872 | tf_op jit(solution)/shard_map/ppermute | solution.py:289
  45.8 5.4 %collective-permute-start.12 = (bf16[16,5120]{1,0:T(8,128)(2,1)S(1)}, bf16[16,5120]{1,0:T(8,128)(2,1)S(1)}, u32[]{:S(2)}, u32[]{:S(2)}) collective-permute-start(bf16[16,5120]{1,0:T(8,128)(2,1)S(1)} %get-tuple-element.117), channel_id=1, source_target_pairs={{0,4},{4,0},{8,12},{12,8},{1,5},{5,1},{9,13},{13,9},{2,6},{6,2},{1... | collective-permute-start | bytes 491528 | tf_op jit(solution)/shard_map/ppermute | solution.py:289
  51.2 8.4 %collective-permute-start.18 = (bf16[16,5120]{1,0:T(8,128)(2,1)S(1)}, bf16[16,5120]{1,0:T(8,128)(2,1)S(1)}, u32[]{:S(2)}, u32[]{:S(2)}) collective-permute-start(bf16[16,5120]{1,0:T(8,128)(2,1)S(1)} %add_convert_fusion.1), channel_id=1, source_target_pairs={{0,8},{4,12},{8,0},{12,4},{1,9},{5,13},{9,1},{13,5},{2,10},{6,14},... | collective-permute-start | bytes 491528 | tf_op jit(solution)/shard_map/ppermute | solution.py:289
  54.5 10.8 %collective-permute-start.16 = (bf16[256,1024]{1,0:T(8,128)(2,1)S(1)}, bf16[256,1024]{1,0:T(8,128)(2,1)S(1)}, u32[]{:S(2)}, u32[]{:S(2)}) collective-permute-start(bf16[256,1024]{1,0:T(8,128)(2,1)S(1)} %get-tuple-element.129), channel_id=1, source_target_pairs={{0,2},{1,3},{2,0},{3,1},{4,6},{5,7},{6,4},{7,5},{8,10},{9,11},{10,... | collective-permute-start | bytes 1572872 | tf_op jit(solution)/shard_map/ppermute | solution.py:289
  56.0 3.9 %collective-permute-start.17 = (bf16[256,1024]{1,0:T(8,128)(2,1)S(1)}, bf16[256,1024]{1,0:T(8,128)(2,1)S(1)}, u32[]{:S(2)}, u32[]{:S(2)}) collective-permute-start(bf16[256,1024]{1,0:T(8,128)(2,1)S(1)} %collective-permute-done.11.refs_7_), channel_id=1, source_target_pairs={{0,1},{1,0},{2,3},{3,2},{4,5},{5,4},{6,7},{7,6},{8,9},{9,8},{10,11... | collective-permute-start | bytes 1572872 | tf_op jit(solution)/shard_map/ppermute | solution.py:289
  56.0 14.3 %collective-permute-start.14 = (bf16[256,1024]{1,0:T(8,128)(2,1)S(1)}, bf16[256,1024]{1,0:T(8,128)(2,1)S(1)}, u32[]{:S(2)}, u32[]{:S(2)}) collective-permute-start(bf16[256,1024]{1,0:T(8,128)(2,1)S(1)} %collective-permute-done.11.refs_7_), channel_id=1, source_target_pairs={{0,16},{16,0},{1,17},{17,1},{2,18},{18,2},{3,19},{19,3},{4,20},{20... | collective-permute-start | bytes 1572872 | tf_op jit(solution)/shard_map/ppermute | solution.py:289
  56.9 13.9 %collective-permute-start.15 = (bf16[256,1024]{1,0:T(8,128)(2,1)S(1)}, bf16[256,1024]{1,0:T(8,128)(2,1)S(1)}, u32[]{:S(2)}, u32[]{:S(2)}) collective-permute-start(bf16[256,1024]{1,0:T(8,128)(2,1)S(1)} %collective-permute-done.11.refs_7_), channel_id=1, source_target_pairs={{0,4},{4,0},{8,12},{12,8},{1,5},{5,1},{9,13},{13,9},{2,6},{6,2},{1... | collective-permute-start | bytes 1572872 | tf_op jit(solution)/shard_map/ppermute | solution.py:289
  59.7 14.5 %collective-permute-start.13 = (bf16[3,256,1024]{2,1,0:T(8,128)(2,1)S(1)}, bf16[3,256,1024]{2,1,0:T(8,128)(2,1)S(1)}, u32[]{:S(2)}, u32[]{:S(2)}) collective-permute-start(bf16[3,256,1024]{2,1,0:T(8,128)(2,1)S(1)} %stack.1), channel_id=1, source_target_pairs={{0,1},{1,0},{2,3},{3,2},{4,5},{5,4},{6,7},{7,6},{8,9},{9,8},{10,11... | collective-permute-start | bytes 4718600 | tf_op jit(solution)/shard_map/ppermute | solution.py:289
  70.8 2.7 %collective-permute-start.19 = (bf16[256,1024]{1,0:T(8,128)(2,1)S(1)}, bf16[256,1024]{1,0:T(8,128)(2,1)S(1)}, u32[]{:S(2)}, u32[]{:S(2)}) collective-permute-start(bf16[256,1024]{1,0:T(8,128)(2,1)S(1)} %collective-permute-done.14.refs_7_), channel_id=1, source_target_pairs={{0,1},{1,0},{2,3},{3,2},{4,5},{5,4},{6,7},{7,6},{8,9},{9,8},{10,11... | collective-permute-start | bytes 1572872 | tf_op jit(solution)/shard_map/ppermute | solution.py:289
  70.8 2.7 %collective-permute-start.20 = (bf16[256,1024]{1,0:T(8,128)(2,1)S(1)}, bf16[256,1024]{1,0:T(8,128)(2,1)S(1)}, u32[]{:S(2)}, u32[]{:S(2)}) collective-permute-start(bf16[256,1024]{1,0:T(8,128)(2,1)S(1)} %collective-permute-done.15.refs_9_), channel_id=1, source_target_pairs={{0,1},{1,0},{2,3},{3,2},{4,5},{5,4},{6,7},{7,6},{8,9},{9,8},{10,11... | collective-permute-start | bytes 1572872 | tf_op jit(solution)/shard_map/ppermute | solution.py:289
  71.3 2.9 %collective-permute-start.21 = (bf16[256,1024]{1,0:T(8,128)(2,1)S(1)}, bf16[256,1024]{1,0:T(8,128)(2,1)S(1)}, u32[]{:S(2)}, u32[]{:S(2)}) collective-permute-start(bf16[256,1024]{1,0:T(8,128)(2,1)S(1)} %collective-permute-done.16.refs_7_), channel_id=1, source_target_pairs={{0,1},{1,0},{2,3},{3,2},{4,5},{5,4},{6,7},{7,6},{8,9},{9,8},{10,11... | collective-permute-start | bytes 1572872 | tf_op jit(solution)/shard_map/ppermute | solution.py:289
  71.3 6.6 %collective-permute-start.22 = (bf16[16,5120]{1,0:T(8,128)(2,1)S(1)}, bf16[16,5120]{1,0:T(8,128)(2,1)S(1)}, u32[]{:S(2)}, u32[]{:S(2)}) collective-permute-start(bf16[16,5120]{1,0:T(8,128)(2,1)S(1)} %add_convert_fusion.mine), channel_id=1, source_target_pairs={{0,4},{4,0},{8,12},{12,8},{1,5},{5,1},{9,13},{13,9},{2,6},{6,2},{1... | collective-permute-start | bytes 491528 | tf_op jit(solution)/shard_map/ppermute | solution.py:289
